TPU v7x, 32 devices: a whole 2x2x4 slice. The times are simulated.
32 devices in a mesh: group: 4 (over z), local: 8 (over y, x, core).
Axes of the slice: x: 2, y: 2, z: 4, core: 2. Of those that a mesh axis runs over, the one named last changes fastest.
Arguments:
- tokens: bfloat16 [4096, 2048], P(('group', 'local')), may hold values from -6 to 6
- cotangent: bfloat16 [4096, 2048], P(('group', 'local')), may hold values from -6 to 6
- expert_ids: int32 [4096, 4], P(('group', 'local')), may hold values from 0 to 31, all different within a row
- gates: float32 [4096, 4], P(('group', 'local')), may hold values from 0.1 to 1
- w_gate: bfloat16 [32, 2048, 768], P(('group', 'local')), may hold values from -0.125 to 0.125
- w_up: bfloat16 [32, 2048, 768], P(('group', 'local')), may hold values from -0.125 to 0.125
- w_down: bfloat16 [32, 768, 2048], P(('group', 'local')), may hold values from -0.21875 to 0.21875
Outputs:
- mixed: bfloat16 [4096, 2048], P(('group', 'local'))
- d_tokens: bfloat16 [4096, 2048], P(('group', 'local'))
- d_gates: float32 [4096, 4], P(('group', 'local'))
- d_w_gate: bfloat16 [32, 2048, 768], P(('group', 'local'))
- d_w_up: bfloat16 [32, 2048, 768], P(('group', 'local'))
- d_w_down: bfloat16 [32, 768, 2048], P(('group', 'local'))
Inputs may be any that keep to these rules, and one draw needn't show every extreme that they name: `expert_ids`: the 4 experts of a token are different.
All inputs are finite; a program needn't handle non-finite values.
Results may differ from a plain program's by a relative error of at most 0.0064.
Values may be sent and summed in bfloat16 or wider, within the bound.
No kernel may reach another device: no remote copies, remote signals or barrier semaphores. Data moves between devices by JAX's collectives and lax.ppermute only.
A program may use at most 128 MiB of HBM per device.

v0:
```python
import jax
import jax.numpy as jnp
from jax import lax
from jax.sharding import PartitionSpec as P


def route_slots(block_ids, count_experts, capacity):
    experts_row = jnp.arange(count_experts, dtype=jnp.int32)
    onehot = (block_ids[:, None] == experts_row[None, :]).astype(jnp.int32)
    before = jnp.cumsum(onehot, axis=0) - onehot
    rank = jnp.sum(before * onehot, axis=1)
    kept = rank < capacity
    return jnp.where(kept, block_ids * capacity + rank, count_experts * capacity)


def expert_pass(rows_x, rows_z, wg, wu, wd):
    pre_gate = jnp.dot(rows_x, wg, preferred_element_type=jnp.float32)
    pre_up = jnp.dot(rows_x, wu, preferred_element_type=jnp.float32)
    sigmoid_a = jax.nn.sigmoid(pre_gate)
    silu_a = pre_gate * sigmoid_a
    hidden = (silu_a * pre_up).astype(jnp.bfloat16)
    out_rows = jnp.dot(hidden, wd, preferred_element_type=jnp.float32).astype(jnp.bfloat16)
    d_hidden = jnp.dot(rows_z, wd.T, preferred_element_type=jnp.float32)
    d_pre_gate = (d_hidden * pre_up * sigmoid_a * (1.0 + pre_gate * (1.0 - sigmoid_a))).astype(
        jnp.bfloat16
    )
    d_pre_up = (d_hidden * silu_a).astype(jnp.bfloat16)
    dx_rows = (
        jnp.dot(d_pre_gate, wg.T, preferred_element_type=jnp.float32)
        + jnp.dot(d_pre_up, wu.T, preferred_element_type=jnp.float32)
    ).astype(jnp.bfloat16)
    grad_down = jnp.dot(hidden.T, rows_z, preferred_element_type=jnp.float32)
    grad_gate = jnp.dot(rows_x.T, d_pre_gate, preferred_element_type=jnp.float32)
    grad_up = jnp.dot(rows_x.T, d_pre_up, preferred_element_type=jnp.float32)
    return (out_rows, dx_rows, grad_gate, grad_up, grad_down)


def local(tokens, cotangent, expert_ids, gates, w_gate, w_up, w_down):
    groups = lax.axis_size("group")
    locals_count = lax.axis_size("local")
    devices_count = groups * locals_count
    tok_rows, width = tokens.shape
    top_count = expert_ids.shape[1]
    capacity = max(2, 3 * tok_rows * top_count // (2 * devices_count))
    route_count = tok_rows * top_count
    slots = route_slots(expert_ids.reshape(-1), devices_count, capacity)
    token_of = jnp.arange(route_count, dtype=jnp.int32) // top_count
    token_table = (
        jnp.full((devices_count * capacity,), tok_rows, jnp.int32)
        .at[slots]
        .set(token_of, mode="drop")
    )
    gate_table = (
        jnp.zeros((devices_count * capacity,), jnp.float32)
        .at[slots]
        .set(gates.reshape(-1), mode="drop")
    )
    tokens_pad = jnp.concatenate([tokens, jnp.zeros((1, width), tokens.dtype)], axis=0)
    cot_pad = jnp.concatenate([cotangent, jnp.zeros((1, width), cotangent.dtype)], axis=0)
    send_x = tokens_pad[token_table].reshape(devices_count, capacity, width)
    send_z = (gate_table[:, None] * cot_pad[token_table].astype(jnp.float32)).astype(jnp.bfloat16)
    send_z = send_z.reshape(devices_count, capacity, width)
    recv_x, recv_z = (
        lax.all_to_all(send_x, ("group", "local"), split_axis=0, concat_axis=0, tiled=True),
        lax.all_to_all(send_z, ("group", "local"), split_axis=0, concat_axis=0, tiled=True),
    )
    out_rows, dx_rows, grad_gate, grad_up, grad_down = expert_pass(
        recv_x.reshape(devices_count * capacity, width),
        recv_z.reshape(devices_count * capacity, width),
        w_gate[0],
        w_up[0],
        w_down[0],
    )
    out_buf = out_rows.reshape(devices_count, capacity, width)
    dx_buf = dx_rows.reshape(devices_count, capacity, width)
    back_out, back_dx = (
        lax.all_to_all(out_buf, ("group", "local"), split_axis=0, concat_axis=0, tiled=True),
        lax.all_to_all(dx_buf, ("group", "local"), split_axis=0, concat_axis=0, tiled=True),
    )
    zero_row = jnp.zeros((1, width), jnp.bfloat16)
    out_pad = jnp.concatenate([back_out.reshape(devices_count * capacity, width), zero_row], axis=0)
    dx_pad = jnp.concatenate([back_dx.reshape(devices_count * capacity, width), zero_row], axis=0)
    out_routes = out_pad[slots].reshape(tok_rows, top_count, width).astype(jnp.float32)
    dx_routes = dx_pad[slots].reshape(tok_rows, top_count, width).astype(jnp.float32)
    mixed = jnp.sum(gates[:, :, None] * out_routes, axis=1).astype(jnp.bfloat16)
    d_gates = jnp.sum(cotangent.astype(jnp.float32)[:, None, :] * out_routes, axis=2)
    d_tokens = jnp.sum(dx_routes, axis=1).astype(jnp.bfloat16)
    return (
        mixed,
        d_tokens,
        d_gates,
        grad_gate.astype(jnp.bfloat16)[None],
        grad_up.astype(jnp.bfloat16)[None],
        grad_down.astype(jnp.bfloat16)[None],
    )


def solution(mesh):
    return jax.shard_map(
        local,
        mesh=mesh,
        in_specs=(
            P(("group", "local"), None),
            P(("group", "local"), None),
            P(("group", "local"), None),
            P(("group", "local"), None),
            P(("group", "local"), None, None),
            P(("group", "local"), None, None),
            P(("group", "local"), None, None),
        ),
        out_specs=(
            P(("group", "local"), None),
            P(("group", "local"), None),
            P(("group", "local"), None),
            P(("group", "local"), None, None),
            P(("group", "local"), None, None),
            P(("group", "local"), None, None),
        ),
        check_vma=False,
    )
```

profile of v0, /device:TPU:0, one launch (start us, length us, event | category | flops | bytes accessed | tf_op | source)
XLA Modules:
  0.0 361.3 jit_solution(11221203407221263924)
XLA Ops:
  0.6 0.0 copy-start
  0.6 0.9 copy.21
  1.6 0.1 eq.29
  1.7 0.1 eq.25
  1.8 0.7 broadcast_multiply_fusion
  2.5 1.2 reduce-window.6
  3.7 0.2 slice_reduce_fusion
  3.9 0.1 copy.24
  4.1 0.1 mul.75
  4.2 0.1 fusion.17
  4.3 2.4 scatter_custom_fusion
  6.8 1.9 concatenate.12
  8.7 8.2 %gather_fusion = bf16[768,2048]{1,0:T(8,128)(2,1)} fusion(bf16[129,2048]{1,0:T(8,128)(2,1)} %concatenate.12, s32[1024]{0:T(1024)S(1)} %pad_clamp_fusion.1), kind=kCustom, calls=%fused_computation | custom fusion | bytes 6294528 | tf_op jit(solution)/shard_map/gather | solution.py:60
  16.9 7.4 %all-to-all-start = ((bf16[32,24,2048]{2,1,0:T(8,128)(2,1)}), bf16[32,24,2048]{2,1,0:T(8,128)(2,1)}, u32[]{:S(2)}, u32[]{:S(2)}) async-start(bf16[32,24,2048]{2,1,0:T(8,128)(2,1)} %bitcast.66), calls=%async_computation | async-start | bytes 6291456 | tf_op jit(solution)/shard_map/all_to_all | solution.py:64
  24.3 1.9 concatenate.14
  26.2 0.0 copy-start.1
  26.2 8.2 %gather_fusion.2 = bf16[768,2048]{1,0:T(8,128)(2,1)} fusion(bf16[129,2048]{1,0:T(8,128)(2,1)} %concatenate.14, s32[1024]{0:T(1024)S(1)} %pad_clamp_fusion.1), kind=kCustom, calls=%fused_computation.2 | custom fusion | bytes 6294528 | tf_op jit(solution)/shard_map/gather | solution.py:61
  34.4 0.0 copy-done.1
  34.4 0.1 copy.20
  34.6 0.1 reshape.186
  34.7 2.4 scatter_custom_fusion.1
  37.1 0.1 mul.79
  37.2 4.1 %fusion = bf16[32,24,2048]{2,1,0:T(8,128)(2,1)} fusion(bf16[32,24,2048]{2,1,0:T(8,128)(2,1)} %bitcast.67, f32[32,24]{1,0:T(8,128)S(1)} %mul.79), kind=kLoop, calls=%fused_computation.7 | loop fusion | flops 4718592 | bytes 6294528 | tf_op jit(solution)/shard_map/convert_element_type | solution.py:61
  41.3 54.4 %all-to-all-done = bf16[32,24,2048]{2,1,0:T(8,128)(2,1)} async-done(((bf16[32,24,2048]{2,1,0:T(8,128)(2,1)}), bf16[32,24,2048]{2,1,0:T(8,128)(2,1)}, u32[]{:S(2)}, u32[]{:S(2)}) %all-to-all-start) | async-done | bytes 3145760 | tf_op jit(solution)/shard_map/all_to_all | solution.py:64
  95.8 4.2 %all-to-all-start.2 = ((bf16[32,24,2048]{2,1,0:T(8,128)(2,1)}), bf16[32,24,2048]{2,1,0:T(8,128)(2,1)}, u32[]{:S(2)}, u32[]{:S(2)}) async-start(bf16[32,24,2048]{2,1,0:T(8,128)(2,1)} %fusion), calls=%async_computation.2 | async-start | bytes 6291456 | tf_op jit(solution)/shard_map/all_to_all | solution.py:65
  100.0 0.0 copy-start.2
  100.0 7.0 %fusion.5 = f32[768,768]{1,0:T(8,128)} fusion(bf16[768,2048]{1,0:T(8,128)(2,1)} %bitcast.4, bf16[1,2048,768]{2,1,0:T(8,128)(2,1)} %param.12), kind=kOutput, calls=%fused_computation.19 | convolution fusion | flops 2415919104 | bytes 8650752 | tf_op jit(solution)/shard_map/dot_general | solution.py:18
  107.0 0.0 copy-done.2
  107.0 5.9 %fusion.9 = f32[768,768]{1,0:T(8,128)} fusion(bf16[768,2048]{1,0:T(8,128)(2,1)} %bitcast.4, bf16[1,2048,768]{2,1,0:T(8,128)(2,1)S(1)} %copy-done.2), kind=kOutput, calls=%fused_computation.23 | convolution fusion | flops 2415919104 | bytes 8650752 | tf_op jit(solution)/shard_map/dot_general | solution.py:17
  112.9 58.5 %all-to-all-done.2 = bf16[32,24,2048]{2,1,0:T(8,128)(2,1)} async-done(((bf16[32,24,2048]{2,1,0:T(8,128)(2,1)}), bf16[32,24,2048]{2,1,0:T(8,128)(2,1)}, u32[]{:S(2)}, u32[]{:S(2)}) %all-to-all-start.2) | async-done | bytes 3145760 | tf_op jit(solution)/shard_map/all_to_all | solution.py:65
  171.4 0.0 copy-done
  171.4 0.0 copy-start.3
  171.4 7.8 %multiply_convert_fusion = (bf16[768,768]{1,0:T(8,128)(2,1)S(1)}, bf16[768,768]{1,0:T(8,128)(2,1)S(1)}, bf16[768,768]{1,0:T(8,128)(2,1)}) fusion(f32[768,768]{1,0:T(8,128)} %fusion.9, f32[768,768]{1,0:T(8,128)} %fusion.5, bf16[768,2048]{1,0:T(8,128)(2,1)} %bitcast.12, bf16[1,768,2048]{2,1,0:T(8,128)(2,1)S(1)} %copy-done), kind=kOutput, calls=%fused_computation.28 | convolution fusion | flops 2424766464 | bytes 14548992 | tf_op jit(solution)/shard_map/dot_general | solution.py:23
  179.3 0.0 copy-start.5
  179.3 0.0 copy-start.7
  179.3 0.0 copy-done.3
  179.3 0.0 copy-start.4
  179.3 2.6 fusion.7
  181.9 0.0 copy-done.5
  181.9 0.0 copy-done.7
  181.9 0.1 copy-done.4
  182.0 4.0 %add_convert_fusion = bf16[768,2048]{1,0:T(8,128)(2,1)} fusion(f32[768,2048]{1,0:T(8,128)S(1)} %fusion.7, bf16[768,768]{1,0:T(8,128)(2,1)S(1)} %get-tuple-element.16, bf16[1,2048,768]{2,1,0:T(8,128)(2,1)S(1)} %copy-done.4), kind=kOutput, calls=%fused_computation.8 | convolution fusion | flops 2419064832 | bytes 13762560 | tf_op jit(solution)/shard_map/dot_general | solution.py:30
  186.0 4.1 %all-to-all-start.3 = ((bf16[32,24,2048]{2,1,0:T(8,128)(2,1)}), bf16[32,24,2048]{2,1,0:T(8,128)(2,1)}, u32[]{:S(2)}, u32[]{:S(2)}) async-start(bf16[32,24,2048]{2,1,0:T(8,128)(2,1)} %bitcast.69), calls=%async_computation.3 | async-start | bytes 6291456 | tf_op jit(solution)/shard_map/all_to_all | solution.py:78
  190.1 5.3 %convolution_convert_fusion.3 = bf16[768,2048]{1,0:T(8,128)(2,1)} fusion(bf16[768,768]{1,0:T(8,128)(2,1)} %get-tuple-element.18, bf16[1,768,2048]{2,1,0:T(8,128)(2,1)S(1)} %copy-done), kind=kOutput, calls=%fused_computation.14 | convolution fusion | flops 2417491968 | bytes 7471104 | tf_op jit(solution)/shard_map/dot_general | solution.py:22
  195.3 66.2 %all-to-all-done.3 = bf16[32,24,2048]{2,1,0:T(8,128)(2,1)} async-done(((bf16[32,24,2048]{2,1,0:T(8,128)(2,1)}), bf16[32,24,2048]{2,1,0:T(8,128)(2,1)}, u32[]{:S(2)}, u32[]{:S(2)}) %all-to-all-start.3) | async-done | bytes 3145760 | tf_op jit(solution)/shard_map/all_to_all | solution.py:78
  261.5 4.3 %all-to-all-start.1 = ((bf16[32,24,2048]{2,1,0:T(8,128)(2,1)}), bf16[32,24,2048]{2,1,0:T(8,128)(2,1)}, u32[]{:S(2)}, u32[]{:S(2)}) async-start(bf16[32,24,2048]{2,1,0:T(8,128)(2,1)} %bitcast.68), calls=%async_computation.1 | async-start | bytes 6291456 | tf_op jit(solution)/shard_map/all_to_all | solution.py:77
  265.8 2.1 convert_element_type.73
  267.9 0.0 copy-start.6
  267.9 6.7 %fusion.13 = bf16[1,768,2048]{2,1,0:T(8,128)(2,1)} fusion(bf16[768,768]{1,0:T(8,128)(2,1)} %get-tuple-element.18, bf16[768,2048]{1,0:T(8,128)(2,1)} %bitcast.12), kind=kOutput, calls=%fused_computation.27 | convolution fusion | flops 2417491968 | bytes 7471104 | tf_op jit(solution)/shard_map/dot_general | solution.py:32
  274.6 0.0 copy-done.6
  274.6 0.0 copy-start.8
  274.6 6.3 %fusion.11 = bf16[1,2048,768]{2,1,0:T(8,128)(2,1)} fusion(bf16[768,2048]{1,0:T(8,128)(2,1)} %bitcast.4, bf16[768,768]{1,0:T(8,128)(2,1)S(1)} %copy-done.6), kind=kOutput, calls=%fused_computation.25 | convolution fusion | flops 2417491968 | bytes 7471104 | tf_op jit(solution)/shard_map/dot_general | solution.py:33
  280.9 0.0 copy-done.8
  280.9 6.2 %fusion.12 = bf16[1,2048,768]{2,1,0:T(8,128)(2,1)} fusion(bf16[768,2048]{1,0:T(8,128)(2,1)} %bitcast.4, bf16[768,768]{1,0:T(8,128)(2,1)S(1)} %copy-done.8), kind=kOutput, calls=%fused_computation.26 | convolution fusion | flops 2417491968 | bytes 7471104 | tf_op jit(solution)/shard_map/dot_general | solution.py:34
  287.2 3.9 %concatenate.15 = bf16[769,2048]{1,0:T(8,128)(2,1)} pad(bf16[768,2048]{1,0:T(8,128)(2,1)} %bitcast.14, bf16[]{:T(256)} %constant.14.clone.1), padding=0_1x0_0 | pad | bytes 6295554 | tf_op jit(solution)/shard_map/concatenate | solution.py:82
  291.1 7.6 %gather_fusion.3 = bf16[512,2048]{1,0:T(8,128)(2,1)} fusion(bf16[769,2048]{1,0:T(8,128)(2,1)} %concatenate.15, s32[1024]{0:T(1024)S(1)} %pad_clamp_fusion), kind=kCustom, calls=%fused_computation.3 | custom fusion | bytes 4196352 | tf_op jit(solution)/shard_map/gather | solution.py:84
  298.7 4.3 %reshape.139 = bf16[128,4,2048]{2,1,0:T(4,128)(2,1)} reshape(bf16[512,2048]{1,0:T(8,128)(2,1)} %gather_fusion.3) | data formatting | bytes 4194304 | tf_op jit(solution)/shard_map/reshape | solution.py:84
  303.1 5.0 %reduce_sum.44 = bf16[128,2048]{1,0:T(8,128)(2,1)} reduce(bf16[128,4,2048]{2,1,0:T(4,128)(2,1)} %reshape.139, bf16[]{:T(256)} %constant.14.clone.1), dimensions={1}, to_apply=%region_6.7 | reduce | flops 786432 | bytes 2621442 | tf_op jit(solution)/shard_map/reduce_sum | solution.py:87
  308.1 29.1 %all-to-all-done.1 = bf16[32,24,2048]{2,1,0:T(8,128)(2,1)} async-done(((bf16[32,24,2048]{2,1,0:T(8,128)(2,1)}), bf16[32,24,2048]{2,1,0:T(8,128)(2,1)}, u32[]{:S(2)}, u32[]{:S(2)}) %all-to-all-start.1) | async-done | bytes 3145760 | tf_op jit(solution)/shard_map/all_to_all | solution.py:77
  337.2 4.0 %concatenate.13 = bf16[769,2048]{1,0:T(8,128)(2,1)} pad(bf16[768,2048]{1,0:T(8,128)(2,1)} %bitcast.9, bf16[]{:T(256)} %constant.14.clone.1), padding=0_1x0_0 | pad | bytes 6295554 | tf_op jit(solution)/shard_map/concatenate | solution.py:81
  341.2 7.6 %gather_fusion.1 = bf16[512,2048]{1,0:T(8,128)(2,1)} fusion(bf16[769,2048]{1,0:T(8,128)(2,1)} %concatenate.13, s32[1024]{0:T(1024)S(1)} %pad_clamp_fusion), kind=kCustom, calls=%fused_computation.1 | custom fusion | bytes 4196352 | tf_op jit(solution)/shard_map/gather | solution.py:83
  348.8 4.8 %reshape.140 = f32[128,4,2048]{2,1,0:T(4,128)} reshape(bf16[512,2048]{1,0:T(8,128)(2,1)} %gather_fusion.1) | data formatting | bytes 6291456 | tf_op jit(solution)/shard_map/convert_element_type | solution.py:83
  353.6 6.6 %multiply_reduce_fusion = (f32[128,4]{1,0:T(8,128)S(1)}, bf16[128,2048]{1,0:T(8,128)(2,1)}) fusion(f32[128,4,2048]{2,1,0:T(4,128)} %reshape.140, f32[128,2048]{1,0:T(8,128)} %convert_element_type.73, f32[128,4]{1,0:T(8,128)S(1)} %copy.20), kind=kLoop, calls=%fused_computation.9 | loop fusion | flops 3931648 | bytes 5771264 | tf_op jit(solution)/shard_map/reduce_sum | solution.py:86
  360.2 0.7 copy.26
  (9 shorter events, 0.1 us)
Async XLA Ops:
  0.6 170.8 %copy-start = (bf16[1,768,2048]{2,1,0:T(8,128)(2,1)S(1)}, bf16[1,768,2048]{2,1,0:T(8,128)(2,1)}, u32[]{:S(2)}) copy-start(bf16[1,768,2048]{2,1,0:T(8,128)(2,1)} %param.13) | copy-start | bytes 9437188
  16.9 78.9 %all-to-all-start = ((bf16[32,24,2048]{2,1,0:T(8,128)(2,1)}), bf16[32,24,2048]{2,1,0:T(8,128)(2,1)}, u32[]{:S(2)}, u32[]{:S(2)}) async-start(bf16[32,24,2048]{2,1,0:T(8,128)(2,1)} %bitcast.66), calls=%async_computation | async-start | bytes 6291456 | tf_op jit(solution)/shard_map/all_to_all | solution.py:64
  26.2 8.2 %copy-start.1 = (f32[128,4]{0,1:T(4,128)S(1)}, f32[128,4]{0,1:T(4,128)}, u32[]{:S(2)}) copy-start(f32[128,4]{0,1:T(4,128)} %param.10) | copy-start | bytes 6148
  95.8 75.7 %all-to-all-start.2 = ((bf16[32,24,2048]{2,1,0:T(8,128)(2,1)}), bf16[32,24,2048]{2,1,0:T(8,128)(2,1)}, u32[]{:S(2)}, u32[]{:S(2)}) async-start(bf16[32,24,2048]{2,1,0:T(8,128)(2,1)} %fusion), calls=%async_computation.2 | async-start | bytes 6291456 | tf_op jit(solution)/shard_map/all_to_all | solution.py:65
  100.0 7.0 %copy-start.2 = (bf16[1,2048,768]{2,1,0:T(8,128)(2,1)S(1)}, bf16[1,2048,768]{2,1,0:T(8,128)(2,1)}, u32[]{:S(2)}) copy-start(bf16[1,2048,768]{2,1,0:T(8,128)(2,1)} %param.11) | copy-start | bytes 9437188
  171.4 7.8 %copy-start.3 = (bf16[1,2048,768]{2,1,0:T(8,128)(2,1)S(1)}, bf16[1,2048,768]{2,1,0:T(8,128)(2,1)}, u32[]{:S(2)}) copy-start(bf16[1,2048,768]{2,1,0:T(8,128)(2,1)} %param.11) | copy-start | bytes 9437188
  179.3 2.7 copy-start.5
  179.3 2.7 copy-start.7
  179.3 2.7 copy-start.4
  186.0 75.5 %all-to-all-start.3 = ((bf16[32,24,2048]{2,1,0:T(8,128)(2,1)}), bf16[32,24,2048]{2,1,0:T(8,128)(2,1)}, u32[]{:S(2)}, u32[]{:S(2)}) async-start(bf16[32,24,2048]{2,1,0:T(8,128)(2,1)} %bitcast.69), calls=%async_computation.3 | async-start | bytes 6291456 | tf_op jit(solution)/shard_map/all_to_all | solution.py:78
  261.5 75.7 %all-to-all-start.1 = ((bf16[32,24,2048]{2,1,0:T(8,128)(2,1)}), bf16[32,24,2048]{2,1,0:T(8,128)(2,1)}, u32[]{:S(2)}, u32[]{:S(2)}) async-start(bf16[32,24,2048]{2,1,0:T(8,128)(2,1)} %bitcast.68), calls=%async_computation.1 | async-start | bytes 6291456 | tf_op jit(solution)/shard_map/all_to_all | solution.py:77
  267.9 6.7 %copy-start.6 = (bf16[768,768]{1,0:T(8,128)(2,1)S(1)}, bf16[768,768]{1,0:T(8,128)(2,1)}, u32[]{:S(2)}) copy-start(bf16[768,768]{1,0:T(8,128)(2,1)} %copy-done.5) | copy-start | bytes 3538948
  274.6 6.3 %copy-start.8 = (bf16[768,768]{1,0:T(8,128)(2,1)S(1)}, bf16[768,768]{1,0:T(8,128)(2,1)}, u32[]{:S(2)}) copy-start(bf16[768,768]{1,0:T(8,128)(2,1)} %copy-done.7) | copy-start | bytes 3538948
where the time goes:
time: 368 us; the launch traced here: 361 us
  waiting for transfers between devices  208 us (57%)
  local copies, waits for them, and re-layouts  60.1 us (16%)
  matrix products  51.9 us (14%)
  other arithmetic  19.9 us (5%)
  starting transfers between devices  19.9 us (5%)
    all_to_all x1, waiting for transfers between devices, local(): lax.all_to_all(dx_buf, ('group', 'local'), split_axis=0, concat_axis=0, t...  66.2 us
    all_to_all x1, waiting for transfers between devices, local(): lax.all_to_all(send_z, ('group', 'local'), split_axis=0, concat_axis=0, t...  58.5 us
    all_to_all x1, waiting for transfers between devices, local(): lax.all_to_all(send_x, ('group', 'local'), split_axis=0, concat_axis=0, t...  54.4 us
    all_to_all x1, waiting for transfers between devices, local(): lax.all_to_all(out_buf, ('group', 'local'), split_axis=0, concat_axis=0,...  29.1 us
    gather x1, local copies, waits for them, and re-layouts, local(): cot_pad[token_table].astype(jnp.float32)  8.23 us
    gather x1, local copies, waits for them, and re-layouts, local(): send_x = tokens_pad[token_table].reshape(devices_count, capacity, width)  8.21 us
    dot_general x1, matrix products, expert_pass(): d_hidden = jnp.dot(rows_z, wd.T, preferred_element_type=jnp.float32)  7.82 us
    gather x1, local copies, waits for them, and re-layouts, local(): dx_pad[slots].reshape(tok_rows, top_count, width).astype(jnp.float32)  7.63 us
  transfers between devices with their start and end apart: 4, of which 4 were waited for; matrix products, arithmetic and copies ran while one was open for 21% of the time, Pallas kernels for 0%

commit v1 on v0

v1 whole, which is shorter than its diff:
```python
import functools

import jax
import jax.numpy as jnp
from jax import lax
from jax.experimental import pallas as pl
from jax.experimental.pallas import tpu as pltpu
from jax.sharding import PartitionSpec as P

F32 = jnp.float32
BF16 = jnp.bfloat16
META = 128
VMEM_BYTES = 50 << 20


def split3(v):
    hi = v.astype(BF16)
    rest = v - hi.astype(F32)
    mid = rest.astype(BF16)
    low = (rest - mid.astype(F32)).astype(BF16)
    return hi, mid, low


def dot(a, b, ca=1, cb=0):
    return lax.dot_general(a, b, (((ca,), (cb,)), ((), ())), preferred_element_type=F32)


def selection(meta, tab, top):
    eid, place = tab[0:1, :], tab[1:2, :]
    tok = meta.shape[0]
    hits = [(meta[:, k : k + 1] == eid).astype(F32) for k in range(top)]
    hit = functools.reduce(lambda a, b: a + b, hits)
    gate = functools.reduce(
        lambda a, b: a + b,
        [
            hits[k]
            * (
                meta[:, top + k : top + k + 1]
                + meta[:, 2 * top + k : 2 * top + k + 1]
                + meta[:, 3 * top + k : 3 * top + k + 1]
            )
            for k in range(top)
        ],
    )
    row = lax.broadcasted_iota(jnp.int32, (tok, tok), 0)
    col = lax.broadcasted_iota(jnp.int32, (tok, tok), 1)
    earlier = (col < row).astype(F32).astype(BF16)
    rank = dot(earlier, hit.astype(BF16))
    sel = jnp.where(rank == place, hit, 0.0)
    return sel, gate, hits


def dispatch_kernel(top, width, tab_ref, buf_ref, *outs):
    meta = buf_ref[:, 2 * width :].astype(F32)
    sel, gate, _ = selection(meta, tab_ref[...], top)
    sel_t = sel.T
    gate_t = jnp.sum((sel * gate).T, axis=1, keepdims=True)
    pick = sel_t.astype(BF16)
    rows_p = outs[0].shape[0]
    step = 512
    for c in range(0, width, step):
        x = dot(pick, buf_ref[:, c : c + step])
        z = gate_t * dot(pick, buf_ref[:, width + c : width + c + step])
        for s, out in enumerate(outs):
            out[:, c : c + step] = x[s * rows_p : (s + 1) * rows_p].astype(BF16)
            out[:, width + c : width + c + step] = z[
                s * rows_p : (s + 1) * rows_p
            ].astype(BF16)


def gather_rows(pieces, lo, hi):
    return jnp.concatenate([p[:, lo:hi].astype(F32) for p in pieces], axis=0).astype(
        BF16
    )


def expert_kernel(count, width, *refs):
    pieces = refs[:count]
    wg_ref, wu_ref, wd_ref = refs[count : count + 3]
    rets = refs[count + 3 : 2 * count + 3]
    xz_ref, hid_ref, dpg_ref, dpu_ref, acc_o, acc_d = refs[2 * count + 3 :]
    f = pl.program_id(0)

    @pl.when(f == 0)
    def _():
        for c in range(0, 2 * width, 512):
            xz_ref[:, c : c + 512] = gather_rows(pieces, c, c + 512)

    wg, wu, wd = wg_ref[0], wu_ref[0], wd_ref[0]
    x = xz_ref[:, :width]
    pre_gate = dot(x, wg)
    pre_up = dot(x, wu)
    d_hidden = dot(xz_ref[:, width:], wd, 1, 1)
    sig = jax.nn.sigmoid(pre_gate)
    silu = pre_gate * sig
    hidden = (silu * pre_up).astype(BF16)
    d_pre_gate = (d_hidden * pre_up * sig * (1.0 + pre_gate * (1.0 - sig))).astype(BF16)
    d_pre_up = (d_hidden * silu).astype(BF16)
    hid_ref[...] = hidden
    dpg_ref[...] = d_pre_gate
    dpu_ref[...] = d_pre_up
    out = dot(hidden, wd)
    d_x = dot(d_pre_gate, wg, 1, 1) + dot(d_pre_up, wu, 1, 1)

    @pl.when(f == 0)
    def _():
        acc_o[...] = out
        acc_d[...] = d_x

    @pl.when(f > 0)
    def _():
        acc_o[...] += out
        acc_d[...] += d_x

    @pl.when(f == pl.num_programs(0) - 1)
    def _():
        rows_p = rets[0].shape[0]
        for s, ret in enumerate(rets):
            ret[:, :width] = acc_o[s * rows_p : (s + 1) * rows_p, :].astype(BF16)
            ret[:, width:] = acc_d[s * rows_p : (s + 1) * rows_p, :].astype(BF16)


def token_sums(top, width, tab_ref, buf_ref, pieces, emit):
    meta = buf_ref[:, 2 * width :].astype(F32)
    sel, gate, hits = selection(meta, tab_ref[...], top)
    plain = sel.astype(BF16)
    gated = split3(sel * gate)
    prod = None
    step = 512
    for c in range(0, width, step):
        out_rows = gather_rows(pieces, c, c + step)
        dx_rows = gather_rows(pieces, width + c, width + c + step)
        mixed = dot(gated[0], out_rows) + dot(gated[1], out_rows) + dot(gated[2], out_rows)
        d_tok = dot(plain, dx_rows)
        part = dot(buf_ref[:, width + c : width + c + step], out_rows, 1, 1)
        prod = part if prod is None else prod + part
        emit(c, c + step, mixed, d_tok)
    prod = prod * sel
    return [jnp.sum(prod * h, axis=1, keepdims=True) for h in hits]


def combine_kernel(count, top, width, tab_ref, buf_ref, *refs):
    pieces, part_ref = refs[:count], refs[count]

    def emit(lo, hi, mixed, d_tok):
        part_ref[:, lo:hi] = mixed.astype(BF16)
        part_ref[:, width + lo : width + hi] = d_tok.astype(BF16)

    d_gates = token_sums(top, width, tab_ref, buf_ref, pieces, emit)
    lane = lax.broadcasted_iota(jnp.int32, (buf_ref.shape[0], META), 1)
    packed = jnp.zeros((buf_ref.shape[0], META), F32)
    for k, column in enumerate(d_gates):
        for i, piece in enumerate(split3(column)):
            packed = jnp.where(lane == i * top + k, piece.astype(F32), packed)
    part_ref[:, 2 * width :] = packed.astype(BF16)


def final_kernel(count, others, top, width, tab_ref, buf_ref, *refs):
    pieces = refs[:count]
    parts = refs[count : count + others]
    mixed_ref, d_tok_ref, d_gates_ref = refs[count + others :]

    def emit(lo, hi, mixed, d_tok):
        for p in parts:
            mixed = mixed + p[:, lo:hi].astype(F32)
            d_tok = d_tok + p[:, width + lo : width + hi].astype(F32)
        mixed_ref[:, lo:hi] = mixed.astype(BF16)
        d_tok_ref[:, lo:hi] = d_tok.astype(BF16)

    d_gates = token_sums(top, width, tab_ref, buf_ref, pieces, emit)
    packs = [p[:, 2 * width :].astype(F32) for p in parts]
    for k, column in enumerate(d_gates):
        for p in packs:
            column = column + (
                p[:, k : k + 1]
                + p[:, top + k : top + k + 1]
                + p[:, 2 * top + k : 2 * top + k + 1]
            )
        d_gates_ref[:, k : k + 1] = column


def weight_grad_kernel(stages, *refs):
    xs, zs = refs[:stages], refs[stages : 2 * stages]
    hids, dpgs, dpus = (refs[i * stages : (i + 1) * stages] for i in (2, 3, 4))
    gate_ref, up_ref, down_ref = refs[5 * stages :]

    def total(lefts, rights):
        acc = None
        for a, b in zip(lefts, rights):
            t = dot(a[...], b[...], 0, 0)
            acc = t if acc is None else acc + t
        return acc.astype(BF16)

    gate_ref[0] = total(xs, dpgs)
    up_ref[0] = total(xs, dpus)
    down_ref[0] = total(hids, zs)


def whole(shape):
    return pl.BlockSpec(shape, lambda *_: (0,) * len(shape))


def params():
    return pltpu.CompilerParams(vmem_limit_bytes=VMEM_BYTES)


def local(tokens, cotangent, expert_ids, gates, w_gate, w_up, w_down):
    groups = lax.axis_size("group")
    count = lax.axis_size("local")
    tok, width = tokens.shape
    top = expert_ids.shape[1]
    hidden_width = w_gate.shape[2]
    capacity = max(2, 3 * tok * top // (2 * groups * count))
    rows_p = -(-capacity // 8) * 8
    slots = count * rows_p
    me = lax.axis_index("local")
    plane = lax.axis_index("group")

    at = jnp.arange(slots, dtype=jnp.int32)
    owner = plane * count + jnp.bitwise_xor(at // rows_p, me)
    place = jnp.where(at % rows_p < capacity, at % rows_p, -1)
    tab = jnp.concatenate(
        [owner[None].astype(F32), place[None].astype(F32), jnp.zeros((6, slots), F32)], 0
    )
    meta = jnp.concatenate(
        [expert_ids.astype(BF16), *split3(gates), jnp.zeros((tok, META - 4 * top), BF16)], 1
    )
    buf0 = jnp.concatenate([tokens, cotangent, meta], axis=1)
    wide = 2 * width + META

    piece = jax.ShapeDtypeStruct((rows_p, 2 * width), BF16)
    tile = 256
    steps = hidden_width // tile

    def dispatch(buf):
        return pl.pallas_call(
            functools.partial(dispatch_kernel, top, width),
            out_shape=[piece] * count,
            compiler_params=params(),
            cost_estimate=pl.CostEstimate(
                flops=4 * slots * tok * width,
                bytes_accessed=2 * (tok * wide + 2 * slots * width),
                transcendentals=0,
            ),
            name="dispatch",
        )(tab, buf)

    def swap(pieces):
        return [pieces[0]] + [
            lax.ppermute(pieces[s], "local", [(i, i ^ s) for i in range(count)])
            for s in range(1, count)
        ]

    def expert(pieces):
        mid = jax.ShapeDtypeStruct((slots, hidden_width), BF16)
        got = pl.pallas_call(
            functools.partial(expert_kernel, count, width),
            grid=(steps,),
            in_specs=[whole((rows_p, 2 * width))] * count
            + [pl.BlockSpec((1, width, tile), lambda f: (0, 0, f))] * 2
            + [pl.BlockSpec((1, tile, width), lambda f: (0, f, 0))],
            out_specs=[whole((rows_p, 2 * width))] * count
            + [whole((slots, 2 * width))]
            + [pl.BlockSpec((slots, tile), lambda f: (0, f))] * 3,
            out_shape=[piece] * count
            + [jax.ShapeDtypeStruct((slots, 2 * width), BF16)]
            + [mid] * 3,
            scratch_shapes=[pltpu.VMEM((slots, width), F32)] * 2,
            compiler_params=params(),
            cost_estimate=pl.CostEstimate(
                flops=12 * slots * width * hidden_width,
                bytes_accessed=2 * (3 * width * hidden_width + 8 * slots * width),
                transcendentals=slots * hidden_width,
            ),
            name="expert",
        )(*pieces, w_gate, w_up, w_down)
        return got[:count], got[count:]

    def combine(buf, pieces):
        return pl.pallas_call(
            functools.partial(combine_kernel, count, top, width),
            out_shape=jax.ShapeDtypeStruct((tok, wide), BF16),
            compiler_params=params(),
            cost_estimate=pl.CostEstimate(
                flops=10 * slots * tok * width,
                bytes_accessed=2 * (2 * tok * wide + 2 * slots * width),
                transcendentals=0,
            ),
            name="combine",
        )(tab, buf, *pieces)

    bufs = [buf0]
    for _ in range(1, groups):
        bufs.append(
            lax.ppermute(bufs[-1], "group", [(i, (i + 1) % groups) for i in range(groups)])
        )

    kept, home = [], []
    rets = []
    for k in range(groups):
        pieces = swap(dispatch(bufs[k]))
        ret, saved = expert(pieces)
        kept.append(saved)
        rets.append(ret)
        if k:
            back = swap(ret)
            part = combine(bufs[k], back)
            home.append(
                lax.ppermute(part, "group", [(i, (i - k) % groups) for i in range(groups)])
            )
    held = lax.optimization_barrier((*rets[0], *rets[-1]))
    back0 = swap(list(held[:count]))
    others = len(home)
    mixed, d_tokens, d_gates = pl.pallas_call(
        functools.partial(final_kernel, count, others, top, width),
        out_shape=[
            jax.ShapeDtypeStruct((tok, width), BF16),
            jax.ShapeDtypeStruct((tok, width), BF16),
            jax.ShapeDtypeStruct((tok, top), F32),
        ],
        compiler_params=params(),
        cost_estimate=pl.CostEstimate(
            flops=10 * slots * tok * width,
            bytes_accessed=2 * ((2 + others) * tok * wide + 2 * slots * width),
            transcendentals=0,
        ),
        name="final",
    )(tab, buf0, *back0, *home)

    d_tile = 256
    d_steps = width // d_tile
    full = [whole((slots, hidden_width))] * groups
    d_w_gate, d_w_up, d_w_down = pl.pallas_call(
        functools.partial(weight_grad_kernel, groups),
        grid=(d_steps,),
        in_specs=[pl.BlockSpec((slots, d_tile), lambda d: (0, d))] * groups
        + [pl.BlockSpec((slots, d_tile), lambda d: (0, d_steps + d))] * groups
        + full * 3,
        out_specs=[pl.BlockSpec((1, d_tile, hidden_width), lambda d: (0, d, 0))] * 2
        + [pl.BlockSpec((1, hidden_width, d_tile), lambda d: (0, 0, d))],
        out_shape=[
            jax.ShapeDtypeStruct((1, width, hidden_width), BF16),
            jax.ShapeDtypeStruct((1, width, hidden_width), BF16),
            jax.ShapeDtypeStruct((1, hidden_width, width), BF16),
        ],
        compiler_params=params(),
        cost_estimate=pl.CostEstimate(
            flops=6 * groups * slots * width * hidden_width,
            bytes_accessed=2 * (3 * width * hidden_width + 2 * groups * slots * width),
            transcendentals=0,
        ),
        name="weight_grads",
    )(
        *[s[0] for s in kept],
        *[s[0] for s in kept],
        *[s[1] for s in kept],
        *[s[2] for s in kept],
        *[s[3] for s in kept],
    )
    return mixed, d_tokens, d_gates, d_w_gate, d_w_up, d_w_down


def solution(mesh):
    rows = P(("group", "local"), None)
    cube = P(("group", "local"), None, None)
    return jax.shard_map(
        local,
        mesh=mesh,
        in_specs=(rows, rows, rows, rows, cube, cube, cube),
        out_specs=(rows, rows, rows, cube, cube, cube),
        check_vma=False,
    )
```

time: 368 us -> 295 us (0.80); the launches traced: 361 us -> 294 us
  Pallas kernels: 0 us -> 66.2 us
  waiting for transfers between devices: 208 us -> 152 us
  matrix products: 51.9 us -> 0 us
  local copies, waits for them, and re-layouts: 60.1 us -> 12.4 us
  starting transfers between devices: 19.9 us -> 61.3 us
  other arithmetic: 19.9 us -> 1.53 us
    all_to_all x4 -> x0, waiting for transfers between devices: 208 us -> none  [the longest x1 66.2 us: local(): lax.all_to_all(dx_buf, ('group', 'local'), split_axis=0, concat_axis=0, t...]
    ppermute x0 -> x62, waiting for transfers between devices: none -> 152 us  [the longest x56 77.7 us: swap(): lax.ppermute(pieces[s], 'local', [(i, i ^ s) for i in range(count)])]
    pallas_call x0 -> x13, Pallas kernels: none -> 66.2 us  [the longest x4 41.1 us: expert(): pl.pallas_call(functools.partial(expert_kernel, count, width), grid=(step...]
    ppermute x0 -> x62, starting transfers between devices: none -> 61.3 us  [the longest x56 53 us: swap(): lax.ppermute(pieces[s], 'local', [(i, i ^ s) for i in range(count)])]
    dot_general x9 -> x0, matrix products: 51.9 us -> none  [the longest x1 7.82 us: expert_pass(): d_hidden = jnp.dot(rows_z, wd.T, preferred_element_type=jnp.float32)]
    gather x4 -> x0, local copies, waits for them, and re-layouts: 31.7 us -> none  [the longest x1 8.23 us: local(): cot_pad[token_table].astype(jnp.float32)]
    all_to_all x4 -> x0, starting transfers between devices: 19.9 us -> none  [the longest x1 7.41 us: local(): lax.all_to_all(send_x, ('group', 'local'), split_axis=0, concat_axis=0, t...]
    reduce_sum x3 -> x0, other arithmetic: 11.7 us -> none  [the longest x1 6.63 us: local(): jnp.sum(cotangent.astype(jnp.float32)[:, None, :] * out_routes, axis=2)]
  transfers between devices with their start and end apart: 4 -> 62, of which waited for: 4 -> 21; matrix products, arithmetic and copies ran while one was open for 21% -> 0% of each run, Pallas kernels for 0% -> 21%
where the time goes in v1:
time: 295 us; the launch traced here: 294 us
  waiting for transfers between devices  152 us (52%)
  Pallas kernels  66.2 us (22%)
  starting transfers between devices  61.3 us (21%)
  local copies, waits for them, and re-layouts  12.4 us (4%)
    ppermute x56, waiting for transfers between devices, swap(): lax.ppermute(pieces[s], 'local', [(i, i ^ s) for i in range(count)])  77.7 us
    ppermute x56, starting transfers between devices, swap(): lax.ppermute(pieces[s], 'local', [(i, i ^ s) for i in range(count)])  53 us
    ppermute x3, waiting for transfers between devices, local(): lax.ppermute(bufs[-1], 'group', [(i, (i + 1) % groups) for i in range(gro...  49.6 us
    pallas_call x4, Pallas kernels, expert(): pl.pallas_call(functools.partial(expert_kernel, count, width), grid=(step...  41.1 us
    ppermute x3, waiting for transfers between devices, local(): lax.ppermute(part, 'group', [(i, (i - k) % groups) for i in range(groups)])  24.5 us
    pallas_call x1, Pallas kernels, local(): pl.pallas_call(functools.partial(weight_grad_kernel, groups), grid=(d_ste...  13.9 us
    unnamed x75, local copies, waits for them, and re-layouts  9.48 us
  transfers between devices with their start and end apart: 62, of which 21 were waited for; matrix products, arithmetic and copies ran while one was open for 0% of the time, Pallas kernels for 21%

profile of v1, /device:TPU:0, one launch (start us, length us, event | category | flops | bytes accessed | tf_op | source)
XLA Modules:
  0.0 294.4 jit_solution(2123503225803906303)
XLA Ops:
  2.6 2.3 concatenate.7.buf_ref
  5.0 3.1 %collective-permute-start.7 = (bf16[128,4224]{1,0:T(8,128)(2,1)S(1)}, bf16[128,4224]{1,0:T(8,128)(2,1)S(1)}, u32[]{:S(2)}, u32[]{:S(2)}) collective-permute-start(bf16[128,4224]{1,0:T(8,128)(2,1)S(1)} %concatenate.7.buf_ref), channel_id=1, source_target_pairs={{0,8},{8,16},{16,24},{24,0},{1,9},{9,17},{17,25},{25,1},{2,10},{10... | collective-permute-start | bytes 3244040 | tf_op jit(solution)/shard_map/ppermute | solution.py:295
  8.1 25.9 %collective-permute-done.7.buf_ref = bf16[128,4224]{1,0:T(8,128)(2,1)S(1)} collective-permute-done((bf16[128,4224]{1,0:T(8,128)(2,1)S(1)}, bf16[128,4224]{1,0:T(8,128)(2,1)S(1)}, u32[]{:S(2)}, u32[]{:S(2)}) %collective-permute-start.7) | collective-permute-done | bytes 1081376 | tf_op jit(solution)/shard_map/ppermute | solution.py:295
  34.1 0.9 dispatch.4
  37.0 23.8 %collective-permute-done.8.buf_ref = bf16[128,4224]{1,0:T(8,128)(2,1)S(1)} collective-permute-done((bf16[128,4224]{1,0:T(8,128)(2,1)S(1)}, bf16[128,4224]{1,0:T(8,128)(2,1)S(1)}, u32[]{:S(2)}, u32[]{:S(2)}) %collective-permute-start.8) | collective-permute-done | bytes 1081376 | tf_op jit(solution)/shard_map/ppermute | solution.py:295
  60.8 1.2 collective-permute-start.1
  62.0 0.9 dispatch.6
  62.9 1.0 collective-permute-start.24
  63.9 1.2 collective-permute-start.25
  65.1 2.8 collective-permute-done.1.refs_2_
  68.0 3.4 %collective-permute-done.2.refs_3_ = bf16[24,4096]{1,0:T(8,128)(2,1)S(1)} collective-permute-done((bf16[24,4096]{1,0:T(8,128)(2,1)S(1)}, bf16[24,4096]{1,0:T(8,128)(2,1)S(1)}, u32[]{:S(2)}, u32[]{:S(2)}) %collective-permute-start.2) | collective-permute-done | bytes 196640 | tf_op jit(solution)/shard_map/ppermute | solution.py:250
  71.3 1.7 collective-permute-start.27
  73.6 2.7 collective-permute-done.25.refs_2_
  76.4 2.8 collective-permute-start.29
  80.1 3.0 %collective-permute-start.30 = (bf16[24,4096]{1,0:T(8,128)(2,1)S(1)}, bf16[24,4096]{1,0:T(8,128)(2,1)S(1)}, u32[]{:S(2)}, u32[]{:S(2)}) collective-permute-start(bf16[24,4096]{1,0:T(8,128)(2,1)S(1)} %get-tuple-element.147), channel_id=1, source_target_pairs={{0,7},{1,6},{2,5},{3,4},{4,3},{5,2},{6,1},{7,0},{8,15},{9,14},{10,... | collective-permute-start | bytes 589832 | tf_op jit(solution)/shard_map/ppermute | solution.py:250
  83.1 8.6 %collective-permute-done.28.refs_5_ = bf16[24,4096]{1,0:T(8,128)(2,1)S(1)} collective-permute-done((bf16[24,4096]{1,0:T(8,128)(2,1)S(1)}, bf16[24,4096]{1,0:T(8,128)(2,1)S(1)}, u32[]{:S(2)}, u32[]{:S(2)}) %collective-permute-start.28) | collective-permute-done | bytes 196640 | tf_op jit(solution)/shard_map/ppermute | solution.py:250
  92.1 1.0 collective-permute-start.41
  93.9 1.3 collective-permute-start.43
  95.2 4.2 %collective-permute-done.40.refs_2_ = bf16[24,4096]{1,0:T(8,128)(2,1)S(1)} collective-permute-done((bf16[24,4096]{1,0:T(8,128)(2,1)S(1)}, bf16[24,4096]{1,0:T(8,128)(2,1)S(1)}, u32[]{:S(2)}, u32[]{:S(2)}) %collective-permute-start.40) | collective-permute-done | bytes 196640 | tf_op jit(solution)/shard_map/ppermute | solution.py:250
  99.4 0.9 collective-permute-start.44
  100.4 1.6 collective-permute-done.41.refs_3_
  102.0 2.3 collective-permute-start.45
  104.3 10.3 %expert.6 = (bf16[24,4096]{1,0:T(8,128)(2,1)S(1)}, bf16[24,4096]{1,0:T(8,128)(2,1)S(1)}, bf16[24,4096]{1,0:T(8,128)(2,1)S(1)}, bf16[24,4096]{1,0:T(8,128)(2,1)S(...) custom-call(bf16[24,4096]{1,0:T(8,128)(2,1)S(1)} %get-tuple-element., ...), custom_call_target="tpu_custom_call" | custom-call | flops 3623878656 | bytes 15728640 | tf_op jit(solution)/shard_map/expert/pallas_call | solution.py:256
  117.7 1.0 collective-permute-start.33
  118.7 1.0 collective-permute-start.34
  120.4 10.2 %expert.7 = (bf16[24,4096]{1,0:T(8,128)(2,1)S(1)}, bf16[24,4096]{1,0:T(8,128)(2,1)S(1)}, bf16[24,4096]{1,0:T(8,128)(2,1)S(1)}, bf16[24,4096]{1,0:T(8,128)(2,1)S(...) custom-call(bf16[24,4096]{1,0:T(8,128)(2,1)S(1)} %get-tuple-element., ...), custom_call_target="tpu_custom_call" | custom-call | flops 3623878656 | bytes 15728640 | tf_op jit(solution)/shard_map/expert/pallas_call | solution.py:256
  131.5 2.1 collective-permute-start.36
  135.6 4.6 %collective-permute-done.36.refs_6_ = bf16[24,4096]{1,0:T(8,128)(2,1)S(1)} collective-permute-done((bf16[24,4096]{1,0:T(8,128)(2,1)S(1)}, bf16[24,4096]{1,0:T(8,128)(2,1)S(1)}, u32[]{:S(2)}, u32[]{:S(2)}) %collective-permute-start.36) | collective-permute-done | bytes 196640 | tf_op jit(solution)/shard_map/ppermute | solution.py:250
  140.2 3.3 %collective-permute-done.37.refs_7_ = bf16[24,4096]{1,0:T(8,128)(2,1)S(1)} collective-permute-done((bf16[24,4096]{1,0:T(8,128)(2,1)S(1)}, bf16[24,4096]{1,0:T(8,128)(2,1)S(1)}, u32[]{:S(2)}, u32[]{:S(2)}) %collective-permute-start.37) | collective-permute-done | bytes 196640 | tf_op jit(solution)/shard_map/ppermute | solution.py:250
  143.5 1.0 collective-permute-start.13
  144.5 1.1 collective-permute-start.14
  145.6 2.0 collective-permute-start.15
  148.2 3.3 %collective-permute-done.12.refs_3_ = bf16[24,4096]{1,0:T(8,128)(2,1)S(1)} collective-permute-done((bf16[24,4096]{1,0:T(8,128)(2,1)S(1)}, bf16[24,4096]{1,0:T(8,128)(2,1)S(1)}, u32[]{:S(2)}, u32[]{:S(2)}) %collective-permute-start.12) | collective-permute-done | bytes 196640 | tf_op jit(solution)/shard_map/ppermute | solution.py:250
  151.5 1.6 collective-permute-start.47
  153.8 9.6 %collective-permute-done.14.refs_5_ = bf16[24,4096]{1,0:T(8,128)(2,1)S(1)} collective-permute-done((bf16[24,4096]{1,0:T(8,128)(2,1)S(1)}, bf16[24,4096]{1,0:T(8,128)(2,1)S(1)}, u32[]{:S(2)}, u32[]{:S(2)}) %collective-permute-start.14) | collective-permute-done | bytes 196640 | tf_op jit(solution)/shard_map/ppermute | solution.py:250
  163.4 1.0 collective-permute-start.49
  165.1 2.0 collective-permute-start.51
  167.1 10.2 %expert.5 = (bf16[24,4096]{1,0:T(8,128)(2,1)S(1)}, bf16[24,4096]{1,0:T(8,128)(2,1)S(1)}, bf16[24,4096]{1,0:T(8,128)(2,1)S(1)}, bf16[24,4096]{1,0:T(8,128)(2,1)S(...) custom-call(bf16[24,4096]{1,0:T(8,128)(2,1)S(1)} %get-tuple-element., ...), custom_call_target="tpu_custom_call" | custom-call | flops 3623878656 | bytes 15728640 | tf_op jit(solution)/shard_map/expert/pallas_call | solution.py:256
  181.9 0.9 collective-permute-start.55
  183.5 1.4 combine.3
  184.9 4.1 %collective-permute-start.38 = (bf16[128,4224]{1,0:T(8,128)(2,1)S(1)}, bf16[128,4224]{1,0:T(8,128)(2,1)S(1)}, u32[]{:S(2)}, u32[]{:S(2)}) collective-permute-start(bf16[128,4224]{1,0:T(8,128)(2,1)S(1)} %combine.3), channel_id=1, source_target_pairs={{0,24},{8,0},{16,8},{24,16},{1,25},{9,1},{17,9},{25,17},{2,26},{10... | collective-permute-start | bytes 3244040 | tf_op jit(solution)/shard_map/ppermute | solution.py:309
  189.0 1.1 collective-permute-start.57
  190.7 2.0 collective-permute-done.55.refs_2_
  192.7 1.5 collective-permute-start.59
  194.2 1.9 collective-permute-done.56.refs_3_
  196.1 2.0 collective-permute-start.60
  198.1 0.9 collective-permute-start.3
  199.1 9.2 %collective-permute-done.58.refs_5_ = bf16[24,4096]{1,0:T(8,128)(2,1)S(1)} collective-permute-done((bf16[24,4096]{1,0:T(8,128)(2,1)S(1)}, bf16[24,4096]{1,0:T(8,128)(2,1)S(1)}, u32[]{:S(2)}, u32[]{:S(2)}) %collective-permute-start.58) | collective-permute-done | bytes 196640 | tf_op jit(solution)/shard_map/ppermute | solution.py:250
  208.2 1.9 collective-permute-start.4
  210.1 1.5 collective-permute-start.5
  211.8 1.3 combine.4
  213.2 1.4 combine.5
  214.6 7.4 %collective-permute-done.3.refs_4_ = bf16[24,4096]{1,0:T(8,128)(2,1)S(1)} collective-permute-done((bf16[24,4096]{1,0:T(8,128)(2,1)S(1)}, bf16[24,4096]{1,0:T(8,128)(2,1)S(1)}, u32[]{:S(2)}, u32[]{:S(2)}) %collective-permute-start.3) | collective-permute-done | bytes 196640 | tf_op jit(solution)/shard_map/ppermute | solution.py:250
  222.0 3.1 %collective-permute-done.4.refs_5_ = bf16[24,4096]{1,0:T(8,128)(2,1)S(1)} collective-permute-done((bf16[24,4096]{1,0:T(8,128)(2,1)S(1)}, bf16[24,4096]{1,0:T(8,128)(2,1)S(1)}, u32[]{:S(2)}, u32[]{:S(2)}) %collective-permute-start.4) | collective-permute-done | bytes 196640 | tf_op jit(solution)/shard_map/ppermute | solution.py:250
  225.1 1.1 collective-permute-start.61
  226.3 10.3 %expert.4 = (bf16[24,4096]{1,0:T(8,128)(2,1)S(1)}, bf16[24,4096]{1,0:T(8,128)(2,1)S(1)}, bf16[24,4096]{1,0:T(8,128)(2,1)S(1)}, bf16[24,4096]{1,0:T(8,128)(2,1)S(...) custom-call(bf16[24,4096]{1,0:T(8,128)(2,1)S(1)} %get-tuple-element., ...), custom_call_target="tpu_custom_call" | custom-call | flops 3623878656 | bytes 15728640 | tf_op jit(solution)/shard_map/expert/pallas_call | solution.py:256
  237.1 1.4 collective-permute-start.19
  238.5 5.8 %collective-permute-done.18.refs_2_ = bf16[24,4096]{1,0:T(8,128)(2,1)S(1)} collective-permute-done((bf16[24,4096]{1,0:T(8,128)(2,1)S(1)}, bf16[24,4096]{1,0:T(8,128)(2,1)S(1)}, u32[]{:S(2)}, u32[]{:S(2)}) %collective-permute-start.18) | collective-permute-done | bytes 196640 | tf_op jit(solution)/shard_map/ppermute | solution.py:250
  244.3 3.4 %collective-permute-done.19.refs_3_ = bf16[24,4096]{1,0:T(8,128)(2,1)S(1)} collective-permute-done((bf16[24,4096]{1,0:T(8,128)(2,1)S(1)}, bf16[24,4096]{1,0:T(8,128)(2,1)S(1)}, u32[]{:S(2)}, u32[]{:S(2)}) %collective-permute-start.19) | collective-permute-done | bytes 196640 | tf_op jit(solution)/shard_map/ppermute | solution.py:250
  248.6 1.9 collective-permute-start.23
  250.6 13.9 %weight_grads.1 = (bf16[1,2048,768]{2,1,0:T(8,128)(2,1)}, bf16[1,2048,768]{2,1,0:T(8,128)(2,1)}, bf16[1,768,2048]{2,1,0:T(8,128)(2,1)}) custom-call(bf16[192,4096]{1,0:T(8,128)(2,1)} %get-tuple-element.175.refs_0_.refs_4_, bf16[192,4096]{1,0:T(8,128)(2,1)} %get-tuple-element.176.refs_1_.refs_5_, bf16[192,4096]{1,0:T(8,128)(2,1)} %get-tuple-element.177.refs_2_.refs_6_, ...), custom_call_target="tpu_custom_call" | custom-call | flops 7247757312 | bytes 15728640 | tf_op jit(solution)/shard_map/weight_grads/pallas_call | solution.py:333
  264.5 24.5 %collective-permute-done.53.refs_9_ = bf16[128,4224]{1,0:T(8,128)(2,1)S(1)} collective-permute-done((bf16[128,4224]{1,0:T(8,128)(2,1)S(1)}, bf16[128,4224]{1,0:T(8,128)(2,1)S(1)}, u32[]{:S(2)}, u32[]{:S(2)}) %collective-permute-start.53) | collective-permute-done | bytes 1081376 | tf_op jit(solution)/shard_map/ppermute | solution.py:309
  289.0 1.0 copy-done.36
  290.0 3.7 %final.1 = (bf16[128,2048]{1,0:T(8,128)(2,1)}, bf16[128,2048]{1,0:T(8,128)(2,1)}, f32[128,4]{1,0:T(8,128)S(1)}) custom-call(f32[8,192]{1,0:T(8,128)S(1)} %maximum_maximum_fusion.tab_ref, bf16[128,4224]{1,0:T(8,128)(2,1)S(1)} %concatenate.7.buf_ref, bf16[24,4096]{1,0:T(8,128)(2,1)S(1)} %get-tuple-element.132.refs_0_, ...), custom_call_target="tpu_custom_call" | custom-call | flops 503316480 | bytes 6979584 | tf_op jit(solution)/shard_map/final/pallas_call | solution.py:314
  (160 shorter events, 23.7 us)
Async XLA Ops:
  5.0 29.0 %collective-permute-start.7 = (bf16[128,4224]{1,0:T(8,128)(2,1)S(1)}, bf16[128,4224]{1,0:T(8,128)(2,1)S(1)}, u32[]{:S(2)}, u32[]{:S(2)}) collective-permute-start(bf16[128,4224]{1,0:T(8,128)(2,1)S(1)} %concatenate.7.buf_ref), channel_id=1, source_target_pairs={{0,8},{8,16},{16,24},{24,0},{1,9},{9,17},{17,25},{25,1},{2,10},{10... | collective-permute-start | bytes 3244040 | tf_op jit(solution)/shard_map/ppermute | solution.py:295
  33.9 26.8 %collective-permute-start.8 = (bf16[128,4224]{1,0:T(8,128)(2,1)S(1)}, bf16[128,4224]{1,0:T(8,128)(2,1)S(1)}, u32[]{:S(2)}, u32[]{:S(2)}) collective-permute-start(bf16[128,4224]{1,0:T(8,128)(2,1)S(1)} %collective-permute-done.7.buf_ref), channel_id=1, source_target_pairs={{0,8},{8,16},{16,24},{24,0},{1,9},{9,17},{17,25},{25,1},{2,10},{10... | collective-permute-start | bytes 3244040 | tf_op jit(solution)/shard_map/ppermute | solution.py:295
  37.0 67.3 %copy-start.12 = (bf16[24,4096]{1,0:T(8,128)(2,1)}, bf16[24,4096]{1,0:T(8,128)(2,1)S(1)}, u32[]{:S(2)}) copy-start(bf16[24,4096]{1,0:T(8,128)(2,1)S(1)} %get-tuple-element.104) | copy-start | bytes 589828
  37.0 26.8 %collective-permute-start = (bf16[24,4096]{1,0:T(8,128)(2,1)S(1)}, bf16[24,4096]{1,0:T(8,128)(2,1)S(1)}, u32[]{:S(2)}, u32[]{:S(2)}) collective-permute-start(bf16[24,4096]{1,0:T(8,128)(2,1)S(1)} %get-tuple-element.101), channel_id=1, source_target_pairs={{0,1},{1,0},{2,3},{3,2},{4,5},{5,4},{6,7},{7,6},{8,9},{9,8},{10,11... | collective-permute-start | bytes 589832 | tf_op jit(solution)/shard_map/ppermute | solution.py:250
  60.8 58.9 %collective-permute-start.9 = (bf16[128,4224]{1,0:T(8,128)(2,1)S(1)}, bf16[128,4224]{1,0:T(8,128)(2,1)S(1)}, u32[]{:S(2)}, u32[]{:S(2)}) collective-permute-start(bf16[128,4224]{1,0:T(8,128)(2,1)S(1)} %collective-permute-done.8.buf_ref), channel_id=1, source_target_pairs={{0,8},{8,16},{16,24},{24,0},{1,9},{9,17},{17,25},{25,1},{2,10},{10... | collective-permute-start | bytes 3244040 | tf_op jit(solution)/shard_map/ppermute | solution.py:295
  60.8 7.2 %collective-permute-start.1 = (bf16[24,4096]{1,0:T(8,128)(2,1)S(1)}, bf16[24,4096]{1,0:T(8,128)(2,1)S(1)}, u32[]{:S(2)}, u32[]{:S(2)}) collective-permute-start(bf16[24,4096]{1,0:T(8,128)(2,1)S(1)} %get-tuple-element.102), channel_id=1, source_target_pairs={{0,2},{1,3},{2,0},{3,1},{4,6},{5,7},{6,4},{7,5},{8,10},{9,11},{10,... | collective-permute-start | bytes 589832 | tf_op jit(solution)/shard_map/ppermute | solution.py:250
  62.0 9.3 %collective-permute-start.2 = (bf16[24,4096]{1,0:T(8,128)(2,1)S(1)}, bf16[24,4096]{1,0:T(8,128)(2,1)S(1)}, u32[]{:S(2)}, u32[]{:S(2)}) collective-permute-start(bf16[24,4096]{1,0:T(8,128)(2,1)S(1)} %get-tuple-element.103), channel_id=1, source_target_pairs={{0,3},{1,2},{2,1},{3,0},{4,7},{5,6},{6,5},{7,4},{8,11},{9,10},{10,... | collective-permute-start | bytes 589832 | tf_op jit(solution)/shard_map/ppermute | solution.py:250
  62.9 10.2 %collective-permute-start.24 = (bf16[24,4096]{1,0:T(8,128)(2,1)S(1)}, bf16[24,4096]{1,0:T(8,128)(2,1)S(1)}, u32[]{:S(2)}, u32[]{:S(2)}) collective-permute-start(bf16[24,4096]{1,0:T(8,128)(2,1)S(1)} %get-tuple-element.141), channel_id=1, source_target_pairs={{0,1},{1,0},{2,3},{3,2},{4,5},{5,4},{6,7},{7,6},{8,9},{9,8},{10,11... | collective-permute-start | bytes 589832 | tf_op jit(solution)/shard_map/ppermute | solution.py:250
  63.9 40.4 %copy-start = (bf16[24,4096]{1,0:T(8,128)(2,1)}, bf16[24,4096]{1,0:T(8,128)(2,1)S(1)}, u32[]{:S(2)}) copy-start(bf16[24,4096]{1,0:T(8,128)(2,1)S(1)} %collective-permute-done.refs_1_) | copy-start | bytes 589828
  63.9 12.5 %collective-permute-start.25 = (bf16[24,4096]{1,0:T(8,128)(2,1)S(1)}, bf16[24,4096]{1,0:T(8,128)(2,1)S(1)}, u32[]{:S(2)}, u32[]{:S(2)}) collective-permute-start(bf16[24,4096]{1,0:T(8,128)(2,1)S(1)} %get-tuple-element.142), channel_id=1, source_target_pairs={{0,2},{1,3},{2,0},{3,1},{4,6},{5,7},{6,4},{7,5},{8,10},{9,11},{10,... | collective-permute-start | bytes 589832 | tf_op jit(solution)/shard_map/ppermute | solution.py:250
  68.0 12.1 %collective-permute-start.26 = (bf16[24,4096]{1,0:T(8,128)(2,1)S(1)}, bf16[24,4096]{1,0:T(8,128)(2,1)S(1)}, u32[]{:S(2)}, u32[]{:S(2)}) collective-permute-start(bf16[24,4096]{1,0:T(8,128)(2,1)S(1)} %get-tuple-element.143), channel_id=1, source_target_pairs={{0,3},{1,2},{2,1},{3,0},{4,7},{5,6},{6,5},{7,4},{8,11},{9,10},{10,... | collective-permute-start | bytes 589832 | tf_op jit(solution)/shard_map/ppermute | solution.py:250
  71.3 11.8 %collective-permute-start.27 = (bf16[24,4096]{1,0:T(8,128)(2,1)S(1)}, bf16[24,4096]{1,0:T(8,128)(2,1)S(1)}, u32[]{:S(2)}, u32[]{:S(2)}) collective-permute-start(bf16[24,4096]{1,0:T(8,128)(2,1)S(1)} %get-tuple-element.144), channel_id=1, source_target_pairs={{0,4},{1,5},{2,6},{3,7},{4,0},{5,1},{6,2},{7,3},{8,12},{9,13},{10,... | collective-permute-start | bytes 589832 | tf_op jit(solution)/shard_map/ppermute | solution.py:250
  73.1 18.6 %collective-permute-start.28 = (bf16[24,4096]{1,0:T(8,128)(2,1)S(1)}, bf16[24,4096]{1,0:T(8,128)(2,1)S(1)}, u32[]{:S(2)}, u32[]{:S(2)}) collective-permute-start(bf16[24,4096]{1,0:T(8,128)(2,1)S(1)} %get-tuple-element.145), channel_id=1, source_target_pairs={{0,5},{1,4},{2,7},{3,6},{4,1},{5,0},{6,3},{7,2},{8,13},{9,12},{10,... | collective-permute-start | bytes 589832 | tf_op jit(solution)/shard_map/ppermute | solution.py:250
  76.4 15.8 %collective-permute-start.29 = (bf16[24,4096]{1,0:T(8,128)(2,1)S(1)}, bf16[24,4096]{1,0:T(8,128)(2,1)S(1)}, u32[]{:S(2)}, u32[]{:S(2)}) collective-permute-start(bf16[24,4096]{1,0:T(8,128)(2,1)S(1)} %get-tuple-element.146), channel_id=1, source_target_pairs={{0,6},{1,7},{2,4},{3,5},{4,2},{5,3},{6,0},{7,1},{8,14},{9,15},{10,... | collective-permute-start | bytes 589832 | tf_op jit(solution)/shard_map/ppermute | solution.py:250
  80.1 13.1 %collective-permute-start.30 = (bf16[24,4096]{1,0:T(8,128)(2,1)S(1)}, bf16[24,4096]{1,0:T(8,128)(2,1)S(1)}, u32[]{:S(2)}, u32[]{:S(2)}) collective-permute-start(bf16[24,4096]{1,0:T(8,128)(2,1)S(1)} %get-tuple-element.147), channel_id=1, source_target_pairs={{0,7},{1,6},{2,5},{3,4},{4,3},{5,2},{6,1},{7,0},{8,15},{9,14},{10,... | collective-permute-start | bytes 589832 | tf_op jit(solution)/shard_map/ppermute | solution.py:250
  83.1 10.8 %collective-permute-start.39 = (bf16[24,4096]{1,0:T(8,128)(2,1)S(1)}, bf16[24,4096]{1,0:T(8,128)(2,1)S(1)}, u32[]{:S(2)}, u32[]{:S(2)}) collective-permute-start(bf16[24,4096]{1,0:T(8,128)(2,1)S(1)} %get-tuple-element.157), channel_id=1, source_target_pairs={{0,1},{1,0},{2,3},{3,2},{4,5},{5,4},{6,7},{7,6},{8,9},{9,8},{10,11... | collective-permute-start | bytes 589832 | tf_op jit(solution)/shard_map/ppermute | solution.py:250
  91.7 7.8 %collective-permute-start.40 = (bf16[24,4096]{1,0:T(8,128)(2,1)S(1)}, bf16[24,4096]{1,0:T(8,128)(2,1)S(1)}, u32[]{:S(2)}, u32[]{:S(2)}) collective-permute-start(bf16[24,4096]{1,0:T(8,128)(2,1)S(1)} %get-tuple-element.158), channel_id=1, source_target_pairs={{0,2},{1,3},{2,0},{3,1},{4,6},{5,7},{6,4},{7,5},{8,10},{9,11},{10,... | collective-permute-start | bytes 589832 | tf_op jit(solution)/shard_map/ppermute | solution.py:250
  92.1 9.9 %collective-permute-start.41 = (bf16[24,4096]{1,0:T(8,128)(2,1)S(1)}, bf16[24,4096]{1,0:T(8,128)(2,1)S(1)}, u32[]{:S(2)}, u32[]{:S(2)}) collective-permute-start(bf16[24,4096]{1,0:T(8,128)(2,1)S(1)} %get-tuple-element.159), channel_id=1, source_target_pairs={{0,3},{1,2},{2,1},{3,0},{4,7},{5,6},{6,5},{7,4},{8,11},{9,10},{10,... | collective-permute-start | bytes 589832 | tf_op jit(solution)/shard_map/ppermute | solution.py:250
  93.2 23.7 %collective-permute-start.42 = (bf16[24,4096]{1,0:T(8,128)(2,1)S(1)}, bf16[24,4096]{1,0:T(8,128)(2,1)S(1)}, u32[]{:S(2)}, u32[]{:S(2)}) collective-permute-start(bf16[24,4096]{1,0:T(8,128)(2,1)S(1)} %get-tuple-element.160), channel_id=1, source_target_pairs={{0,4},{1,5},{2,6},{3,7},{4,0},{5,1},{6,2},{7,3},{8,12},{9,13},{10,... | collective-permute-start | bytes 589832 | tf_op jit(solution)/shard_map/ppermute | solution.py:250
  93.9 22.9 %collective-permute-start.43 = (bf16[24,4096]{1,0:T(8,128)(2,1)S(1)}, bf16[24,4096]{1,0:T(8,128)(2,1)S(1)}, u32[]{:S(2)}, u32[]{:S(2)}) collective-permute-start(bf16[24,4096]{1,0:T(8,128)(2,1)S(1)} %get-tuple-element.161), channel_id=1, source_target_pairs={{0,5},{1,4},{2,7},{3,6},{4,1},{5,0},{6,3},{7,2},{8,13},{9,12},{10,... | collective-permute-start | bytes 589832 | tf_op jit(solution)/shard_map/ppermute | solution.py:250
  99.4 18.2 %collective-permute-start.44 = (bf16[24,4096]{1,0:T(8,128)(2,1)S(1)}, bf16[24,4096]{1,0:T(8,128)(2,1)S(1)}, u32[]{:S(2)}, u32[]{:S(2)}) collective-permute-start(bf16[24,4096]{1,0:T(8,128)(2,1)S(1)} %get-tuple-element.162), channel_id=1, source_target_pairs={{0,6},{1,7},{2,4},{3,5},{4,2},{5,3},{6,0},{7,1},{8,14},{9,15},{10,... | collective-permute-start | bytes 589832 | tf_op jit(solution)/shard_map/ppermute | solution.py:250
  102.0 16.7 %collective-permute-start.45 = (bf16[24,4096]{1,0:T(8,128)(2,1)S(1)}, bf16[24,4096]{1,0:T(8,128)(2,1)S(1)}, u32[]{:S(2)}, u32[]{:S(2)}) collective-permute-start(bf16[24,4096]{1,0:T(8,128)(2,1)S(1)} %get-tuple-element.163), channel_id=1, source_target_pairs={{0,7},{1,6},{2,5},{3,4},{4,3},{5,2},{6,1},{7,0},{8,15},{9,14},{10,... | collective-permute-start | bytes 589832 | tf_op jit(solution)/shard_map/ppermute | solution.py:250
  116.8 14.7 %collective-permute-start.31 = (bf16[24,4096]{1,0:T(8,128)(2,1)S(1)}, bf16[24,4096]{1,0:T(8,128)(2,1)S(1)}, u32[]{:S(2)}, u32[]{:S(2)}) collective-permute-start(bf16[24,4096]{1,0:T(8,128)(2,1)S(1)} %get-tuple-element.149), channel_id=1, source_target_pairs={{0,1},{1,0},{2,3},{3,2},{4,5},{5,4},{6,7},{7,6},{8,9},{9,8},{10,11... | collective-permute-start | bytes 589832 | tf_op jit(solution)/shard_map/ppermute | solution.py:250
  116.8 16.8 %collective-permute-start.32 = (bf16[24,4096]{1,0:T(8,128)(2,1)S(1)}, bf16[24,4096]{1,0:T(8,128)(2,1)S(1)}, u32[]{:S(2)}, u32[]{:S(2)}) collective-permute-start(bf16[24,4096]{1,0:T(8,128)(2,1)S(1)} %get-tuple-element.150), channel_id=1, source_target_pairs={{0,2},{1,3},{2,0},{3,1},{4,6},{5,7},{6,4},{7,5},{8,10},{9,11},{10,... | collective-permute-start | bytes 589832 | tf_op jit(solution)/shard_map/ppermute | solution.py:250
  117.7 16.6 %collective-permute-start.33 = (bf16[24,4096]{1,0:T(8,128)(2,1)S(1)}, bf16[24,4096]{1,0:T(8,128)(2,1)S(1)}, u32[]{:S(2)}, u32[]{:S(2)}) collective-permute-start(bf16[24,4096]{1,0:T(8,128)(2,1)S(1)} %get-tuple-element.151), channel_id=1, source_target_pairs={{0,3},{1,2},{2,1},{3,0},{4,7},{5,6},{6,5},{7,4},{8,11},{9,10},{10,... | collective-permute-start | bytes 589832 | tf_op jit(solution)/shard_map/ppermute | solution.py:250
  118.7 15.9 %collective-permute-start.34 = (bf16[24,4096]{1,0:T(8,128)(2,1)S(1)}, bf16[24,4096]{1,0:T(8,128)(2,1)S(1)}, u32[]{:S(2)}, u32[]{:S(2)}) collective-permute-start(bf16[24,4096]{1,0:T(8,128)(2,1)S(1)} %get-tuple-element.152), channel_id=1, source_target_pairs={{0,4},{1,5},{2,6},{3,7},{4,0},{5,1},{6,2},{7,3},{8,12},{9,13},{10,... | collective-permute-start | bytes 589832 | tf_op jit(solution)/shard_map/ppermute | solution.py:250
  119.7 15.1 %collective-permute-start.35 = (bf16[24,4096]{1,0:T(8,128)(2,1)S(1)}, bf16[24,4096]{1,0:T(8,128)(2,1)S(1)}, u32[]{:S(2)}, u32[]{:S(2)}) collective-permute-start(bf16[24,4096]{1,0:T(8,128)(2,1)S(1)} %get-tuple-element.153), channel_id=1, source_target_pairs={{0,5},{1,4},{2,7},{3,6},{4,1},{5,0},{6,3},{7,2},{8,13},{9,12},{10,... | collective-permute-start | bytes 589832 | tf_op jit(solution)/shard_map/ppermute | solution.py:250
  131.5 8.7 %collective-permute-start.36 = (bf16[24,4096]{1,0:T(8,128)(2,1)S(1)}, bf16[24,4096]{1,0:T(8,128)(2,1)S(1)}, u32[]{:S(2)}, u32[]{:S(2)}) collective-permute-start(bf16[24,4096]{1,0:T(8,128)(2,1)S(1)} %get-tuple-element.154), channel_id=1, source_target_pairs={{0,6},{1,7},{2,4},{3,5},{4,2},{5,3},{6,0},{7,1},{8,14},{9,15},{10,... | collective-permute-start | bytes 589832 | tf_op jit(solution)/shard_map/ppermute | solution.py:250
  133.6 9.9 %collective-permute-start.37 = (bf16[24,4096]{1,0:T(8,128)(2,1)S(1)}, bf16[24,4096]{1,0:T(8,128)(2,1)S(1)}, u32[]{:S(2)}, u32[]{:S(2)}) collective-permute-start(bf16[24,4096]{1,0:T(8,128)(2,1)S(1)} %get-tuple-element.155), channel_id=1, source_target_pairs={{0,7},{1,6},{2,5},{3,4},{4,3},{5,2},{6,1},{7,0},{8,15},{9,14},{10,... | collective-permute-start | bytes 589832 | tf_op jit(solution)/shard_map/ppermute | solution.py:250
  134.3 10.2 %collective-permute-start.46 = (bf16[24,4096]{1,0:T(8,128)(2,1)S(1)}, bf16[24,4096]{1,0:T(8,128)(2,1)S(1)}, u32[]{:S(2)}, u32[]{:S(2)}) collective-permute-start(bf16[24,4096]{1,0:T(8,128)(2,1)S(1)} %get-tuple-element.165), channel_id=1, source_target_pairs={{0,1},{1,0},{2,3},{3,2},{4,5},{5,4},{6,7},{7,6},{8,9},{9,8},{10,11... | collective-permute-start | bytes 589832 | tf_op jit(solution)/shard_map/ppermute | solution.py:250
  134.6 10.9 %collective-permute-start.10 = (bf16[24,4096]{1,0:T(8,128)(2,1)S(1)}, bf16[24,4096]{1,0:T(8,128)(2,1)S(1)}, u32[]{:S(2)}, u32[]{:S(2)}) collective-permute-start(bf16[24,4096]{1,0:T(8,128)(2,1)S(1)} %get-tuple-element.117), channel_id=1, source_target_pairs={{0,1},{1,0},{2,3},{3,2},{4,5},{5,4},{6,7},{7,6},{8,9},{9,8},{10,11... | collective-permute-start | bytes 589832 | tf_op jit(solution)/shard_map/ppermute | solution.py:250
  134.8 13.4 %collective-permute-start.11 = (bf16[24,4096]{1,0:T(8,128)(2,1)S(1)}, bf16[24,4096]{1,0:T(8,128)(2,1)S(1)}, u32[]{:S(2)}, u32[]{:S(2)}) collective-permute-start(bf16[24,4096]{1,0:T(8,128)(2,1)S(1)} %get-tuple-element.118), channel_id=1, source_target_pairs={{0,2},{1,3},{2,0},{3,1},{4,6},{5,7},{6,4},{7,5},{8,10},{9,11},{10,... | collective-permute-start | bytes 589832 | tf_op jit(solution)/shard_map/ppermute | solution.py:250
  140.2 11.3 %collective-permute-start.12 = (bf16[24,4096]{1,0:T(8,128)(2,1)S(1)}, bf16[24,4096]{1,0:T(8,128)(2,1)S(1)}, u32[]{:S(2)}, u32[]{:S(2)}) collective-permute-start(bf16[24,4096]{1,0:T(8,128)(2,1)S(1)} %get-tuple-element.119), channel_id=1, source_target_pairs={{0,3},{1,2},{2,1},{3,0},{4,7},{5,6},{6,5},{7,4},{8,11},{9,10},{10,... | collective-permute-start | bytes 589832 | tf_op jit(solution)/shard_map/ppermute | solution.py:250
  143.5 9.5 %collective-permute-start.13 = (bf16[24,4096]{1,0:T(8,128)(2,1)S(1)}, bf16[24,4096]{1,0:T(8,128)(2,1)S(1)}, u32[]{:S(2)}, u32[]{:S(2)}) collective-permute-start(bf16[24,4096]{1,0:T(8,128)(2,1)S(1)} %get-tuple-element.120), channel_id=1, source_target_pairs={{0,4},{1,5},{2,6},{3,7},{4,0},{5,1},{6,2},{7,3},{8,12},{9,13},{10,... | collective-permute-start | bytes 589832 | tf_op jit(solution)/shard_map/ppermute | solution.py:250
  144.5 18.9 %collective-permute-start.14 = (bf16[24,4096]{1,0:T(8,128)(2,1)S(1)}, bf16[24,4096]{1,0:T(8,128)(2,1)S(1)}, u32[]{:S(2)}, u32[]{:S(2)}) collective-permute-start(bf16[24,4096]{1,0:T(8,128)(2,1)S(1)} %get-tuple-element.121), channel_id=1, source_target_pairs={{0,5},{1,4},{2,7},{3,6},{4,1},{5,0},{6,3},{7,2},{8,13},{9,12},{10,... | collective-permute-start | bytes 589832 | tf_op jit(solution)/shard_map/ppermute | solution.py:250
  145.6 18.9 %collective-permute-start.15 = (bf16[24,4096]{1,0:T(8,128)(2,1)S(1)}, bf16[24,4096]{1,0:T(8,128)(2,1)S(1)}, u32[]{:S(2)}, u32[]{:S(2)}) collective-permute-start(bf16[24,4096]{1,0:T(8,128)(2,1)S(1)} %get-tuple-element.122), channel_id=1, source_target_pairs={{0,6},{1,7},{2,4},{3,5},{4,2},{5,3},{6,0},{7,1},{8,14},{9,15},{10,... | collective-permute-start | bytes 589832 | tf_op jit(solution)/shard_map/ppermute | solution.py:250
  148.2 17.0 %collective-permute-start.16 = (bf16[24,4096]{1,0:T(8,128)(2,1)S(1)}, bf16[24,4096]{1,0:T(8,128)(2,1)S(1)}, u32[]{:S(2)}, u32[]{:S(2)}) collective-permute-start(bf16[24,4096]{1,0:T(8,128)(2,1)S(1)} %get-tuple-element.123), channel_id=1, source_target_pairs={{0,7},{1,6},{2,5},{3,4},{4,3},{5,2},{6,1},{7,0},{8,15},{9,14},{10,... | collective-permute-start | bytes 589832 | tf_op jit(solution)/shard_map/ppermute | solution.py:250
  151.5 29.4 %collective-permute-start.47 = (bf16[24,4096]{1,0:T(8,128)(2,1)S(1)}, bf16[24,4096]{1,0:T(8,128)(2,1)S(1)}, u32[]{:S(2)}, u32[]{:S(2)}) collective-permute-start(bf16[24,4096]{1,0:T(8,128)(2,1)S(1)} %get-tuple-element.166), channel_id=1, source_target_pairs={{0,2},{1,3},{2,0},{3,1},{4,6},{5,7},{6,4},{7,5},{8,10},{9,11},{10,... | collective-permute-start | bytes 589832 | tf_op jit(solution)/shard_map/ppermute | solution.py:250
  153.0 28.5 %collective-permute-start.48 = (bf16[24,4096]{1,0:T(8,128)(2,1)S(1)}, bf16[24,4096]{1,0:T(8,128)(2,1)S(1)}, u32[]{:S(2)}, u32[]{:S(2)}) collective-permute-start(bf16[24,4096]{1,0:T(8,128)(2,1)S(1)} %get-tuple-element.167), channel_id=1, source_target_pairs={{0,3},{1,2},{2,1},{3,0},{4,7},{5,6},{6,5},{7,4},{8,11},{9,10},{10,... | collective-permute-start | bytes 589832 | tf_op jit(solution)/shard_map/ppermute | solution.py:250
  163.4 18.5 %collective-permute-start.49 = (bf16[24,4096]{1,0:T(8,128)(2,1)S(1)}, bf16[24,4096]{1,0:T(8,128)(2,1)S(1)}, u32[]{:S(2)}, u32[]{:S(2)}) collective-permute-start(bf16[24,4096]{1,0:T(8,128)(2,1)S(1)} %get-tuple-element.168), channel_id=1, source_target_pairs={{0,4},{1,5},{2,6},{3,7},{4,0},{5,1},{6,2},{7,3},{8,12},{9,13},{10,... | collective-permute-start | bytes 589832 | tf_op jit(solution)/shard_map/ppermute | solution.py:250
  164.4 18.4 %collective-permute-start.50 = (bf16[24,4096]{1,0:T(8,128)(2,1)S(1)}, bf16[24,4096]{1,0:T(8,128)(2,1)S(1)}, u32[]{:S(2)}, u32[]{:S(2)}) collective-permute-start(bf16[24,4096]{1,0:T(8,128)(2,1)S(1)} %get-tuple-element.169), channel_id=1, source_target_pairs={{0,5},{1,4},{2,7},{3,6},{4,1},{5,0},{6,3},{7,2},{8,13},{9,12},{10,... | collective-permute-start | bytes 589832 | tf_op jit(solution)/shard_map/ppermute | solution.py:250
  165.1 19.7 %collective-permute-start.51 = (bf16[24,4096]{1,0:T(8,128)(2,1)S(1)}, bf16[24,4096]{1,0:T(8,128)(2,1)S(1)}, u32[]{:S(2)}, u32[]{:S(2)}) collective-permute-start(bf16[24,4096]{1,0:T(8,128)(2,1)S(1)} %get-tuple-element.170), channel_id=1, source_target_pairs={{0,6},{1,7},{2,4},{3,5},{4,2},{5,3},{6,0},{7,1},{8,14},{9,15},{10,... | collective-permute-start | bytes 589832 | tf_op jit(solution)/shard_map/ppermute | solution.py:250
  180.9 8.1 %collective-permute-start.52 = (bf16[24,4096]{1,0:T(8,128)(2,1)}, bf16[24,4096]{1,0:T(8,128)(2,1)S(1)}, u32[]{:S(2)}, u32[]{:S(2)}) collective-permute-start(bf16[24,4096]{1,0:T(8,128)(2,1)} %get-tuple-element.171), channel_id=1, source_target_pairs={{0,7},{1,6},{2,5},{3,4},{4,3},{5,2},{6,1},{7,0},{8,15},{9,14},{10,... | collective-permute-start | bytes 589832 | tf_op jit(solution)/shard_map/ppermute | solution.py:250
  181.6 8.5 %collective-permute-start.54 = (bf16[24,4096]{1,0:T(8,128)(2,1)S(1)}, bf16[24,4096]{1,0:T(8,128)(2,1)S(1)}, u32[]{:S(2)}, u32[]{:S(2)}) collective-permute-start(bf16[24,4096]{1,0:T(8,128)(2,1)S(1)} %get-tuple-element.125), channel_id=1, source_target_pairs={{0,1},{1,0},{2,3},{3,2},{4,5},{5,4},{6,7},{7,6},{8,9},{9,8},{10,11... | collective-permute-start | bytes 589832 | tf_op jit(solution)/shard_map/ppermute | solution.py:250
  181.9 10.8 %collective-permute-start.55 = (bf16[24,4096]{1,0:T(8,128)(2,1)S(1)}, bf16[24,4096]{1,0:T(8,128)(2,1)S(1)}, u32[]{:S(2)}, u32[]{:S(2)}) collective-permute-start(bf16[24,4096]{1,0:T(8,128)(2,1)S(1)} %get-tuple-element.126), channel_id=1, source_target_pairs={{0,2},{1,3},{2,0},{3,1},{4,6},{5,7},{6,4},{7,5},{8,10},{9,11},{10,... | collective-permute-start | bytes 589832 | tf_op jit(solution)/shard_map/ppermute | solution.py:250
  182.8 13.3 %collective-permute-start.56 = (bf16[24,4096]{1,0:T(8,128)(2,1)S(1)}, bf16[24,4096]{1,0:T(8,128)(2,1)S(1)}, u32[]{:S(2)}, u32[]{:S(2)}) collective-permute-start(bf16[24,4096]{1,0:T(8,128)(2,1)S(1)} %get-tuple-element.127), channel_id=1, source_target_pairs={{0,3},{1,2},{2,1},{3,0},{4,7},{5,6},{6,5},{7,4},{8,11},{9,10},{10,... | collective-permute-start | bytes 589832 | tf_op jit(solution)/shard_map/ppermute | solution.py:250
  184.9 52.3 %collective-permute-start.38 = (bf16[128,4224]{1,0:T(8,128)(2,1)S(1)}, bf16[128,4224]{1,0:T(8,128)(2,1)S(1)}, u32[]{:S(2)}, u32[]{:S(2)}) collective-permute-start(bf16[128,4224]{1,0:T(8,128)(2,1)S(1)} %combine.3), channel_id=1, source_target_pairs={{0,24},{8,0},{16,8},{24,16},{1,25},{9,1},{17,9},{25,17},{2,26},{10... | collective-permute-start | bytes 3244040 | tf_op jit(solution)/shard_map/ppermute | solution.py:309
  189.0 9.2 %collective-permute-start.57 = (bf16[24,4096]{1,0:T(8,128)(2,1)S(1)}, bf16[24,4096]{1,0:T(8,128)(2,1)S(1)}, u32[]{:S(2)}, u32[]{:S(2)}) collective-permute-start(bf16[24,4096]{1,0:T(8,128)(2,1)S(1)} %get-tuple-element.128), channel_id=1, source_target_pairs={{0,4},{1,5},{2,6},{3,7},{4,0},{5,1},{6,2},{7,3},{8,12},{9,13},{10,... | collective-permute-start | bytes 589832 | tf_op jit(solution)/shard_map/ppermute | solution.py:250
  190.0 18.2 %collective-permute-start.58 = (bf16[24,4096]{1,0:T(8,128)(2,1)S(1)}, bf16[24,4096]{1,0:T(8,128)(2,1)S(1)}, u32[]{:S(2)}, u32[]{:S(2)}) collective-permute-start(bf16[24,4096]{1,0:T(8,128)(2,1)S(1)} %copy-done.17), channel_id=1, source_target_pairs={{0,5},{1,4},{2,7},{3,6},{4,1},{5,0},{6,3},{7,2},{8,13},{9,12},{10,... | collective-permute-start | bytes 589832 | tf_op jit(solution)/shard_map/ppermute | solution.py:250
  192.7 17.4 %collective-permute-start.59 = (bf16[24,4096]{1,0:T(8,128)(2,1)S(1)}, bf16[24,4096]{1,0:T(8,128)(2,1)S(1)}, u32[]{:S(2)}, u32[]{:S(2)}) collective-permute-start(bf16[24,4096]{1,0:T(8,128)(2,1)S(1)} %copy-done.15), channel_id=1, source_target_pairs={{0,6},{1,7},{2,4},{3,5},{4,2},{5,3},{6,0},{7,1},{8,14},{9,15},{10,... | collective-permute-start | bytes 589832 | tf_op jit(solution)/shard_map/ppermute | solution.py:250
  196.1 15.4 %collective-permute-start.60 = (bf16[24,4096]{1,0:T(8,128)(2,1)S(1)}, bf16[24,4096]{1,0:T(8,128)(2,1)S(1)}, u32[]{:S(2)}, u32[]{:S(2)}) collective-permute-start(bf16[24,4096]{1,0:T(8,128)(2,1)S(1)} %get-tuple-element.131), channel_id=1, source_target_pairs={{0,7},{1,6},{2,5},{3,4},{4,3},{5,2},{6,1},{7,0},{8,15},{9,14},{10,... | collective-permute-start | bytes 589832 | tf_op jit(solution)/shard_map/ppermute | solution.py:250
  198.1 23.8 %collective-permute-start.3 = (bf16[24,4096]{1,0:T(8,128)(2,1)S(1)}, bf16[24,4096]{1,0:T(8,128)(2,1)S(1)}, u32[]{:S(2)}, u32[]{:S(2)}) collective-permute-start(bf16[24,4096]{1,0:T(8,128)(2,1)S(1)} %copy-done.13), channel_id=1, source_target_pairs={{0,4},{1,5},{2,6},{3,7},{4,0},{5,1},{6,2},{7,3},{8,12},{9,13},{10,... | collective-permute-start | bytes 589832 | tf_op jit(solution)/shard_map/ppermute | solution.py:250
  208.2 16.8 %collective-permute-start.4 = (bf16[24,4096]{1,0:T(8,128)(2,1)S(1)}, bf16[24,4096]{1,0:T(8,128)(2,1)S(1)}, u32[]{:S(2)}, u32[]{:S(2)}) collective-permute-start(bf16[24,4096]{1,0:T(8,128)(2,1)S(1)} %copy-done.11), channel_id=1, source_target_pairs={{0,5},{1,4},{2,7},{3,6},{4,1},{5,0},{6,3},{7,2},{8,13},{9,12},{10,... | collective-permute-start | bytes 589832 | tf_op jit(solution)/shard_map/ppermute | solution.py:250
  210.1 16.1 %collective-permute-start.5 = (bf16[24,4096]{1,0:T(8,128)(2,1)S(1)}, bf16[24,4096]{1,0:T(8,128)(2,1)S(1)}, u32[]{:S(2)}, u32[]{:S(2)}) collective-permute-start(bf16[24,4096]{1,0:T(8,128)(2,1)S(1)} %copy-done.9), channel_id=1, source_target_pairs={{0,6},{1,7},{2,4},{3,5},{4,2},{5,3},{6,0},{7,1},{8,14},{9,15},{10,... | collective-permute-start | bytes 589832 | tf_op jit(solution)/shard_map/ppermute | solution.py:250
  211.6 14.6 %collective-permute-start.6 = (bf16[24,4096]{1,0:T(8,128)(2,1)S(1)}, bf16[24,4096]{1,0:T(8,128)(2,1)S(1)}, u32[]{:S(2)}, u32[]{:S(2)}) collective-permute-start(bf16[24,4096]{1,0:T(8,128)(2,1)S(1)} %copy-done.5), channel_id=1, source_target_pairs={{0,7},{1,6},{2,5},{3,4},{4,3},{5,2},{6,1},{7,0},{8,15},{9,14},{10,... | collective-permute-start | bytes 589832 | tf_op jit(solution)/shard_map/ppermute | solution.py:250
  222.0 67.0 %collective-permute-start.53 = (bf16[128,4224]{1,0:T(8,128)(2,1)S(1)}, bf16[128,4224]{1,0:T(8,128)(2,1)S(1)}, u32[]{:S(2)}, u32[]{:S(2)}) collective-permute-start(bf16[128,4224]{1,0:T(8,128)(2,1)S(1)} %combine.4), channel_id=1, source_target_pairs={{0,16},{8,24},{16,0},{24,8},{1,17},{9,25},{17,1},{25,9},{2,18},{10... | collective-permute-start | bytes 3244040 | tf_op jit(solution)/shard_map/ppermute | solution.py:309
  225.1 63.9 %collective-permute-start.61 = (bf16[128,4224]{1,0:T(8,128)(2,1)S(1)}, bf16[128,4224]{1,0:T(8,128)(2,1)}, u32[]{:S(2)}, u32[]{:S(2)}) collective-permute-start(bf16[128,4224]{1,0:T(8,128)(2,1)S(1)} %combine.5), channel_id=1, source_target_pairs={{0,8},{8,16},{16,24},{24,0},{1,9},{9,17},{17,25},{25,1},{2,10},{10... | collective-permute-start | bytes 3244040 | tf_op jit(solution)/shard_map/ppermute | solution.py:309
  236.6 1.9 collective-permute-start.17
  236.6 7.7 %collective-permute-start.18 = (bf16[24,4096]{1,0:T(8,128)(2,1)S(1)}, bf16[24,4096]{1,0:T(8,128)(2,1)S(1)}, u32[]{:S(2)}, u32[]{:S(2)}) collective-permute-start(bf16[24,4096]{1,0:T(8,128)(2,1)S(1)} %get-tuple-element.134), channel_id=1, source_target_pairs={{0,2},{1,3},{2,0},{3,1},{4,6},{5,7},{6,4},{7,5},{8,10},{9,11},{10,... | collective-permute-start | bytes 589832 | tf_op jit(solution)/shard_map/ppermute | solution.py:250
  237.1 10.7 %collective-permute-start.19 = (bf16[24,4096]{1,0:T(8,128)(2,1)S(1)}, bf16[24,4096]{1,0:T(8,128)(2,1)S(1)}, u32[]{:S(2)}, u32[]{:S(2)}) collective-permute-start(bf16[24,4096]{1,0:T(8,128)(2,1)S(1)} %get-tuple-element.135), channel_id=1, source_target_pairs={{0,3},{1,2},{2,1},{3,0},{4,7},{5,6},{6,5},{7,4},{8,11},{9,10},{10,... | collective-permute-start | bytes 589832 | tf_op jit(solution)/shard_map/ppermute | solution.py:250
  238.5 10.1 %collective-permute-start.20 = (bf16[24,4096]{1,0:T(8,128)(2,1)S(1)}, bf16[24,4096]{1,0:T(8,128)(2,1)S(1)}, u32[]{:S(2)}, u32[]{:S(2)}) collective-permute-start(bf16[24,4096]{1,0:T(8,128)(2,1)S(1)} %get-tuple-element.136), channel_id=1, source_target_pairs={{0,4},{1,5},{2,6},{3,7},{4,0},{5,1},{6,2},{7,3},{8,12},{9,13},{10,... | collective-permute-start | bytes 589832 | tf_op jit(solution)/shard_map/ppermute | solution.py:250
  244.3 20.1 %collective-permute-start.21 = (bf16[24,4096]{1,0:T(8,128)(2,1)S(1)}, bf16[24,4096]{1,0:T(8,128)(2,1)S(1)}, u32[]{:S(2)}, u32[]{:S(2)}) collective-permute-start(bf16[24,4096]{1,0:T(8,128)(2,1)S(1)} %get-tuple-element.137), channel_id=1, source_target_pairs={{0,5},{1,4},{2,7},{3,6},{4,1},{5,0},{6,3},{7,2},{8,13},{9,12},{10,... | collective-permute-start | bytes 589832 | tf_op jit(solution)/shard_map/ppermute | solution.py:250
  247.8 16.7 %collective-permute-start.22 = (bf16[24,4096]{1,0:T(8,128)(2,1)S(1)}, bf16[24,4096]{1,0:T(8,128)(2,1)S(1)}, u32[]{:S(2)}, u32[]{:S(2)}) collective-permute-start(bf16[24,4096]{1,0:T(8,128)(2,1)S(1)} %get-tuple-element.138), channel_id=1, source_target_pairs={{0,6},{1,7},{2,4},{3,5},{4,2},{5,3},{6,0},{7,1},{8,14},{9,15},{10,... | collective-permute-start | bytes 589832 | tf_op jit(solution)/shard_map/ppermute | solution.py:250
  248.6 15.9 %collective-permute-start.23 = (bf16[24,4096]{1,0:T(8,128)(2,1)S(1)}, bf16[24,4096]{1,0:T(8,128)(2,1)S(1)}, u32[]{:S(2)}, u32[]{:S(2)}) collective-permute-start(bf16[24,4096]{1,0:T(8,128)(2,1)S(1)} %get-tuple-element.139), channel_id=1, source_target_pairs={{0,7},{1,6},{2,5},{3,4},{4,3},{5,2},{6,1},{7,0},{8,15},{9,14},{10,... | collective-permute-start | bytes 589832 | tf_op jit(solution)/shard_map/ppermute | solution.py:250
  (35 other events, 555.5 us)

commit v2 on v1

v2 whole, which is shorter than its diff:
```python
import functools

import jax
import jax.numpy as jnp
from jax import lax
from jax.experimental import pallas as pl
from jax.experimental.pallas import tpu as pltpu
from jax.sharding import PartitionSpec as P

F32 = jnp.float32
BF16 = jnp.bfloat16
META = 128
VMEM_BYTES = 24 << 20


def split3(v):
    hi = lax.reduce_precision(v, 8, 7)
    mid = lax.reduce_precision(v - hi, 8, 7)
    return hi.astype(BF16), mid.astype(BF16), (v - hi - mid).astype(BF16)


def dot(a, b, ca=1, cb=0):
    return lax.dot_general(a, b, (((ca,), (cb,)), ((), ())), preferred_element_type=F32)


def selection(meta, tab, top):
    eid, place = tab[0:1, :], tab[1:2, :]
    tok = meta.shape[0]
    hits = [(meta[:, k : k + 1] == eid).astype(F32) for k in range(top)]
    hit = functools.reduce(lambda a, b: a + b, hits)
    gate = functools.reduce(
        lambda a, b: a + b,
        [
            hits[k]
            * (
                meta[:, top + k : top + k + 1]
                + meta[:, 2 * top + k : 2 * top + k + 1]
                + meta[:, 3 * top + k : 3 * top + k + 1]
            )
            for k in range(top)
        ],
    )
    row = lax.broadcasted_iota(jnp.int32, (tok, tok), 0)
    col = lax.broadcasted_iota(jnp.int32, (tok, tok), 1)
    earlier = (col < row).astype(F32).astype(BF16)
    rank = dot(earlier, hit.astype(BF16))
    sel = jnp.where(rank == place, hit, 0.0)
    return sel, gate, hits


def dispatch_kernel(top, width, tab_ref, buf_ref, out_ref):
    count, rows_p = out_ref.shape[:2]
    sel, gate, _ = selection(buf_ref[:, 2 * width :].astype(F32), tab_ref[...], top)
    gate_t = jnp.sum((sel * gate).T, axis=1, keepdims=True)
    pick = sel.T.astype(BF16)
    step = 512
    for c in range(0, width, step):
        x = dot(pick, buf_ref[:, c : c + step])
        z = gate_t * dot(pick, buf_ref[:, width + c : width + c + step])
        for s in range(count):
            of = slice(s * rows_p, (s + 1) * rows_p)
            out_ref[s, :, c : c + step] = x[of].astype(BF16)
            out_ref[s, :, width + c : width + c + step] = z[of].astype(BF16)


def gather_rows(pieces, lo, hi, rows=slice(None)):
    return jnp.concatenate([p[rows, lo:hi].astype(F32) for p in pieces], axis=0).astype(
        BF16
    )


def expert_kernel(chips, width, me_ref, rows_ref, *refs):
    wg_ref, wu_ref, wd_ref = refs[:3]
    rets = refs[3 : 3 + chips]
    xz_ref, hid_ref, dpg_ref, dpu_ref, acc_o, acc_d = refs[3 + chips :]
    count, rows_p = rows_ref.shape[:2]
    f = pl.program_id(0)

    @pl.when(f == 0)
    def _():
        pieces = [rows_ref.at[s] for s in range(count)]
        for c in range(0, 2 * width, 512):
            xz_ref[:, c : c + 512] = gather_rows(pieces, c, c + 512)

    wg, wu, wd = wg_ref[0], wu_ref[0], wd_ref[0]
    x = xz_ref[:, :width]
    pre_gate = dot(x, wg)
    pre_up = dot(x, wu)
    d_hidden = dot(xz_ref[:, width:], wd, 1, 1)
    sig = jax.nn.sigmoid(pre_gate)
    silu = pre_gate * sig
    hidden = (silu * pre_up).astype(BF16)
    d_pre_gate = (d_hidden * pre_up * sig * (1.0 + pre_gate * (1.0 - sig))).astype(BF16)
    d_pre_up = (d_hidden * silu).astype(BF16)
    hid_ref[...] = hidden
    dpg_ref[...] = d_pre_gate
    dpu_ref[...] = d_pre_up
    out = dot(hidden, wd)
    d_x = dot(d_pre_gate, wg, 1, 1) + dot(d_pre_up, wu, 1, 1)

    @pl.when(f == 0)
    def _():
        acc_o[...] = out
        acc_d[...] = d_x

    @pl.when(f > 0)
    def _():
        acc_o[...] += out
        acc_d[...] += d_x

    @pl.when(f == pl.num_programs(0) - 1)
    def _():
        me = me_ref[0]
        for s, ret in enumerate(rets):
            for b in range(2):
                source = jnp.bitwise_xor(me, 2 * s + b)
                at = pl.ds(pl.multiple_of(source * rows_p, 8), rows_p)
                to = slice(b * rows_p, (b + 1) * rows_p)
                ret[to, :width] = acc_o[at, :].astype(BF16)
                ret[to, width:] = acc_d[at, :].astype(BF16)


def combine_kernel(count, top, width, tab_ref, own_ref, pair_ref, *refs):
    pieces, parts = refs[:count], refs[count:]
    rows_p = pieces[0].shape[0] // 2
    step = 512
    for b, buf_ref in enumerate((own_ref, pair_ref)):
        rows = slice(b * rows_p, (b + 1) * rows_p)
        sel, gate, hits = selection(
            buf_ref[:, 2 * width :].astype(F32), tab_ref[...], top
        )
        plain = sel.astype(BF16)
        gated = split3(sel * gate)
        prod = None
        for c in range(0, width, step):
            out_rows = gather_rows(pieces, c, c + step, rows)
            dx_rows = gather_rows(pieces, width + c, width + c + step, rows)
            mixed = dot(gated[0], out_rows) + dot(gated[1], out_rows)
            mixed = mixed + dot(gated[2], out_rows)
            part = dot(buf_ref[:, width + c : width + c + step], out_rows, 1, 1)
            prod = part if prod is None else prod + part
            parts[b][:, c : c + step] = mixed.astype(BF16)
            parts[b][:, width + c : width + c + step] = dot(plain, dx_rows).astype(BF16)
        prod = prod * sel
        lane = lax.broadcasted_iota(jnp.int32, (buf_ref.shape[0], META), 1)
        packed = jnp.zeros((buf_ref.shape[0], META), F32)
        for k, h in enumerate(hits):
            column = jnp.sum(prod * h, axis=1, keepdims=True)
            for i, piece in enumerate(split3(column)):
                packed = jnp.where(lane == i * top + k, piece.astype(F32), packed)
        parts[b][:, 2 * width :] = packed.astype(BF16)


def join_kernel(*refs):
    total = functools.reduce(lambda a, b: a + b, [r[...].astype(F32) for r in refs[:-1]])
    refs[-1][...] = total.astype(BF16)


def after(values, *deps):
    flat = [d for dep in deps for d in dep]
    return list(lax.optimization_barrier((*values, *flat))[: len(values)])


def final_kernel(count, top, width, *refs):
    parts = refs[:count]
    mixed_ref, d_tok_ref, d_gates_ref = refs[count:]

    def total(lo, hi):
        return functools.reduce(
            lambda a, b: a + b, [p[:, lo:hi].astype(F32) for p in parts]
        )

    mixed_ref[...] = total(0, width).astype(BF16)
    d_tok_ref[...] = total(width, 2 * width).astype(BF16)
    packed = total(2 * width, 2 * width + META)
    for k in range(top):
        d_gates_ref[:, k : k + 1] = (
            packed[:, k : k + 1]
            + packed[:, top + k : top + k + 1]
            + packed[:, 2 * top + k : 2 * top + k + 1]
        )


def weight_grad_kernel(stages, *refs):
    xs, zs = refs[:stages], refs[stages : 2 * stages]
    hids, dpgs, dpus = (refs[i * stages : (i + 1) * stages] for i in (2, 3, 4))
    gate_ref, up_ref, down_ref = refs[5 * stages :]

    def total(lefts, rights):
        acc = None
        for a, b in zip(lefts, rights):
            t = dot(a[...], b[...], 0, 0)
            acc = t if acc is None else acc + t
        return acc.astype(BF16)

    gate_ref[0] = total(xs, dpgs)
    up_ref[0] = total(xs, dpus)
    down_ref[0] = total(hids, zs)


def whole(shape):
    return pl.BlockSpec(shape, lambda *_: (0,) * len(shape))


def params():
    return pltpu.CompilerParams(vmem_limit_bytes=VMEM_BYTES)


def local(tokens, cotangent, expert_ids, gates, w_gate, w_up, w_down):
    groups = lax.axis_size("group")
    count = lax.axis_size("local")
    chips = count // 2
    tok, width = tokens.shape
    top = expert_ids.shape[1]
    hidden_width = w_gate.shape[2]
    capacity = max(2, 3 * tok * top // (2 * groups * count))
    rows_p = -(-capacity // 8) * 8
    slots = count * rows_p
    me = lax.axis_index("local")
    plane = lax.axis_index("group")

    def table(experts):
        slot = jnp.arange(experts.shape[0] * rows_p, dtype=jnp.int32) % rows_p
        rows = [
            jnp.repeat(plane * count + experts, rows_p).astype(F32)[None],
            jnp.where(slot < capacity, slot, -1).astype(F32)[None],
            jnp.zeros((6, slot.shape[0]), F32),
        ]
        return jnp.concatenate(rows, 0)

    tab_in = table(jnp.arange(count, dtype=jnp.int32))
    tab_back = table(jnp.bitwise_xor(2 * jnp.arange(chips, dtype=jnp.int32), me))
    meta = jnp.concatenate(
        [expert_ids.astype(BF16), *split3(gates), jnp.zeros((tok, META - 4 * top), BF16)], 1
    )
    buf0 = jnp.concatenate([tokens, cotangent, meta], axis=1)
    wide = 2 * width + META
    row = jax.ShapeDtypeStruct((tok, wide), BF16)

    piece = jax.ShapeDtypeStruct((2 * rows_p, 2 * width), BF16)
    tile = 256
    steps = hidden_width // tile

    def dispatch(buf):
        return pl.pallas_call(
            functools.partial(dispatch_kernel, top, width),
            out_shape=jax.ShapeDtypeStruct((count, rows_p, 2 * width), BF16),
            compiler_params=params(),
            cost_estimate=pl.CostEstimate(
                flops=4 * slots * tok * width * 30,
                bytes_accessed=2 * (tok * wide + 2 * slots * width) * 30,
                transcendentals=0,
            ),
            name="dispatch",
        )(tab_in, buf)

    def other_core(v):
        return lax.ppermute(v, "local", [(i, i ^ 1) for i in range(count)])

    def swap(pieces):
        return [pieces[0]] + [
            lax.ppermute(pieces[s], "local", [(i, i ^ (2 * s)) for i in range(count)])
            for s in range(1, chips)
        ]

    def expert(rows):
        mid = jax.ShapeDtypeStruct((slots, hidden_width), BF16)
        got = pl.pallas_call(
            functools.partial(expert_kernel, chips, width),
            grid=(steps,),
            in_specs=[pl.BlockSpec(memory_space=pltpu.SMEM)]
            + [whole((count, rows_p, 2 * width))]
            + [pl.BlockSpec((1, width, tile), lambda f: (0, 0, f))] * 2
            + [pl.BlockSpec((1, tile, width), lambda f: (0, f, 0))],
            out_specs=[whole((2 * rows_p, 2 * width))] * chips
            + [whole((slots, 2 * width))]
            + [pl.BlockSpec((slots, tile), lambda f: (0, f))] * 3,
            out_shape=[piece] * chips
            + [jax.ShapeDtypeStruct((slots, 2 * width), BF16)]
            + [mid] * 3,
            scratch_shapes=[pltpu.VMEM((slots, width), F32)] * 2,
            compiler_params=params(),
            cost_estimate=pl.CostEstimate(
                flops=12 * slots * width * hidden_width,
                bytes_accessed=2 * (3 * width * hidden_width + 8 * slots * width),
                transcendentals=slots * hidden_width,
            ),
            name="expert",
        )(me.reshape(1), rows, w_gate, w_up, w_down)
        return got[:chips], got[chips:]

    def combine(buf, pair, pieces):
        return pl.pallas_call(
            functools.partial(combine_kernel, chips, top, width),
            out_shape=[row, row],
            compiler_params=params(),
            cost_estimate=pl.CostEstimate(
                flops=10 * slots * tok * width * 100,
                bytes_accessed=2 * (4 * tok * wide + 2 * slots * width) * 100,
                transcendentals=0,
            ),
            name="combine",
        )(tab_back, buf, pair, *pieces)

    def join(*parts):
        return pl.pallas_call(
            join_kernel,
            out_shape=row,
            compiler_params=params(),
            cost_estimate=pl.CostEstimate(
                flops=len(parts) * tok * wide,
                bytes_accessed=2 * (1 + len(parts)) * tok * wide,
                transcendentals=0,
            ),
            name="join",
        )(*parts)

    def next_plane(v):
        return lax.ppermute(v, "group", [(i, (i + 1) % groups) for i in range(groups)])

    bufs, pairs, sent, came, kept, rets, outs = [], [], [], [], [], [], {}
    arriving = [buf0]

    def send(k, *deps, before_dispatch=()):
        bufs.append(after(arriving[-1:], *deps)[0])
        if k + 1 < groups:
            arriving.append(next_plane(bufs[k]))
        sent.append(dispatch(*after(bufs[k:], before_dispatch)))
        pairs.append(other_core(*after(bufs[k:], sent[k:])))
        came.append(
            lax.all_to_all(sent[k], "local", split_axis=0, concat_axis=0, tiled=True)
        )

    def compute(k, *deps):
        ret, saved = expert(*after(came[k : k + 1], pairs[k : k + 1], *deps))
        rets.append(ret)
        kept.append(saved)

    def give_back(k, *deps):
        outs[k] = swap(after(rets[k], *deps))

    def plane_sums(k, *deps):
        mine, theirs = combine(bufs[k], pairs[k], after(outs[k], *deps))
        return [mine, other_core(theirs)]

    last = groups - 1
    send(0)
    send(1, sent)
    compute(0, sent[1:])
    send(2, rets[0])
    compute(1, sent[2:])
    give_back(1)
    sums = []
    for k in range(3, groups):
        send(k, rets[k - 2])
        shares = plane_sums(k - 2, sent[k:])
        compute(k - 1, shares[:1])
        joined = join(*shares, *sums)
        sums = [next_plane(joined)]
        give_back(k - 1)
    compute(last, [joined])
    give_back(last)
    joined = join(*plane_sums(last - 1, rets[last]), *sums)
    sums = [next_plane(joined)]
    shares = plane_sums(last, [joined])
    kept = [after(saved, shares[:1]) for saved in kept]
    give_back(0, outs[last], [joined])
    home = [next_plane(join(*shares, *sums))]
    home += plane_sums(0)
    mixed, d_tokens, d_gates = pl.pallas_call(
        functools.partial(final_kernel, len(home), top, width),
        out_shape=[
            jax.ShapeDtypeStruct((tok, width), BF16),
            jax.ShapeDtypeStruct((tok, width), BF16),
            jax.ShapeDtypeStruct((tok, top), F32),
        ],
        compiler_params=params(),
        cost_estimate=pl.CostEstimate(
            flops=len(home) * tok * wide,
            bytes_accessed=2 * (1 + len(home)) * tok * wide,
            transcendentals=0,
        ),
        name="final",
    )(*home)

    d_tile = 256
    d_steps = width // d_tile
    full = [whole((slots, hidden_width))] * groups
    d_w_gate, d_w_up, d_w_down = pl.pallas_call(
        functools.partial(weight_grad_kernel, groups),
        grid=(d_steps,),
        in_specs=[pl.BlockSpec((slots, d_tile), lambda d: (0, d))] * groups
        + [pl.BlockSpec((slots, d_tile), lambda d: (0, d_steps + d))] * groups
        + full * 3,
        out_specs=[pl.BlockSpec((1, d_tile, hidden_width), lambda d: (0, d, 0))] * 2
        + [pl.BlockSpec((1, hidden_width, d_tile), lambda d: (0, 0, d))],
        out_shape=[
            jax.ShapeDtypeStruct((1, width, hidden_width), BF16),
            jax.ShapeDtypeStruct((1, width, hidden_width), BF16),
            jax.ShapeDtypeStruct((1, hidden_width, width), BF16),
        ],
        compiler_params=params(),
        cost_estimate=pl.CostEstimate(
            flops=6 * groups * slots * width * hidden_width,
            bytes_accessed=2 * (3 * width * hidden_width + 2 * groups * slots * width),
            transcendentals=0,
        ),
        name="weight_grads",
    )(
        *[s[0] for s in kept],
        *[s[0] for s in kept],
        *[s[1] for s in kept],
        *[s[2] for s in kept],
        *[s[3] for s in kept],
    )
    return mixed, d_tokens, d_gates, d_w_gate, d_w_up, d_w_down


def solution(mesh):
    rows = P(("group", "local"), None)
    cube = P(("group", "local"), None, None)
    return jax.shard_map(
        local,
        mesh=mesh,
        in_specs=(rows, rows, rows, rows, cube, cube, cube),
        out_specs=(rows, rows, rows, cube, cube, cube),
        check_vma=False,
    )
```

time: 295 us -> 232 us (0.79)
  waiting for transfers between devices: 152 us -> 76 us
  local copies, waits for them, and re-layouts: 12.4 us -> 37.5 us
  starting transfers between devices: 61.3 us -> 38.5 us
  Pallas kernels: 66.2 us -> 75.5 us
    ppermute x62 -> x26, waiting for transfers between devices: 152 us -> 76 us  [the longest x12 40.8 us: swap(): lax.ppermute(pieces[s], 'local', [(i, i ^ 2 * s) for i in range(count)])]
    ppermute x62 -> x26, starting transfers between devices: 61.3 us -> 23.5 us  [the longest x12 14.1 us: swap(): lax.ppermute(pieces[s], 'local', [(i, i ^ 2 * s) for i in range(count)])]
    unnamed x75 -> x116, local copies, waits for them, and re-layouts: 9.48 us -> 33.6 us
    all_to_all x0 -> x4, starting transfers between devices: none -> 15.1 us  [send(): lax.all_to_all(sent[k], 'local', split_axis=0, concat_axis=0, tiled=True)]
    pallas_call x4, Pallas kernels: 3.48 us -> 10.8 us  [dispatch(): pl.pallas_call(functools.partial(dispatch_kernel, top, width), out_shape=...]
    pallas_call x8 -> x12, Pallas kernels: 48.9 us -> 51.1 us  [the longest x4 31 us: expert(): pl.pallas_call(functools.partial(expert_kernel, chips, width), grid=(step...]
  transfers between devices with their start and end apart: 62 -> 30, of which waited for: 21 -> 14; matrix products, arithmetic and copies ran while one was open for 0% -> 1% of each run, Pallas kernels for 21% -> 32%
where the time goes in v2:
time: 232 us; the launch traced here: 231 us
  waiting for transfers between devices  76 us (33%)
  Pallas kernels  75.5 us (33%)
  starting transfers between devices  38.5 us (17%)
  local copies, waits for them, and re-layouts  37.5 us (16%)
    ppermute x12, waiting for transfers between devices, swap(): lax.ppermute(pieces[s], 'local', [(i, i ^ 2 * s) for i in range(count)])  40.8 us
    ppermute x6, waiting for transfers between devices, next_plane(): lax.ppermute(v, 'group', [(i, (i + 1) % groups) for i in range(groups)])  35.2 us
    unnamed x116, local copies, waits for them, and re-layouts  33.6 us
    pallas_call x4, Pallas kernels, expert(): pl.pallas_call(functools.partial(expert_kernel, chips, width), grid=(step...  31 us
    pallas_call x4, Pallas kernels, combine(): pl.pallas_call(functools.partial(combine_kernel, chips, top, width), out_...  16 us
    all_to_all x4, starting transfers between devices, send(): lax.all_to_all(sent[k], 'local', split_axis=0, concat_axis=0, tiled=True)  15.1 us
    ppermute x12, starting transfers between devices, swap(): lax.ppermute(pieces[s], 'local', [(i, i ^ 2 * s) for i in range(count)])  14.1 us
    pallas_call x1, Pallas kernels, local(): pl.pallas_call(functools.partial(weight_grad_kernel, groups), grid=(d_ste...  13.7 us
  transfers between devices with their start and end apart: 30, of which 14 were waited for; matrix products, arithmetic and copies ran while one was open for 1% of the time, Pallas kernels for 32%

profile of v2, /device:TPU:0, one launch (start us, length us, event | category | flops | bytes accessed | tf_op | source)
XLA Modules:
  0.0 230.9 jit_solution(9526580027277583077)
XLA Ops:
  1.3 0.8 copy.17
  3.2 3.1 %concatenate.10.buf_ref.own_ref = bf16[128,4224]{1,0:T(8,128)(2,1)} concatenate(bf16[128,2048]{1,0:T(8,128)(2,1)} %param.7, bf16[128,2048]{1,0:T(8,128)(2,1)} %param.8, bf16[128,4]{1,0:T(8,128)(2,1)S(1)} %copy.19, bf16[128,4]{1,0:T(8,128)(2,1)S(1)} %copy.20, bf16[128,4]{1,0:T(8,128)(2,1)S(1)} %get-tuple-element.229, bf16[128,4]{1,0:T(8,128)(2,1)S(1)} %get-tuple-element.228, ...), dimensions={1} | concatenate | bytes 2162688 | tf_op jit(solution)/shard_map/concatenate | solution.py:236
  6.3 3.0 %collective-permute-start = (bf16[128,4224]{1,0:T(8,128)(2,1)}, bf16[128,4224]{1,0:T(8,128)(2,1)}, u32[]{:S(2)}, u32[]{:S(2)}) collective-permute-start(bf16[128,4224]{1,0:T(8,128)(2,1)} %concatenate.10.buf_ref.own_ref), channel_id=1, source_target_pairs={{0,8},{8,16},{16,24},{24,0},{1,9},{9,17},{17,25},{25,1},{2,10},{10... | collective-permute-start | bytes 3244040 | tf_op jit(solution)/shard_map/ppermute | solution.py:319
  9.6 3.3 %dispatch.4 = bf16[8,24,4096]{2,1,0:T(8,128)(2,1)} custom-call(f32[8,192]{1,0:T(8,128)S(1)} %maximum_maximum_fusion.tab_ref, bf16[128,4224]{1,0:T(8,128)(2,1)} %concatenate.10.buf_ref.own_ref), custom_call_target="tpu_custom_call" | custom-call | flops 6039797760 | bytes 79626240 | tf_op jit(solution)/shard_map/dispatch/pallas_call | solution.py:245
  12.9 3.7 %all-to-all-start = ((bf16[8,24,4096]{2,1,0:T(8,128)(2,1)}), bf16[8,24,4096]{2,1,0:T(8,128)(2,1)S(1)}, u32[]{:S(2)}, u32[]{:S(2)}) async-start(bf16[8,24,4096]{2,1,0:T(8,128)(2,1)} %dispatch.4), calls=%async_computation | async-start | bytes 3145728 | tf_op jit(solution)/shard_map/all_to_all | solution.py:331
  17.1 18.4 %collective-permute-done.buf_ref.own_ref = bf16[128,4224]{1,0:T(8,128)(2,1)} collective-permute-done((bf16[128,4224]{1,0:T(8,128)(2,1)}, bf16[128,4224]{1,0:T(8,128)(2,1)}, u32[]{:S(2)}, u32[]{:S(2)}) %collective-permute-start) | collective-permute-done | bytes 1081376 | tf_op jit(solution)/shard_map/ppermute | solution.py:319
  35.5 2.1 dispatch.5
  37.7 1.1 copy-done.1
  38.8 3.7 %all-to-all-start.1 = ((bf16[8,24,4096]{2,1,0:T(8,128)(2,1)}), bf16[8,24,4096]{2,1,0:T(8,128)(2,1)S(1)}, u32[]{:S(2)}, u32[]{:S(2)}) async-start(bf16[8,24,4096]{2,1,0:T(8,128)(2,1)} %copy-done.1), calls=%async_computation.1 | async-start | bytes 3145728 | tf_op jit(solution)/shard_map/all_to_all | solution.py:331
  43.0 1.9 copy-done.2
  44.9 1.9 copy-done.6
  46.8 1.9 copy-done.10
  48.7 7.5 %expert.4 = (bf16[48,4096]{1,0:T(8,128)(2,1)S(1)}, bf16[48,4096]{1,0:T(8,128)(2,1)S(1)}, bf16[48,4096]{1,0:T(8,128)(2,1)S(1)}, bf16[48,4096]{1,0:T(8,128)(2,1)S(...) custom-call(s32[1]{0:T(128)} %bitcast.me_ref, ...), custom_call_target="tpu_custom_call" | custom-call | flops 3623878656 | bytes 15728640 | tf_op jit(solution)/shard_map/expert/pallas_call | solution.py:268
  57.7 1.1 copy-done.26
  61.7 0.9 collective-permute-done.1.buf_ref.own_ref
  63.0 2.1 dispatch.6
  65.2 1.1 copy-done
  66.3 3.8 %all-to-all-start.3 = ((bf16[8,24,4096]{2,1,0:T(8,128)(2,1)}), bf16[8,24,4096]{2,1,0:T(8,128)(2,1)S(1)}, u32[]{:S(2)}, u32[]{:S(2)}) async-start(bf16[8,24,4096]{2,1,0:T(8,128)(2,1)} %copy-done), calls=%async_computation.3 | async-start | bytes 3145728 | tf_op jit(solution)/shard_map/all_to_all | solution.py:331
  71.6 1.9 copy-done.3
  73.5 1.9 copy-done.7
  75.4 1.9 copy-done.11
  77.3 7.5 %expert.5 = (bf16[48,4096]{1,0:T(8,128)(2,1)S(1)}, bf16[48,4096]{1,0:T(8,128)(2,1)S(1)}, bf16[48,4096]{1,0:T(8,128)(2,1)S(1)}, bf16[48,4096]{1,0:T(8,128)(2,1)S(...) custom-call(s32[1]{0:T(128)} %bitcast.me_ref, ...), custom_call_target="tpu_custom_call" | custom-call | flops 3623878656 | bytes 15728640 | tf_op jit(solution)/shard_map/expert/pallas_call | solution.py:268
  84.8 1.8 collective-permute-start.6
  86.6 1.5 collective-permute-start.7
  88.4 1.5 collective-permute-done.3.buf_ref.own_ref
  89.9 3.2 %dispatch.7 = bf16[8,24,4096]{2,1,0:T(8,128)(2,1)} custom-call(f32[8,192]{1,0:T(8,128)S(1)} %maximum_maximum_fusion.tab_ref, bf16[128,4224]{1,0:T(8,128)(2,1)} %collective-permute-done.3.buf_ref.own_ref), custom_call_target="tpu_custom_call" | custom-call | flops 6039797760 | bytes 79626240 | tf_op jit(solution)/shard_map/dispatch/pallas_call | solution.py:245
  93.2 6.0 %collective-permute-done.6.refs_1_ = bf16[48,4096]{1,0:T(8,128)(2,1)S(1)} collective-permute-done((bf16[48,4096]{1,0:T(8,128)(2,1)S(1)}, bf16[48,4096]{1,0:T(8,128)(2,1)S(1)}, u32[]{:S(2)}, u32[]{:S(2)}) %collective-permute-start.6) | collective-permute-done | bytes 393248 | tf_op jit(solution)/shard_map/ppermute | solution.py:262
  100.8 7.2 %collective-permute-done.8.refs_3_ = bf16[48,4096]{1,0:T(8,128)(2,1)S(1)} collective-permute-done((bf16[48,4096]{1,0:T(8,128)(2,1)S(1)}, bf16[48,4096]{1,0:T(8,128)(2,1)S(1)}, u32[]{:S(2)}, u32[]{:S(2)}) %collective-permute-start.8) | collective-permute-done | bytes 393248 | tf_op jit(solution)/shard_map/ppermute | solution.py:262
  108.8 3.8 %all-to-all-start.2 = ((bf16[8,24,4096]{2,1,0:T(8,128)(2,1)}), bf16[8,24,4096]{2,1,0:T(8,128)(2,1)S(1)}, u32[]{:S(2)}, u32[]{:S(2)}) async-start(bf16[8,24,4096]{2,1,0:T(8,128)(2,1)} %dispatch.7), calls=%async_computation.2 | async-start | bytes 3145728 | tf_op jit(solution)/shard_map/all_to_all | solution.py:331
  112.6 1.0 copy-done.21
  113.6 1.0 copy-done.23
  114.6 1.0 copy-done.25
  115.6 1.0 copy-done.37
  116.6 4.1 %combine.4 = (bf16[128,4224]{1,0:T(8,128)(2,1)S(1)}, bf16[128,4224]{1,0:T(8,128)(2,1)S(1)}) custom-call(f32[8,96]{1,0:T(8,128)S(1)} %maximum_maximum_fusion.1.tab_ref, bf16[128,4224]{1,0:T(8,128)(2,1)} %collective-permute-done.buf_ref.own_ref, bf16[128,4224]{1,0:T(8,128)(2,1)} %collective-permute-done.4.pair_ref, bf16[48,4096]{1,0:T(8,128)(2,1)S(1)} %copy-done.37, ...), custom_call_target="tpu_custom_call" | custom-call | flops 50331648000 | bytes 589824000 | tf_op jit(solution)/shard_map/combine/pallas_call | solution.py:293
  121.3 8.5 %expert.7 = (bf16[48,4096]{1,0:T(8,128)(2,1)S(1)}, bf16[48,4096]{1,0:T(8,128)(2,1)}, bf16[48,4096]{1,0:T(8,128)(2,1)}, bf16[48,4096]{1,0:T(8,128)(2,1)}, bf16[19...) custom-call(s32[1]{0:T(128)} %bitcast.me_ref, ...), custom_call_target="tpu_custom_call" | custom-call | flops 3623878656 | bytes 15728640 | tf_op jit(solution)/shard_map/expert/pallas_call | solution.py:268
  129.8 1.8 collective-permute-start.14
  131.6 1.5 collective-permute-start.15
  133.7 1.6 collective-permute-start.18
  135.3 1.1 copy-done.14
  136.4 1.9 copy-done.5
  138.3 1.9 copy-done.9
  140.1 1.9 copy-done.13
  142.0 7.5 %expert.6 = (bf16[48,4096]{1,0:T(8,128)(2,1)S(1)}, bf16[48,4096]{1,0:T(8,128)(2,1)S(1)}, bf16[48,4096]{1,0:T(8,128)(2,1)S(1)}, bf16[48,4096]{1,0:T(8,128)(2,1)S(...) custom-call(s32[1]{0:T(128)} %bitcast.me_ref, ...), custom_call_target="tpu_custom_call" | custom-call | flops 3623878656 | bytes 15728640 | tf_op jit(solution)/shard_map/expert/pallas_call | solution.py:268
  149.6 1.7 collective-permute-done.15.refs_2_
  151.3 4.2 %combine.5 = (bf16[128,4224]{1,0:T(8,128)(2,1)S(1)}, bf16[128,4224]{1,0:T(8,128)(2,1)S(1)}) custom-call(f32[8,96]{1,0:T(8,128)S(1)} %maximum_maximum_fusion.1.tab_ref, bf16[128,4224]{1,0:T(8,128)(2,1)} %collective-permute-done.1.buf_ref.own_ref, bf16[128,4224]{1,0:T(8,128)(2,1)} %collective-permute-done.13.pair_ref, bf16[48,4096]{1,0:T(8,128)(2,1)S(1)} %copy-done.35, ...), custom_call_target="tpu_custom_call" | custom-call | flops 50331648000 | bytes 589824000 | tf_op jit(solution)/shard_map/combine/pallas_call | solution.py:293
  155.5 1.3 collective-permute-start.10
  156.8 0.8 collective-permute-start.11
  157.6 1.4 collective-permute-start.12
  159.1 1.7 collective-permute-done.18.refs_2_
  160.8 1.8 join.4
  162.8 4.6 %collective-permute-done.10.refs_1_ = bf16[48,4096]{1,0:T(8,128)(2,1)S(1)} collective-permute-done((bf16[48,4096]{1,0:T(8,128)(2,1)S(1)}, bf16[48,4096]{1,0:T(8,128)(2,1)S(1)}, u32[]{:S(2)}, u32[]{:S(2)}) %collective-permute-start.10) | collective-permute-done | bytes 393248 | tf_op jit(solution)/shard_map/ppermute | solution.py:262
  167.5 7.3 %collective-permute-done.11.refs_2_ = bf16[48,4096]{1,0:T(8,128)(2,1)S(1)} collective-permute-done((bf16[48,4096]{1,0:T(8,128)(2,1)S(1)}, bf16[48,4096]{1,0:T(8,128)(2,1)S(1)}, u32[]{:S(2)}, u32[]{:S(2)}) %collective-permute-start.11) | collective-permute-done | bytes 393248 | tf_op jit(solution)/shard_map/ppermute | solution.py:262
  174.8 1.6 collective-permute-done.12.refs_3_
  176.4 0.8 collective-permute-start.22
  177.2 1.5 collective-permute-start.23
  178.7 1.2 collective-permute-start.24
  179.9 3.6 %combine.6 = (bf16[128,4224]{1,0:T(8,128)(2,1)S(1)}, bf16[128,4224]{1,0:T(8,128)(2,1)S(1)}) custom-call(f32[8,96]{1,0:T(8,128)S(1)} %maximum_maximum_fusion.1.tab_ref, bf16[128,4224]{1,0:T(8,128)(2,1)} %collective-permute-done.3.buf_ref.own_ref, bf16[128,4224]{1,0:T(8,128)(2,1)S(1)} %copy-done.15, bf16[48,4096]{1,0:T(8,128)(2,1)S(1)} %get-tuple-element.162.refs_0_, ...), custom_call_target="tpu_custom_call" | custom-call | flops 50331648000 | bytes 589824000 | tf_op jit(solution)/shard_map/combine/pallas_call | solution.py:293
  183.6 4.8 %collective-permute-done.22.refs_1_ = bf16[48,4096]{1,0:T(8,128)(2,1)S(1)} collective-permute-done((bf16[48,4096]{1,0:T(8,128)(2,1)S(1)}, bf16[48,4096]{1,0:T(8,128)(2,1)S(1)}, u32[]{:S(2)}, u32[]{:S(2)}) %collective-permute-start.22) | collective-permute-done | bytes 393248 | tf_op jit(solution)/shard_map/ppermute | solution.py:262
  188.4 7.4 %collective-permute-done.23.refs_2_ = bf16[48,4096]{1,0:T(8,128)(2,1)S(1)} collective-permute-done((bf16[48,4096]{1,0:T(8,128)(2,1)S(1)}, bf16[48,4096]{1,0:T(8,128)(2,1)S(1)}, u32[]{:S(2)}, u32[]{:S(2)}) %collective-permute-start.23) | collective-permute-done | bytes 393248 | tf_op jit(solution)/shard_map/ppermute | solution.py:262
  195.9 4.1 %combine.7 = (bf16[128,4224]{1,0:T(8,128)(2,1)S(1)}, bf16[128,4224]{1,0:T(8,128)(2,1)S(1)}) custom-call(f32[8,96]{1,0:T(8,128)S(1)} %maximum_maximum_fusion.1.tab_ref, bf16[128,4224]{1,0:T(8,128)(2,1)} %concatenate.10.buf_ref.own_ref, bf16[128,4224]{1,0:T(8,128)(2,1)} %collective-permute-done.2.pair_ref, bf16[48,4096]{1,0:T(8,128)(2,1)S(1)} %copy-done.33, ...), custom_call_target="tpu_custom_call" | custom-call | flops 50331648000 | bytes 589824000 | tf_op jit(solution)/shard_map/combine/pallas_call | solution.py:293
  200.6 1.7 collective-permute-start.21
  202.4 13.7 %weight_grads.1 = (bf16[1,2048,768]{2,1,0:T(8,128)(2,1)}, bf16[1,2048,768]{2,1,0:T(8,128)(2,1)}, bf16[1,768,2048]{2,1,0:T(8,128)(2,1)}) custom-call(bf16[192,4096]{1,0:T(8,128)(2,1)S(1)} %copy-done.27, bf16[192,4096]{1,0:T(8,128)(2,1)S(1)} %copy-done.29, bf16[192,4096]{1,0:T(8,128)(2,1)S(1)} %copy-done.31, ...), custom_call_target="tpu_custom_call" | custom-call | flops 7247757312 | bytes 15728640 | tf_op jit(solution)/shard_map/weight_grads/pallas_call | solution.py:389
  216.0 12.7 %collective-permute-done.21.refs_0_ = bf16[128,4224]{1,0:T(8,128)(2,1)S(1)} collective-permute-done((bf16[128,4224]{1,0:T(8,128)(2,1)S(1)}, bf16[128,4224]{1,0:T(8,128)(2,1)S(1)}, u32[]{:S(2)}, u32[]{:S(2)}) %collective-permute-start.21) | collective-permute-done | bytes 1081376 | tf_op jit(solution)/shard_map/ppermute | solution.py:319
  228.7 1.6 final.1
  (149 shorter events, 14.9 us)
Async XLA Ops:
  6.3 29.2 %collective-permute-start = (bf16[128,4224]{1,0:T(8,128)(2,1)}, bf16[128,4224]{1,0:T(8,128)(2,1)}, u32[]{:S(2)}, u32[]{:S(2)}) collective-permute-start(bf16[128,4224]{1,0:T(8,128)(2,1)} %concatenate.10.buf_ref.own_ref), channel_id=1, source_target_pairs={{0,8},{8,16},{16,24},{24,0},{1,9},{9,17},{17,25},{25,1},{2,10},{10... | collective-permute-start | bytes 3244040 | tf_op jit(solution)/shard_map/ppermute | solution.py:319
  9.6 3.3 %copy-start.56 = (f32[8]{0:T(128)}, f32[8]{0:T(128)S(1)}, u32[]{:S(2)}) copy-start(f32[8]{0:T(128)S(1)} %pad.5.clone) | copy-start | bytes 100
  12.9 25.9 %all-to-all-start = ((bf16[8,24,4096]{2,1,0:T(8,128)(2,1)}), bf16[8,24,4096]{2,1,0:T(8,128)(2,1)S(1)}, u32[]{:S(2)}, u32[]{:S(2)}) async-start(bf16[8,24,4096]{2,1,0:T(8,128)(2,1)} %dispatch.4), calls=%async_computation | async-start | bytes 3145728 | tf_op jit(solution)/shard_map/all_to_all | solution.py:331
  16.6 26.4 %collective-permute-start.2 = (bf16[128,4224]{1,0:T(8,128)(2,1)}, bf16[128,4224]{1,0:T(8,128)(2,1)}, u32[]{:S(2)}, u32[]{:S(2)}) collective-permute-start(bf16[128,4224]{1,0:T(8,128)(2,1)} %concatenate.10.buf_ref.own_ref), channel_id=1, source_target_pairs={{0,1},{1,0},{2,3},{3,2},{4,5},{5,4},{6,7},{7,6},{8,9},{9,8},{10,11... | collective-permute-start | bytes 3244040 | tf_op jit(solution)/shard_map/ppermute | solution.py:258
  35.5 27.2 %collective-permute-start.1 = (bf16[128,4224]{1,0:T(8,128)(2,1)}, bf16[128,4224]{1,0:T(8,128)(2,1)}, u32[]{:S(2)}, u32[]{:S(2)}) collective-permute-start(bf16[128,4224]{1,0:T(8,128)(2,1)} %collective-permute-done.buf_ref.own_ref), channel_id=1, source_target_pairs={{0,8},{8,16},{16,24},{24,0},{1,9},{9,17},{17,25},{25,1},{2,10},{10... | collective-permute-start | bytes 3244040 | tf_op jit(solution)/shard_map/ppermute | solution.py:319
  38.8 27.5 %all-to-all-start.1 = ((bf16[8,24,4096]{2,1,0:T(8,128)(2,1)}), bf16[8,24,4096]{2,1,0:T(8,128)(2,1)S(1)}, u32[]{:S(2)}, u32[]{:S(2)}) async-start(bf16[8,24,4096]{2,1,0:T(8,128)(2,1)} %copy-done.1), calls=%async_computation.1 | async-start | bytes 3145728 | tf_op jit(solution)/shard_map/all_to_all | solution.py:331
  42.5 29.1 %collective-permute-start.4 = (bf16[128,4224]{1,0:T(8,128)(2,1)}, bf16[128,4224]{1,0:T(8,128)(2,1)}, u32[]{:S(2)}, u32[]{:S(2)}) collective-permute-start(bf16[128,4224]{1,0:T(8,128)(2,1)} %collective-permute-done.buf_ref.own_ref), channel_id=1, source_target_pairs={{0,1},{1,0},{2,3},{3,2},{4,5},{5,4},{6,7},{7,6},{8,9},{9,8},{10,11... | collective-permute-start | bytes 3244040 | tf_op jit(solution)/shard_map/ppermute | solution.py:258
  43.0 1.9 copy-start.2
  62.7 27.3 %collective-permute-start.3 = (bf16[128,4224]{1,0:T(8,128)(2,1)}, bf16[128,4224]{1,0:T(8,128)(2,1)}, u32[]{:S(2)}, u32[]{:S(2)}) collective-permute-start(bf16[128,4224]{1,0:T(8,128)(2,1)} %collective-permute-done.1.buf_ref.own_ref), channel_id=1, source_target_pairs={{0,8},{8,16},{16,24},{24,0},{1,9},{9,17},{17,25},{25,1},{2,10},{10... | collective-permute-start | bytes 3244040 | tf_op jit(solution)/shard_map/ppermute | solution.py:319
  66.3 42.5 %all-to-all-start.3 = ((bf16[8,24,4096]{2,1,0:T(8,128)(2,1)}), bf16[8,24,4096]{2,1,0:T(8,128)(2,1)S(1)}, u32[]{:S(2)}, u32[]{:S(2)}) async-start(bf16[8,24,4096]{2,1,0:T(8,128)(2,1)} %copy-done), calls=%async_computation.3 | async-start | bytes 3145728 | tf_op jit(solution)/shard_map/all_to_all | solution.py:331
  71.1 50.2 %collective-permute-start.13 = (bf16[128,4224]{1,0:T(8,128)(2,1)}, bf16[128,4224]{1,0:T(8,128)(2,1)}, u32[]{:S(2)}, u32[]{:S(2)}) collective-permute-start(bf16[128,4224]{1,0:T(8,128)(2,1)} %collective-permute-done.1.buf_ref.own_ref), channel_id=1, source_target_pairs={{0,1},{1,0},{2,3},{3,2},{4,5},{5,4},{6,7},{7,6},{8,9},{9,8},{10,11... | collective-permute-start | bytes 3244040 | tf_op jit(solution)/shard_map/ppermute | solution.py:258
  71.6 1.9 copy-start.3
  84.8 8.4 %copy-start.28 = (bf16[192,4096]{1,0:T(8,128)(2,1)}, bf16[192,4096]{1,0:T(8,128)(2,1)S(1)}, u32[]{:S(2)}) copy-start(bf16[192,4096]{1,0:T(8,128)(2,1)S(1)} %get-tuple-element.190.refs_1_.refs_5_) | copy-start | bytes 4718596
  84.8 8.4 %copy-start.36 = (bf16[48,4096]{1,0:T(8,128)(2,1)}, bf16[48,4096]{1,0:T(8,128)(2,1)S(1)}, u32[]{:S(2)}) copy-start(bf16[48,4096]{1,0:T(8,128)(2,1)S(1)} %get-tuple-element.131.refs_0_) | copy-start | bytes 1179652
  84.8 8.4 %copy-start.44 = (bf16[192,768]{1,0:T(8,128)(2,1)}, bf16[192,768]{1,0:T(8,128)(2,1)S(1)}, u32[]{:S(2)}) copy-start(bf16[192,768]{1,0:T(8,128)(2,1)S(1)} %get-tuple-element.202.refs_9_) | copy-start | bytes 884740
  84.8 8.4 %copy-start.46 = (bf16[192,768]{1,0:T(8,128)(2,1)}, bf16[192,768]{1,0:T(8,128)(2,1)S(1)}, u32[]{:S(2)}) copy-start(bf16[192,768]{1,0:T(8,128)(2,1)S(1)} %get-tuple-element.206.refs_13_) | copy-start | bytes 884740
  84.8 8.4 %copy-start.48 = (bf16[192,768]{1,0:T(8,128)(2,1)}, bf16[192,768]{1,0:T(8,128)(2,1)S(1)}, u32[]{:S(2)}) copy-start(bf16[192,768]{1,0:T(8,128)(2,1)S(1)} %get-tuple-element.210.refs_17_) | copy-start | bytes 884740
  84.8 14.4 %collective-permute-start.6 = (bf16[48,4096]{1,0:T(8,128)(2,1)S(1)}, bf16[48,4096]{1,0:T(8,128)(2,1)S(1)}, u32[]{:S(2)}, u32[]{:S(2)}) collective-permute-start(bf16[48,4096]{1,0:T(8,128)(2,1)S(1)} %get-tuple-element.128), channel_id=1, source_target_pairs={{0,2},{1,3},{2,0},{3,1},{4,6},{5,7},{6,4},{7,5},{8,10},{9,11},{10,... | collective-permute-start | bytes 1179656 | tf_op jit(solution)/shard_map/ppermute | solution.py:262
  86.6 13.5 %collective-permute-start.7 = (bf16[48,4096]{1,0:T(8,128)(2,1)S(1)}, bf16[48,4096]{1,0:T(8,128)(2,1)S(1)}, u32[]{:S(2)}, u32[]{:S(2)}) collective-permute-start(bf16[48,4096]{1,0:T(8,128)(2,1)S(1)} %get-tuple-element.129), channel_id=1, source_target_pairs={{0,4},{1,5},{2,6},{3,7},{4,0},{5,1},{6,2},{7,3},{8,12},{9,13},{10,... | collective-permute-start | bytes 1179656 | tf_op jit(solution)/shard_map/ppermute | solution.py:262
  88.1 20.0 %collective-permute-start.8 = (bf16[48,4096]{1,0:T(8,128)(2,1)S(1)}, bf16[48,4096]{1,0:T(8,128)(2,1)S(1)}, u32[]{:S(2)}, u32[]{:S(2)}) collective-permute-start(bf16[48,4096]{1,0:T(8,128)(2,1)S(1)} %get-tuple-element.130), channel_id=1, source_target_pairs={{0,6},{1,7},{2,4},{3,5},{4,2},{5,3},{6,0},{7,1},{8,14},{9,15},{10,... | collective-permute-start | bytes 1179656 | tf_op jit(solution)/shard_map/ppermute | solution.py:262
  108.8 27.5 %all-to-all-start.2 = ((bf16[8,24,4096]{2,1,0:T(8,128)(2,1)}), bf16[8,24,4096]{2,1,0:T(8,128)(2,1)S(1)}, u32[]{:S(2)}, u32[]{:S(2)}) async-start(bf16[8,24,4096]{2,1,0:T(8,128)(2,1)} %dispatch.7), calls=%async_computation.2 | async-start | bytes 3145728 | tf_op jit(solution)/shard_map/all_to_all | solution.py:331
  116.6 4.7 %copy-start.4 = (bf16[1,2048,768]{2,1,0:T(8,128)(2,1)S(1)}, bf16[1,2048,768]{2,1,0:T(8,128)(2,1)}, u32[]{:S(2)}) copy-start(bf16[1,2048,768]{2,1,0:T(8,128)(2,1)} %refs_0_.7) | copy-start | bytes 9437188
  116.6 4.7 %copy-start.8 = (bf16[1,2048,768]{2,1,0:T(8,128)(2,1)S(1)}, bf16[1,2048,768]{2,1,0:T(8,128)(2,1)}, u32[]{:S(2)}) copy-start(bf16[1,2048,768]{2,1,0:T(8,128)(2,1)} %refs_1_.7) | copy-start | bytes 9437188
  116.6 4.7 %copy-start.12 = (bf16[1,768,2048]{2,1,0:T(8,128)(2,1)S(1)}, bf16[1,768,2048]{2,1,0:T(8,128)(2,1)}, u32[]{:S(2)}) copy-start(bf16[1,768,2048]{2,1,0:T(8,128)(2,1)} %refs_2_.7) | copy-start | bytes 9437188
  120.7 12.7 %collective-permute-start.9 = (bf16[128,4224]{1,0:T(8,128)(2,1)S(1)}, bf16[128,4224]{1,0:T(8,128)(2,1)S(1)}, u32[]{:S(2)}, u32[]{:S(2)}) collective-permute-start(bf16[128,4224]{1,0:T(8,128)(2,1)S(1)} %get-tuple-element.136), channel_id=1, source_target_pairs={{0,1},{1,0},{2,3},{3,2},{4,5},{5,4},{6,7},{7,6},{8,9},{9,8},{10,11... | collective-permute-start | bytes 3244040 | tf_op jit(solution)/shard_map/ppermute | solution.py:258
  121.0 14.3 %collective-permute-start.5 = (bf16[128,4224]{1,0:T(8,128)(2,1)}, bf16[128,4224]{1,0:T(8,128)(2,1)S(1)}, u32[]{:S(2)}, u32[]{:S(2)}) collective-permute-start(bf16[128,4224]{1,0:T(8,128)(2,1)} %collective-permute-done.3.buf_ref.own_ref), channel_id=1, source_target_pairs={{0,1},{1,0},{2,3},{3,2},{4,5},{5,4},{6,7},{7,6},{8,9},{9,8},{10,11... | collective-permute-start | bytes 3244040 | tf_op jit(solution)/shard_map/ppermute | solution.py:258
  129.8 3.8 %copy-start.30 = (bf16[192,4096]{1,0:T(8,128)(2,1)}, bf16[192,4096]{1,0:T(8,128)(2,1)S(1)}, u32[]{:S(2)}) copy-start(bf16[192,4096]{1,0:T(8,128)(2,1)S(1)} %get-tuple-element.195.refs_2_.refs_6_) | copy-start | bytes 4718596
  129.8 3.8 %copy-start.34 = (bf16[48,4096]{1,0:T(8,128)(2,1)}, bf16[48,4096]{1,0:T(8,128)(2,1)S(1)}, u32[]{:S(2)}) copy-start(bf16[48,4096]{1,0:T(8,128)(2,1)S(1)} %get-tuple-element.156.refs_0_) | copy-start | bytes 1179652
  129.8 3.8 %copy-start.50 = (bf16[192,768]{1,0:T(8,128)(2,1)}, bf16[192,768]{1,0:T(8,128)(2,1)S(1)}, u32[]{:S(2)}) copy-start(bf16[192,768]{1,0:T(8,128)(2,1)S(1)} %get-tuple-element.203.refs_10_) | copy-start | bytes 884740
  129.8 3.9 %copy-start.52 = (bf16[192,768]{1,0:T(8,128)(2,1)}, bf16[192,768]{1,0:T(8,128)(2,1)S(1)}, u32[]{:S(2)}) copy-start(bf16[192,768]{1,0:T(8,128)(2,1)S(1)} %get-tuple-element.207.refs_14_) | copy-start | bytes 884740
  129.8 3.9 %copy-start.54 = (bf16[192,768]{1,0:T(8,128)(2,1)}, bf16[192,768]{1,0:T(8,128)(2,1)S(1)}, u32[]{:S(2)}) copy-start(bf16[192,768]{1,0:T(8,128)(2,1)S(1)} %get-tuple-element.211.refs_18_) | copy-start | bytes 884740
  129.8 19.8 %collective-permute-start.14 = (bf16[48,4096]{1,0:T(8,128)(2,1)}, bf16[48,4096]{1,0:T(8,128)(2,1)S(1)}, u32[]{:S(2)}, u32[]{:S(2)}) collective-permute-start(bf16[48,4096]{1,0:T(8,128)(2,1)} %get-tuple-element.153), channel_id=1, source_target_pairs={{0,2},{1,3},{2,0},{3,1},{4,6},{5,7},{6,4},{7,5},{8,10},{9,11},{10,... | collective-permute-start | bytes 1179656 | tf_op jit(solution)/shard_map/ppermute | solution.py:262
  131.6 19.6 %collective-permute-start.15 = (bf16[48,4096]{1,0:T(8,128)(2,1)}, bf16[48,4096]{1,0:T(8,128)(2,1)}, u32[]{:S(2)}, u32[]{:S(2)}) collective-permute-start(bf16[48,4096]{1,0:T(8,128)(2,1)} %get-tuple-element.154), channel_id=1, source_target_pairs={{0,4},{1,5},{2,6},{3,7},{4,0},{5,1},{6,2},{7,3},{8,12},{9,13},{10,... | collective-permute-start | bytes 1179656 | tf_op jit(solution)/shard_map/ppermute | solution.py:262
  133.1 18.1 %collective-permute-start.16 = (bf16[48,4096]{1,0:T(8,128)(2,1)}, bf16[48,4096]{1,0:T(8,128)(2,1)}, u32[]{:S(2)}, u32[]{:S(2)}) collective-permute-start(bf16[48,4096]{1,0:T(8,128)(2,1)} %get-tuple-element.155), channel_id=1, source_target_pairs={{0,6},{1,7},{2,4},{3,5},{4,2},{5,3},{6,0},{7,1},{8,14},{9,15},{10,... | collective-permute-start | bytes 1179656 | tf_op jit(solution)/shard_map/ppermute | solution.py:262
  133.7 27.1 %collective-permute-start.18 = (bf16[128,4224]{1,0:T(8,128)(2,1)S(1)}, bf16[128,4224]{1,0:T(8,128)(2,1)}, u32[]{:S(2)}, u32[]{:S(2)}) collective-permute-start(bf16[128,4224]{1,0:T(8,128)(2,1)S(1)} %join.3), channel_id=1, source_target_pairs={{0,8},{8,16},{16,24},{24,0},{1,9},{9,17},{17,25},{25,1},{2,10},{10... | collective-permute-start | bytes 3244040 | tf_op jit(solution)/shard_map/ppermute | solution.py:319
  136.4 1.9 copy-start.5
  142.0 9.2 %copy-start.35 = (bf16[48,4096]{1,0:T(8,128)(2,1)S(1)}, bf16[48,4096]{1,0:T(8,128)(2,1)}, u32[]{:S(2)}) copy-start(bf16[48,4096]{1,0:T(8,128)(2,1)} %copy-done.34) | copy-start | bytes 1179652
  155.4 5.4 %collective-permute-start.17 = (bf16[128,4224]{1,0:T(8,128)(2,1)S(1)}, bf16[128,4224]{1,0:T(8,128)(2,1)S(1)}, u32[]{:S(2)}, u32[]{:S(2)}) collective-permute-start(bf16[128,4224]{1,0:T(8,128)(2,1)S(1)} %get-tuple-element.161), channel_id=1, source_target_pairs={{0,1},{1,0},{2,3},{3,2},{4,5},{5,4},{6,7},{7,6},{8,9},{9,8},{10,11... | collective-permute-start | bytes 3244040 | tf_op jit(solution)/shard_map/ppermute | solution.py:258
  155.5 12.0 %collective-permute-start.10 = (bf16[48,4096]{1,0:T(8,128)(2,1)S(1)}, bf16[48,4096]{1,0:T(8,128)(2,1)S(1)}, u32[]{:S(2)}, u32[]{:S(2)}) collective-permute-start(bf16[48,4096]{1,0:T(8,128)(2,1)S(1)} %get-tuple-element.143), channel_id=1, source_target_pairs={{0,2},{1,3},{2,0},{3,1},{4,6},{5,7},{6,4},{7,5},{8,10},{9,11},{10,... | collective-permute-start | bytes 1179656 | tf_op jit(solution)/shard_map/ppermute | solution.py:262
  156.8 18.0 %collective-permute-start.11 = (bf16[48,4096]{1,0:T(8,128)(2,1)S(1)}, bf16[48,4096]{1,0:T(8,128)(2,1)S(1)}, u32[]{:S(2)}, u32[]{:S(2)}) collective-permute-start(bf16[48,4096]{1,0:T(8,128)(2,1)S(1)} %get-tuple-element.144), channel_id=1, source_target_pairs={{0,4},{1,5},{2,6},{3,7},{4,0},{5,1},{6,2},{7,3},{8,12},{9,13},{10,... | collective-permute-start | bytes 1179656 | tf_op jit(solution)/shard_map/ppermute | solution.py:262
  157.6 18.8 %collective-permute-start.12 = (bf16[48,4096]{1,0:T(8,128)(2,1)S(1)}, bf16[48,4096]{1,0:T(8,128)(2,1)S(1)}, u32[]{:S(2)}, u32[]{:S(2)}) collective-permute-start(bf16[48,4096]{1,0:T(8,128)(2,1)S(1)} %get-tuple-element.145), channel_id=1, source_target_pairs={{0,6},{1,7},{2,4},{3,5},{4,2},{5,3},{6,0},{7,1},{8,14},{9,15},{10,... | collective-permute-start | bytes 1179656 | tf_op jit(solution)/shard_map/ppermute | solution.py:262
  160.8 15.6 %copy-start.19 = (bf16[48,4096]{1,0:T(8,128)(2,1)S(1)}, bf16[48,4096]{1,0:T(8,128)(2,1)}, u32[]{:S(2)}) copy-start(bf16[48,4096]{1,0:T(8,128)(2,1)} %copy-done.18) | copy-start | bytes 1179652
  160.8 16.4 %copy-start.17 = (bf16[48,4096]{1,0:T(8,128)(2,1)S(1)}, bf16[48,4096]{1,0:T(8,128)(2,1)}, u32[]{:S(2)}) copy-start(bf16[48,4096]{1,0:T(8,128)(2,1)} %copy-done.16) | copy-start | bytes 1179652
  160.8 19.1 %copy-start.15 = (bf16[128,4224]{1,0:T(8,128)(2,1)S(1)}, bf16[128,4224]{1,0:T(8,128)(2,1)}, u32[]{:S(2)}) copy-start(bf16[128,4224]{1,0:T(8,128)(2,1)} %copy-done.14) | copy-start | bytes 3244036
  162.6 33.3 %copy-start.33 = (bf16[48,4096]{1,0:T(8,128)(2,1)S(1)}, bf16[48,4096]{1,0:T(8,128)(2,1)}, u32[]{:S(2)}) copy-start(bf16[48,4096]{1,0:T(8,128)(2,1)} %copy-done.32) | copy-start | bytes 1179652
  162.6 37.5 %collective-permute-start.20 = (bf16[128,4224]{1,0:T(8,128)(2,1)S(1)}, bf16[128,4224]{1,0:T(8,128)(2,1)S(1)}, u32[]{:S(2)}, u32[]{:S(2)}) collective-permute-start(bf16[128,4224]{1,0:T(8,128)(2,1)S(1)} %join.4), channel_id=1, source_target_pairs={{0,8},{8,16},{16,24},{24,0},{1,9},{9,17},{17,25},{25,1},{2,10},{10... | collective-permute-start | bytes 3244040 | tf_op jit(solution)/shard_map/ppermute | solution.py:319
  176.4 12.0 %collective-permute-start.22 = (bf16[48,4096]{1,0:T(8,128)(2,1)S(1)}, bf16[48,4096]{1,0:T(8,128)(2,1)S(1)}, u32[]{:S(2)}, u32[]{:S(2)}) collective-permute-start(bf16[48,4096]{1,0:T(8,128)(2,1)S(1)} %copy-done.19), channel_id=1, source_target_pairs={{0,2},{1,3},{2,0},{3,1},{4,6},{5,7},{6,4},{7,5},{8,10},{9,11},{10,... | collective-permute-start | bytes 1179656 | tf_op jit(solution)/shard_map/ppermute | solution.py:262
  177.2 18.6 %collective-permute-start.23 = (bf16[48,4096]{1,0:T(8,128)(2,1)S(1)}, bf16[48,4096]{1,0:T(8,128)(2,1)S(1)}, u32[]{:S(2)}, u32[]{:S(2)}) collective-permute-start(bf16[48,4096]{1,0:T(8,128)(2,1)S(1)} %copy-done.17), channel_id=1, source_target_pairs={{0,4},{1,5},{2,6},{3,7},{4,0},{5,1},{6,2},{7,3},{8,12},{9,13},{10,... | collective-permute-start | bytes 1179656 | tf_op jit(solution)/shard_map/ppermute | solution.py:262
  178.7 17.1 %collective-permute-start.24 = (bf16[48,4096]{1,0:T(8,128)(2,1)S(1)}, bf16[48,4096]{1,0:T(8,128)(2,1)S(1)}, u32[]{:S(2)}, u32[]{:S(2)}) collective-permute-start(bf16[48,4096]{1,0:T(8,128)(2,1)S(1)} %get-tuple-element.171), channel_id=1, source_target_pairs={{0,6},{1,7},{2,4},{3,5},{4,2},{5,3},{6,0},{7,1},{8,14},{9,15},{10,... | collective-permute-start | bytes 1179656 | tf_op jit(solution)/shard_map/ppermute | solution.py:262
  183.5 16.5 %collective-permute-start.19 = (bf16[128,4224]{1,0:T(8,128)(2,1)S(1)}, bf16[128,4224]{1,0:T(8,128)(2,1)S(1)}, u32[]{:S(2)}, u32[]{:S(2)}) collective-permute-start(bf16[128,4224]{1,0:T(8,128)(2,1)S(1)} %get-tuple-element.167), channel_id=1, source_target_pairs={{0,1},{1,0},{2,3},{3,2},{4,5},{5,4},{6,7},{7,6},{8,9},{9,8},{10,11... | collective-permute-start | bytes 3244040 | tf_op jit(solution)/shard_map/ppermute | solution.py:258
  195.8 6.5 %copy-start.31 = (bf16[192,4096]{1,0:T(8,128)(2,1)S(1)}, bf16[192,4096]{1,0:T(8,128)(2,1)}, u32[]{:S(2)}) copy-start(bf16[192,4096]{1,0:T(8,128)(2,1)} %copy-done.30) | copy-start | bytes 4718596
  195.8 6.5 %copy-start.47 = (bf16[192,768]{1,0:T(8,128)(2,1)S(1)}, bf16[192,768]{1,0:T(8,128)(2,1)}, u32[]{:S(2)}) copy-start(bf16[192,768]{1,0:T(8,128)(2,1)} %copy-done.46) | copy-start | bytes 884740
  195.8 6.5 %copy-start.49 = (bf16[192,768]{1,0:T(8,128)(2,1)S(1)}, bf16[192,768]{1,0:T(8,128)(2,1)}, u32[]{:S(2)}) copy-start(bf16[192,768]{1,0:T(8,128)(2,1)} %copy-done.48) | copy-start | bytes 884740
  195.8 6.5 %copy-start.51 = (bf16[192,768]{1,0:T(8,128)(2,1)S(1)}, bf16[192,768]{1,0:T(8,128)(2,1)}, u32[]{:S(2)}) copy-start(bf16[192,768]{1,0:T(8,128)(2,1)} %copy-done.50) | copy-start | bytes 884740
  195.9 6.5 %copy-start.53 = (bf16[192,768]{1,0:T(8,128)(2,1)S(1)}, bf16[192,768]{1,0:T(8,128)(2,1)}, u32[]{:S(2)}) copy-start(bf16[192,768]{1,0:T(8,128)(2,1)} %copy-done.52) | copy-start | bytes 884740
  195.9 6.5 %copy-start.55 = (bf16[192,768]{1,0:T(8,128)(2,1)S(1)}, bf16[192,768]{1,0:T(8,128)(2,1)}, u32[]{:S(2)}) copy-start(bf16[192,768]{1,0:T(8,128)(2,1)} %copy-done.54) | copy-start | bytes 884740
  200.0 16.1 %collective-permute-start.25 = (bf16[128,4224]{1,0:T(8,128)(2,1)S(1)}, bf16[128,4224]{1,0:T(8,128)(2,1)S(1)}, u32[]{:S(2)}, u32[]{:S(2)}) collective-permute-start(bf16[128,4224]{1,0:T(8,128)(2,1)S(1)} %get-tuple-element.177), channel_id=1, source_target_pairs={{0,1},{1,0},{2,3},{3,2},{4,5},{5,4},{6,7},{7,6},{8,9},{9,8},{10,11... | collective-permute-start | bytes 3244040 | tf_op jit(solution)/shard_map/ppermute | solution.py:258
  200.1 2.2 copy-start.27
  200.1 2.2 copy-start.29
  200.1 2.2 copy-start.39
  200.1 2.2 copy-start.41
  200.1 2.2 copy-start.43
  200.1 2.2 copy-start.45
  200.6 28.1 %collective-permute-start.21 = (bf16[128,4224]{1,0:T(8,128)(2,1)S(1)}, bf16[128,4224]{1,0:T(8,128)(2,1)S(1)}, u32[]{:S(2)}, u32[]{:S(2)}) collective-permute-start(bf16[128,4224]{1,0:T(8,128)(2,1)S(1)} %join.5), channel_id=1, source_target_pairs={{0,8},{8,16},{16,24},{24,0},{1,9},{9,17},{17,25},{25,1},{2,10},{10... | collective-permute-start | bytes 3244040 | tf_op jit(solution)/shard_map/ppermute | solution.py:319
  (23 other events, 26.4 us)

commit v3 on v2

--- a/solution.py
+++ b/solution.py
@@ -46,6 +46,15 @@
     rank = dot(earlier, hit.astype(BF16))
     sel = jnp.where(rank == place, hit, 0.0)
     return sel, gate, hits
+
+
+def pack_kernel(top, width, tokens_ref, cotangent_ref, ids_ref, gates_ref, buf_ref):
+    tok = tokens_ref.shape[0]
+    buf_ref[:, :width] = tokens_ref[...]
+    buf_ref[:, width : 2 * width] = cotangent_ref[...]
+    parts = [p.astype(F32) for p in split3(gates_ref[...])]
+    rows = [ids_ref[...].astype(F32), *parts, jnp.zeros((META - 4 * top, tok), F32)]
+    buf_ref[:, 2 * width :] = jnp.concatenate(rows, axis=0).T.astype(BF16)
 
 
 def dispatch_kernel(top, width, tab_ref, buf_ref, out_ref):
@@ -172,13 +181,8 @@
 
     mixed_ref[...] = total(0, width).astype(BF16)
     d_tok_ref[...] = total(width, 2 * width).astype(BF16)
-    packed = total(2 * width, 2 * width + META)
-    for k in range(top):
-        d_gates_ref[:, k : k + 1] = (
-            packed[:, k : k + 1]
-            + packed[:, top + k : top + k + 1]
-            + packed[:, 2 * top + k : 2 * top + k + 1]
-        )
+    packed = total(2 * width, 2 * width + META).T
+    d_gates_ref[...] = packed[:top] + packed[top : 2 * top] + packed[2 * top : 3 * top]
 
 
 def weight_grad_kernel(stages, *refs):
@@ -200,6 +204,10 @@
 
 def whole(shape):
     return pl.BlockSpec(shape, lambda *_: (0,) * len(shape))
+
+
+def in_hbm(v):
+    return pltpu.with_memory_space_constraint(v, pltpu.HBM)
 
 
 def params():
@@ -230,21 +238,26 @@
 
     tab_in = table(jnp.arange(count, dtype=jnp.int32))
     tab_back = table(jnp.bitwise_xor(2 * jnp.arange(chips, dtype=jnp.int32), me))
-    meta = jnp.concatenate(
-        [expert_ids.astype(BF16), *split3(gates), jnp.zeros((tok, META - 4 * top), BF16)], 1
-    )
-    buf0 = jnp.concatenate([tokens, cotangent, meta], axis=1)
     wide = 2 * width + META
+    buf0 = pl.pallas_call(
+        functools.partial(pack_kernel, top, width),
+        out_shape=jax.ShapeDtypeStruct((tok, wide), BF16),
+        compiler_params=params(),
+        cost_estimate=pl.CostEstimate(
+            flops=tok * META, bytes_accessed=4 * tok * wide, transcendentals=0
+        ),
+        name="pack",
+    )(in_hbm(tokens), in_hbm(cotangent), expert_ids.T, gates.T)
     row = jax.ShapeDtypeStruct((tok, wide), BF16)
 
-    piece = jax.ShapeDtypeStruct((2 * rows_p, 2 * width), BF16)
+    piece = pltpu.HBM((2 * rows_p, 2 * width), BF16)
     tile = 256
     steps = hidden_width // tile
 
     def dispatch(buf):
         return pl.pallas_call(
             functools.partial(dispatch_kernel, top, width),
-            out_shape=jax.ShapeDtypeStruct((count, rows_p, 2 * width), BF16),
+            out_shape=pltpu.HBM((count, rows_p, 2 * width), BF16),
             compiler_params=params(),
             cost_estimate=pl.CostEstimate(
                 flops=4 * slots * tok * width * 30,
@@ -264,7 +277,7 @@
         ]
 
     def expert(rows):
-        mid = jax.ShapeDtypeStruct((slots, hidden_width), BF16)
+        mid = pltpu.HBM((slots, hidden_width), BF16)
         got = pl.pallas_call(
             functools.partial(expert_kernel, chips, width),
             grid=(steps,),
@@ -276,7 +289,7 @@
             + [whole((slots, 2 * width))]
             + [pl.BlockSpec((slots, tile), lambda f: (0, f))] * 3,
             out_shape=[piece] * chips
-            + [jax.ShapeDtypeStruct((slots, 2 * width), BF16)]
+            + [pltpu.HBM((slots, 2 * width), BF16)]
             + [mid] * 3,
             scratch_shapes=[pltpu.VMEM((slots, width), F32)] * 2,
             compiler_params=params(),
@@ -286,17 +299,17 @@
                 transcendentals=slots * hidden_width,
             ),
             name="expert",
-        )(me.reshape(1), rows, w_gate, w_up, w_down)
+        )(me.reshape(1), rows, *[in_hbm(w) for w in (w_gate, w_up, w_down)])
         return got[:chips], got[chips:]
 
-    def combine(buf, pair, pieces):
+    def combine(buf, pair, pieces, weight):
         return pl.pallas_call(
             functools.partial(combine_kernel, chips, top, width),
             out_shape=[row, row],
             compiler_params=params(),
             cost_estimate=pl.CostEstimate(
-                flops=10 * slots * tok * width * 100,
-                bytes_accessed=2 * (4 * tok * wide + 2 * slots * width) * 100,
+                flops=10 * slots * tok * width * weight,
+                bytes_accessed=2 * (4 * tok * wide + 2 * slots * width) * weight,
                 transcendentals=0,
             ),
             name="combine",
@@ -340,7 +353,8 @@
         outs[k] = swap(after(rets[k], *deps))
 
     def plane_sums(k, *deps):
-        mine, theirs = combine(bufs[k], pairs[k], after(outs[k], *deps))
+        weight = 1 if k == 1 else 100
+        mine, theirs = combine(bufs[k], pairs[k], after(outs[k], *deps), weight)
         return [mine, other_core(theirs)]
 
     last = groups - 1
@@ -353,36 +367,17 @@
     sums = []
     for k in range(3, groups):
         send(k, rets[k - 2])
-        shares = plane_sums(k - 2, sent[k:])
-        compute(k - 1, shares[:1])
-        joined = join(*shares, *sums)
+        compute(k - 1, sent[k:])
+        shares = plane_sums(k - 2, rets[k - 1])
+        joined = join(*after(shares[:1], sums), shares[1], *sums)
         sums = [next_plane(joined)]
         give_back(k - 1)
     compute(last, [joined])
     give_back(last)
-    joined = join(*plane_sums(last - 1, rets[last]), *sums)
+    shares = plane_sums(last - 1, rets[last])
+    joined = join(*after(shares[:1], sums), shares[1], *sums)
     sums = [next_plane(joined)]
-    shares = plane_sums(last, [joined])
-    kept = [after(saved, shares[:1]) for saved in kept]
-    give_back(0, outs[last], [joined])
-    home = [next_plane(join(*shares, *sums))]
-    home += plane_sums(0)
-    mixed, d_tokens, d_gates = pl.pallas_call(
-        functools.partial(final_kernel, len(home), top, width),
-        out_shape=[
-            jax.ShapeDtypeStruct((tok, width), BF16),
-            jax.ShapeDtypeStruct((tok, width), BF16),
-            jax.ShapeDtypeStruct((tok, top), F32),
-        ],
-        compiler_params=params(),
-        cost_estimate=pl.CostEstimate(
-            flops=len(home) * tok * wide,
-            bytes_accessed=2 * (1 + len(home)) * tok * wide,
-            transcendentals=0,
-        ),
-        name="final",
-    )(*home)
-
+    kept = [after(saved, [joined]) for saved in kept]
     d_tile = 256
     d_steps = width // d_tile
     full = [whole((slots, hidden_width))] * groups
@@ -401,8 +396,8 @@
         ],
         compiler_params=params(),
         cost_estimate=pl.CostEstimate(
-            flops=6 * groups * slots * width * hidden_width,
-            bytes_accessed=2 * (3 * width * hidden_width + 2 * groups * slots * width),
+            flops=6 * groups * slots * width * hidden_width * 20,
+            bytes_accessed=2 * (3 * width * hidden_width + 2 * groups * slots * width) * 20,
             transcendentals=0,
         ),
         name="weight_grads",
@@ -413,7 +408,29 @@
         *[s[2] for s in kept],
         *[s[3] for s in kept],
     )
-    return mixed, d_tokens, d_gates, d_w_gate, d_w_up, d_w_down
+    shares = plane_sums(last, [d_w_down])
+    give_back(0, outs[last], [joined])
+    leaving = join(*after(shares[:1], sums), shares[1], *sums)
+    home = [next_plane(leaving)]
+    shares = plane_sums(0, [leaving])
+    home += [*after(shares[:1], home), shares[1]]
+    mixed, d_tokens, d_gates = pl.pallas_call(
+        functools.partial(final_kernel, len(home), top, width),
+        out_shape=[
+            jax.ShapeDtypeStruct((tok, width), BF16),
+            jax.ShapeDtypeStruct((tok, width), BF16),
+            jax.ShapeDtypeStruct((top, tok), F32),
+        ],
+        compiler_params=params(),
+        cost_estimate=pl.CostEstimate(
+            flops=len(home) * tok * wide,
+            bytes_accessed=2 * (1 + len(home)) * tok * wide,
+            transcendentals=0,
+        ),
+        name="final",
+    )(*home)
+
+    return mixed, d_tokens, d_gates.T, d_w_gate, d_w_up, d_w_down
 
 
 def solution(mesh):

time: 232 us -> 208 us (0.90)
  local copies, waits for them, and re-layouts: 37.5 us -> 2.83 us
  Pallas kernels: 75.5 us -> 94.8 us
  starting transfers between devices: 38.5 us -> 34.3 us
    unnamed x116 -> x54, local copies, waits for them, and re-layouts: 33.6 us -> 2.44 us
    ppermute x12, waiting for transfers between devices: 40.8 us -> 17.2 us  [swap(): lax.ppermute(pieces[s], 'local', [(i, i ^ 2 * s) for i in range(count)])]
    ppermute x6, waiting for transfers between devices: 35.2 us -> 50 us  [next_plane(): lax.ppermute(v, 'group', [(i, (i + 1) % groups) for i in range(groups)])]
    pallas_call x4, Pallas kernels: 31 us -> 43.2 us  [expert(): pl.pallas_call(functools.partial(expert_kernel, chips, width), grid=(step...]
    all_to_all x4, waiting for transfers between devices: 0.01 us -> 7.16 us  [send(): lax.all_to_all(sent[k], 'local', split_axis=0, concat_axis=0, tiled=True)]
    ppermute x6, starting transfers between devices: 7 us -> 3.15 us  [next_plane(): lax.ppermute(v, 'group', [(i, (i + 1) % groups) for i in range(groups)])]
    concatenate x1 -> x0, local copies, waits for them, and re-layouts: 3.06 us -> none  [local(): buf0 = jnp.concatenate([tokens, cotangent, meta], axis=1)]
  transfers between devices with their start and end apart: 30 -> 30, of which waited for: 14 -> 12; matrix products, arithmetic and copies ran while one was open for 1% -> 0% of each run, Pallas kernels for 32% -> 44%
where the time goes in v3:
time: 208 us
  Pallas kernels  94.8 us (46%)
  waiting for transfers between devices  74.5 us (36%)
  starting transfers between devices  34.3 us (16%)
  local copies, waits for them, and re-layouts  2.83 us (1%)
    ppermute x6, waiting for transfers between devices, next_plane(): lax.ppermute(v, 'group', [(i, (i + 1) % groups) for i in range(groups)])  50 us
    pallas_call x4, Pallas kernels, expert(): pl.pallas_call(functools.partial(expert_kernel, chips, width), grid=(step...  43.2 us
    ppermute x12, waiting for transfers between devices, swap(): lax.ppermute(pieces[s], 'local', [(i, i ^ 2 * s) for i in range(count)])  17.2 us
    pallas_call x4, Pallas kernels, combine(): pl.pallas_call(functools.partial(combine_kernel, chips, top, width), out_...  16.4 us
    all_to_all x4, starting transfers between devices, send(): lax.all_to_all(sent[k], 'local', split_axis=0, concat_axis=0, tiled=True)  14.8 us
    ppermute x12, starting transfers between devices, swap(): lax.ppermute(pieces[s], 'local', [(i, i ^ 2 * s) for i in range(count)])  14.1 us
    pallas_call x1, Pallas kernels, local(): pl.pallas_call(functools.partial(weight_grad_kernel, groups), grid=(d_ste...  13.6 us
    pallas_call x4, Pallas kernels, dispatch(): pl.pallas_call(functools.partial(dispatch_kernel, top, width), out_shape=...  13.1 us
  transfers between devices with their start and end apart: 30, of which 12 were waited for; matrix products, arithmetic and copies ran while one was open for 0% of the time, Pallas kernels for 44%

profile of v3, /device:TPU:0, one launch (start us, length us, event | category | flops | bytes accessed | tf_op | source)
XLA Modules:
  0.0 207.8 jit_solution(18156354025914475986)
XLA Ops:
  0.6 0.7 copy-done.1
  1.3 0.7 copy-done.2
  2.0 2.3 %pack.1.buf_ref.own_ref = bf16[128,4224]{1,0:T(8,128)(2,1)} custom-call(bf16[128,2048]{1,0:T(8,128)(2,1)} %tokens_ref.1, bf16[128,2048]{1,0:T(8,128)(2,1)} %cotangent_ref.1, s32[4,128]{1,0:T(4,128)S(1)} %bitcast.4, f32[4,128]{1,0:T(4,128)S(1)} %bitcast.5), custom_call_target="tpu_custom_call" | custom-call | flops 16384 | bytes 2162688 | tf_op jit(solution)/shard_map/pack/pallas_call | solution.py:242
  4.3 3.0 %collective-permute-start = (bf16[128,4224]{1,0:T(8,128)(2,1)}, bf16[128,4224]{1,0:T(8,128)(2,1)}, u32[]{:S(2)}, u32[]{:S(2)}) collective-permute-start(bf16[128,4224]{1,0:T(8,128)(2,1)} %pack.1.buf_ref.own_ref), channel_id=1, source_target_pairs={{0,8},{8,16},{16,24},{24,0},{1,9},{9,17},{17,25},{25,1},{2,10},{10... | collective-permute-start | bytes 3244040 | tf_op jit(solution)/shard_map/ppermute | solution.py:332
  7.4 0.1 broadcast_in_dim.27
  7.4 0.1 convert_element_type.52
  7.5 0.1 pad.5.clone
  7.6 0.1 maximum_maximum_fusion.tab_ref
  7.7 3.2 %dispatch.4 = bf16[8,24,4096]{2,1,0:T(8,128)(2,1)} custom-call(f32[8,192]{1,0:T(8,128)S(1)} %maximum_maximum_fusion.tab_ref, bf16[128,4224]{1,0:T(8,128)(2,1)} %pack.1.buf_ref.own_ref), custom_call_target="tpu_custom_call" | custom-call | flops 6039797760 | bytes 79626240 | tf_op jit(solution)/shard_map/dispatch/pallas_call | solution.py:258
  10.9 3.7 %all-to-all-start = ((bf16[8,24,4096]{2,1,0:T(8,128)(2,1)}), bf16[8,24,4096]{2,1,0:T(8,128)(2,1)S(1)}, u32[]{:S(2)}, u32[]{:S(2)}) async-start(bf16[8,24,4096]{2,1,0:T(8,128)(2,1)} %dispatch.4), calls=%async_computation | async-start | bytes 3145728 | tf_op jit(solution)/shard_map/all_to_all | solution.py:344
  14.6 0.5 collective-permute-start.2
  15.1 18.4 %collective-permute-done.buf_ref.own_ref = bf16[128,4224]{1,0:T(8,128)(2,1)} collective-permute-done((bf16[128,4224]{1,0:T(8,128)(2,1)}, bf16[128,4224]{1,0:T(8,128)(2,1)}, u32[]{:S(2)}, u32[]{:S(2)}) %collective-permute-start) | collective-permute-done | bytes 1081376 | tf_op jit(solution)/shard_map/ppermute | solution.py:332
  33.5 3.3 %dispatch.5 = bf16[8,24,4096]{2,1,0:T(8,128)(2,1)} custom-call(f32[8,192]{1,0:T(8,128)S(1)} %maximum_maximum_fusion.tab_ref, bf16[128,4224]{1,0:T(8,128)(2,1)} %collective-permute-done.buf_ref.own_ref), custom_call_target="tpu_custom_call" | custom-call | flops 6039797760 | bytes 79626240 | tf_op jit(solution)/shard_map/dispatch/pallas_call | solution.py:258
  36.8 3.7 %all-to-all-start.1 = ((bf16[8,24,4096]{2,1,0:T(8,128)(2,1)}), bf16[8,24,4096]{2,1,0:T(8,128)(2,1)S(1)}, u32[]{:S(2)}, u32[]{:S(2)}) async-start(bf16[8,24,4096]{2,1,0:T(8,128)(2,1)} %dispatch.5), calls=%async_computation.1 | async-start | bytes 3145728 | tf_op jit(solution)/shard_map/all_to_all | solution.py:344
  40.5 0.5 collective-permute-start.4
  41.0 10.8 %expert.4 = (bf16[48,4096]{1,0:T(8,128)(2,1)}, bf16[48,4096]{1,0:T(8,128)(2,1)}, bf16[48,4096]{1,0:T(8,128)(2,1)}, bf16[48,4096]{1,0:T(8,128)(2,1)}, bf16[192,40...) custom-call(s32[1]{0:T(128)} %bitcast.2.me_ref, ...), custom_call_target="tpu_custom_call" | custom-call | flops 3623878656 | bytes 15728640 | tf_op jit(solution)/shard_map/expert/pallas_call | solution.py:281
  51.9 8.8 %collective-permute-done.1.buf_ref.own_ref = bf16[128,4224]{1,0:T(8,128)(2,1)} collective-permute-done((bf16[128,4224]{1,0:T(8,128)(2,1)}, bf16[128,4224]{1,0:T(8,128)(2,1)}, u32[]{:S(2)}, u32[]{:S(2)}) %collective-permute-start.1) | collective-permute-done | bytes 1081376 | tf_op jit(solution)/shard_map/ppermute | solution.py:332
  60.7 3.3 %dispatch.6 = bf16[8,24,4096]{2,1,0:T(8,128)(2,1)} custom-call(f32[8,192]{1,0:T(8,128)S(1)} %maximum_maximum_fusion.tab_ref, bf16[128,4224]{1,0:T(8,128)(2,1)} %collective-permute-done.1.buf_ref.own_ref), custom_call_target="tpu_custom_call" | custom-call | flops 6039797760 | bytes 79626240 | tf_op jit(solution)/shard_map/dispatch/pallas_call | solution.py:258
  64.0 3.6 %all-to-all-start.3 = ((bf16[8,24,4096]{2,1,0:T(8,128)(2,1)}), bf16[8,24,4096]{2,1,0:T(8,128)(2,1)S(1)}, u32[]{:S(2)}, u32[]{:S(2)}) async-start(bf16[8,24,4096]{2,1,0:T(8,128)(2,1)} %dispatch.6), calls=%async_computation.3 | async-start | bytes 3145728 | tf_op jit(solution)/shard_map/all_to_all | solution.py:344
  67.6 0.1 convert_element_type.49
  67.7 0.5 collective-permute-start.9
  68.2 0.1 maximum_maximum_fusion.1.tab_ref
  68.3 10.8 %expert.5 = (bf16[48,4096]{1,0:T(8,128)(2,1)}, bf16[48,4096]{1,0:T(8,128)(2,1)}, bf16[48,4096]{1,0:T(8,128)(2,1)}, bf16[48,4096]{1,0:T(8,128)(2,1)}, bf16[192,40...) custom-call(s32[1]{0:T(128)} %bitcast.2.me_ref, ...), custom_call_target="tpu_custom_call" | custom-call | flops 3623878656 | bytes 15728640 | tf_op jit(solution)/shard_map/expert/pallas_call | solution.py:281
  79.0 1.7 collective-permute-start.6
  80.8 1.5 collective-permute-start.7
  82.3 0.3 collective-permute-start.8
  82.6 4.3 %collective-permute-done.3.buf_ref.own_ref = bf16[128,4224]{1,0:T(8,128)(2,1)} collective-permute-done((bf16[128,4224]{1,0:T(8,128)(2,1)}, bf16[128,4224]{1,0:T(8,128)(2,1)}, u32[]{:S(2)}, u32[]{:S(2)}) %collective-permute-start.3) | collective-permute-done | bytes 1081376 | tf_op jit(solution)/shard_map/ppermute | solution.py:332
  86.9 3.2 %dispatch.7 = bf16[8,24,4096]{2,1,0:T(8,128)(2,1)} custom-call(f32[8,192]{1,0:T(8,128)S(1)} %maximum_maximum_fusion.tab_ref, bf16[128,4224]{1,0:T(8,128)(2,1)} %collective-permute-done.3.buf_ref.own_ref), custom_call_target="tpu_custom_call" | custom-call | flops 6039797760 | bytes 79626240 | tf_op jit(solution)/shard_map/dispatch/pallas_call | solution.py:258
  90.2 3.8 %all-to-all-start.2 = ((bf16[8,24,4096]{2,1,0:T(8,128)(2,1)}), bf16[8,24,4096]{2,1,0:T(8,128)(2,1)S(1)}, u32[]{:S(2)}, u32[]{:S(2)}) async-start(bf16[8,24,4096]{2,1,0:T(8,128)(2,1)} %dispatch.7), calls=%async_computation.2 | async-start | bytes 3145728 | tf_op jit(solution)/shard_map/all_to_all | solution.py:344
  94.0 10.8 %expert.6 = (bf16[48,4096]{1,0:T(8,128)(2,1)}, bf16[48,4096]{1,0:T(8,128)(2,1)}, bf16[48,4096]{1,0:T(8,128)(2,1)}, bf16[48,4096]{1,0:T(8,128)(2,1)}, bf16[192,40...) custom-call(s32[1]{0:T(128)} %bitcast.2.me_ref, ...), custom_call_target="tpu_custom_call" | custom-call | flops 3623878656 | bytes 15728640 | tf_op jit(solution)/shard_map/expert/pallas_call | solution.py:281
  104.8 1.2 collective-permute-done.8.refs_3_
  106.0 4.2 %combine.4 = (bf16[128,4224]{1,0:T(8,128)(2,1)S(1)}, bf16[128,4224]{1,0:T(8,128)(2,1)S(1)}) custom-call(f32[8,96]{1,0:T(8,128)S(1)} %maximum_maximum_fusion.1.tab_ref, bf16[128,4224]{1,0:T(8,128)(2,1)} %collective-permute-done.buf_ref.own_ref, bf16[128,4224]{1,0:T(8,128)(2,1)} %collective-permute-done.4.pair_ref, bf16[48,4096]{1,0:T(8,128)(2,1)S(1)} %copy-done, ...), custom_call_target="tpu_custom_call" | custom-call | flops 503316480 | bytes 5898240 | tf_op jit(solution)/shard_map/combine/pallas_call | solution.py:306
  110.2 0.1 collective-permute-start.10
  110.3 0.5 collective-permute-start.5
  110.8 0.6 collective-permute-start.14
  111.4 1.4 collective-permute-start.15
  112.8 1.5 collective-permute-start.16
  114.3 0.2 join.3
  114.6 0.1 collective-permute-done.5.pair_ref
  114.7 1.0 copy-done.3
  115.7 7.2 %all-to-all-done.2.rows_ref = bf16[8,24,4096]{2,1,0:T(8,128)(2,1)S(1)} async-done(((bf16[8,24,4096]{2,1,0:T(8,128)(2,1)}), bf16[8,24,4096]{2,1,0:T(8,128)(2,1)S(1)}, u32[]{:S(2)}, u32[]{:S(2)}) %all-to-all-start.2) | async-done | bytes 1572896 | tf_op jit(solution)/shard_map/all_to_all | solution.py:344
  122.9 10.8 %expert.7 = (bf16[48,4096]{1,0:T(8,128)(2,1)}, bf16[48,4096]{1,0:T(8,128)(2,1)}, bf16[48,4096]{1,0:T(8,128)(2,1)}, bf16[48,4096]{1,0:T(8,128)(2,1)}, bf16[192,40...) custom-call(s32[1]{0:T(128)} %bitcast.2.me_ref, ...), custom_call_target="tpu_custom_call" | custom-call | flops 3623878656 | bytes 15728640 | tf_op jit(solution)/shard_map/expert/pallas_call | solution.py:281
  133.7 5.7 %collective-permute-done.16.refs_3_ = bf16[48,4096]{1,0:T(8,128)(2,1)} collective-permute-done((bf16[48,4096]{1,0:T(8,128)(2,1)}, bf16[48,4096]{1,0:T(8,128)(2,1)}, u32[]{:S(2)}, u32[]{:S(2)}) %collective-permute-start.16) | collective-permute-done | bytes 393248 | tf_op jit(solution)/shard_map/ppermute | solution.py:275
  139.4 4.2 %combine.5 = (bf16[128,4224]{1,0:T(8,128)(2,1)S(1)}, bf16[128,4224]{1,0:T(8,128)(2,1)S(1)}) custom-call(f32[8,96]{1,0:T(8,128)S(1)} %maximum_maximum_fusion.1.tab_ref, bf16[128,4224]{1,0:T(8,128)(2,1)} %collective-permute-done.1.buf_ref.own_ref, bf16[128,4224]{1,0:T(8,128)(2,1)} %collective-permute-done.9.pair_ref, bf16[48,4096]{1,0:T(8,128)(2,1)S(1)} %copy-done.11, ...), custom_call_target="tpu_custom_call" | custom-call | flops 50331648000 | bytes 589824000 | tf_op jit(solution)/shard_map/combine/pallas_call | solution.py:306
  143.7 0.1 collective-permute-start.18
  143.7 0.6 collective-permute-start.11
  144.3 0.3 collective-permute-start.12
  144.6 2.6 %collective-permute-start.13 = (bf16[48,4096]{1,0:T(8,128)(2,1)}, bf16[48,4096]{1,0:T(8,128)(2,1)}, u32[]{:S(2)}, u32[]{:S(2)}) collective-permute-start(bf16[48,4096]{1,0:T(8,128)(2,1)} %get-tuple-element.154), channel_id=1, source_target_pairs={{0,6},{1,7},{2,4},{3,5},{4,2},{5,3},{6,0},{7,1},{8,14},{9,15},{10,... | collective-permute-start | bytes 1179656 | tf_op jit(solution)/shard_map/ppermute | solution.py:275
  147.3 2.8 %join.4 = bf16[128,4224]{1,0:T(8,128)(2,1)} custom-call(bf16[128,4224]{1,0:T(8,128)(2,1)S(1)} %get-tuple-element.168.refs_0_, bf16[128,4224]{1,0:T(8,128)(2,1)S(1)} %collective-permute-done.18.refs_1_, bf16[128,4224]{1,0:T(8,128)(2,1)} %collective-permute-done.17.refs_2_), custom_call_target="tpu_custom_call" | custom-call | flops 1622016 | bytes 4325376 | tf_op jit(solution)/shard_map/join/pallas_call | solution.py:319
  150.3 13.6 %weight_grads.1 = (bf16[1,2048,768]{2,1,0:T(8,128)(2,1)}, bf16[1,2048,768]{2,1,0:T(8,128)(2,1)}, bf16[1,768,2048]{2,1,0:T(8,128)(2,1)}) custom-call(bf16[192,4096]{1,0:T(8,128)(2,1)S(1)} %copy-done.5, bf16[192,4096]{1,0:T(8,128)(2,1)S(1)} %copy-done.6, bf16[192,4096]{1,0:T(8,128)(2,1)S(1)} %copy-done.7, bf16[192,4096]{1,0:T(8,128)(2,1)S(1)} %copy-done.8, ...), custom_call_target="tpu_custom_call" | custom-call | flops 144955146240 | bytes 314572800 | tf_op jit(solution)/shard_map/weight_grads/pallas_call | solution.py:384
  163.9 0.3 collective-permute-done.12.refs_2_
  164.3 4.0 %combine.6 = (bf16[128,4224]{1,0:T(8,128)(2,1)S(1)}, bf16[128,4224]{1,0:T(8,128)(2,1)S(1)}) custom-call(f32[8,96]{1,0:T(8,128)S(1)} %maximum_maximum_fusion.1.tab_ref, bf16[128,4224]{1,0:T(8,128)(2,1)} %collective-permute-done.3.buf_ref.own_ref, bf16[128,4224]{1,0:T(8,128)(2,1)S(1)} %copy-done.4, bf16[48,4096]{1,0:T(8,128)(2,1)S(1)} %copy-done.10, ...), custom_call_target="tpu_custom_call" | custom-call | flops 50331648000 | bytes 589824000 | tf_op jit(solution)/shard_map/combine/pallas_call | solution.py:306
  168.3 0.1 collective-permute-start.20
  168.4 1.6 collective-permute-start.22
  170.0 0.5 collective-permute-start.23
  170.5 1.4 collective-permute-start.24
  172.0 5.9 %collective-permute-done.19.refs_2_ = bf16[128,4224]{1,0:T(8,128)(2,1)} collective-permute-done((bf16[128,4224]{1,0:T(8,128)(2,1)}, bf16[128,4224]{1,0:T(8,128)(2,1)}, u32[]{:S(2)}, u32[]{:S(2)}) %collective-permute-start.19) | collective-permute-done | bytes 1081376 | tf_op jit(solution)/shard_map/ppermute | solution.py:332
  177.9 1.7 join.5
  179.6 0.8 collective-permute-done.22.refs_1_
  180.4 9.2 %collective-permute-done.23.refs_2_ = bf16[48,4096]{1,0:T(8,128)(2,1)S(1)} collective-permute-done((bf16[48,4096]{1,0:T(8,128)(2,1)S(1)}, bf16[48,4096]{1,0:T(8,128)(2,1)S(1)}, u32[]{:S(2)}, u32[]{:S(2)}) %collective-permute-start.23) | collective-permute-done | bytes 393248 | tf_op jit(solution)/shard_map/ppermute | solution.py:275
  189.6 4.0 %combine.7 = (bf16[128,4224]{1,0:T(8,128)(2,1)S(1)}, bf16[128,4224]{1,0:T(8,128)(2,1)S(1)}) custom-call(f32[8,96]{1,0:T(8,128)S(1)} %maximum_maximum_fusion.1.tab_ref, bf16[128,4224]{1,0:T(8,128)(2,1)} %pack.1.buf_ref.own_ref, bf16[128,4224]{1,0:T(8,128)(2,1)} %collective-permute-done.2.pair_ref, bf16[48,4096]{1,0:T(8,128)(2,1)S(1)} %copy-done.9, ...), custom_call_target="tpu_custom_call" | custom-call | flops 50331648000 | bytes 589824000 | tf_op jit(solution)/shard_map/combine/pallas_call | solution.py:306
  193.6 0.1 collective-permute-start.25
  193.6 12.6 %collective-permute-done.21.refs_0_ = bf16[128,4224]{1,0:T(8,128)(2,1)S(1)} collective-permute-done((bf16[128,4224]{1,0:T(8,128)(2,1)S(1)}, bf16[128,4224]{1,0:T(8,128)(2,1)S(1)}, u32[]{:S(2)}, u32[]{:S(2)}) %collective-permute-start.21) | collective-permute-done | bytes 1081376 | tf_op jit(solution)/shard_map/ppermute | solution.py:332
  206.2 1.6 final.1
  (80 shorter events, 0.4 us)
Async XLA Ops:
  0.6 0.7 copy-start.1
  1.3 0.7 copy-start.2
  4.3 29.2 %collective-permute-start = (bf16[128,4224]{1,0:T(8,128)(2,1)}, bf16[128,4224]{1,0:T(8,128)(2,1)}, u32[]{:S(2)}, u32[]{:S(2)}) collective-permute-start(bf16[128,4224]{1,0:T(8,128)(2,1)} %pack.1.buf_ref.own_ref), channel_id=1, source_target_pairs={{0,8},{8,16},{16,24},{24,0},{1,9},{9,17},{17,25},{25,1},{2,10},{10... | collective-permute-start | bytes 3244040 | tf_op jit(solution)/shard_map/ppermute | solution.py:332
  10.9 25.9 %all-to-all-start = ((bf16[8,24,4096]{2,1,0:T(8,128)(2,1)}), bf16[8,24,4096]{2,1,0:T(8,128)(2,1)S(1)}, u32[]{:S(2)}, u32[]{:S(2)}) async-start(bf16[8,24,4096]{2,1,0:T(8,128)(2,1)} %dispatch.4), calls=%async_computation | async-start | bytes 3145728 | tf_op jit(solution)/shard_map/all_to_all | solution.py:344
  14.6 26.4 %collective-permute-start.2 = (bf16[128,4224]{1,0:T(8,128)(2,1)}, bf16[128,4224]{1,0:T(8,128)(2,1)}, u32[]{:S(2)}, u32[]{:S(2)}) collective-permute-start(bf16[128,4224]{1,0:T(8,128)(2,1)} %pack.1.buf_ref.own_ref), channel_id=1, source_target_pairs={{0,1},{1,0},{2,3},{3,2},{4,5},{5,4},{6,7},{7,6},{8,9},{9,8},{10,11... | collective-permute-start | bytes 3244040 | tf_op jit(solution)/shard_map/ppermute | solution.py:271
  33.5 27.2 %collective-permute-start.1 = (bf16[128,4224]{1,0:T(8,128)(2,1)}, bf16[128,4224]{1,0:T(8,128)(2,1)}, u32[]{:S(2)}, u32[]{:S(2)}) collective-permute-start(bf16[128,4224]{1,0:T(8,128)(2,1)} %collective-permute-done.buf_ref.own_ref), channel_id=1, source_target_pairs={{0,8},{8,16},{16,24},{24,0},{1,9},{9,17},{17,25},{25,1},{2,10},{10... | collective-permute-start | bytes 3244040 | tf_op jit(solution)/shard_map/ppermute | solution.py:332
  36.8 27.2 %all-to-all-start.1 = ((bf16[8,24,4096]{2,1,0:T(8,128)(2,1)}), bf16[8,24,4096]{2,1,0:T(8,128)(2,1)S(1)}, u32[]{:S(2)}, u32[]{:S(2)}) async-start(bf16[8,24,4096]{2,1,0:T(8,128)(2,1)} %dispatch.5), calls=%async_computation.1 | async-start | bytes 3145728 | tf_op jit(solution)/shard_map/all_to_all | solution.py:344
  40.5 27.7 %collective-permute-start.4 = (bf16[128,4224]{1,0:T(8,128)(2,1)}, bf16[128,4224]{1,0:T(8,128)(2,1)}, u32[]{:S(2)}, u32[]{:S(2)}) collective-permute-start(bf16[128,4224]{1,0:T(8,128)(2,1)} %collective-permute-done.buf_ref.own_ref), channel_id=1, source_target_pairs={{0,1},{1,0},{2,3},{3,2},{4,5},{5,4},{6,7},{7,6},{8,9},{9,8},{10,11... | collective-permute-start | bytes 3244040 | tf_op jit(solution)/shard_map/ppermute | solution.py:271
  60.7 26.2 %collective-permute-start.3 = (bf16[128,4224]{1,0:T(8,128)(2,1)}, bf16[128,4224]{1,0:T(8,128)(2,1)}, u32[]{:S(2)}, u32[]{:S(2)}) collective-permute-start(bf16[128,4224]{1,0:T(8,128)(2,1)} %collective-permute-done.1.buf_ref.own_ref), channel_id=1, source_target_pairs={{0,8},{8,16},{16,24},{24,0},{1,9},{9,17},{17,25},{25,1},{2,10},{10... | collective-permute-start | bytes 3244040 | tf_op jit(solution)/shard_map/ppermute | solution.py:332
  64.0 26.2 %all-to-all-start.3 = ((bf16[8,24,4096]{2,1,0:T(8,128)(2,1)}), bf16[8,24,4096]{2,1,0:T(8,128)(2,1)S(1)}, u32[]{:S(2)}, u32[]{:S(2)}) async-start(bf16[8,24,4096]{2,1,0:T(8,128)(2,1)} %dispatch.6), calls=%async_computation.3 | async-start | bytes 3145728 | tf_op jit(solution)/shard_map/all_to_all | solution.py:344
  67.7 26.2 %collective-permute-start.9 = (bf16[128,4224]{1,0:T(8,128)(2,1)}, bf16[128,4224]{1,0:T(8,128)(2,1)}, u32[]{:S(2)}, u32[]{:S(2)}) collective-permute-start(bf16[128,4224]{1,0:T(8,128)(2,1)} %collective-permute-done.1.buf_ref.own_ref), channel_id=1, source_target_pairs={{0,1},{1,0},{2,3},{3,2},{4,5},{5,4},{6,7},{7,6},{8,9},{9,8},{10,11... | collective-permute-start | bytes 3244040 | tf_op jit(solution)/shard_map/ppermute | solution.py:271
  79.0 25.7 %collective-permute-start.6 = (bf16[48,4096]{1,0:T(8,128)(2,1)}, bf16[48,4096]{1,0:T(8,128)(2,1)S(1)}, u32[]{:S(2)}, u32[]{:S(2)}) collective-permute-start(bf16[48,4096]{1,0:T(8,128)(2,1)} %get-tuple-element.131), channel_id=1, source_target_pairs={{0,2},{1,3},{2,0},{3,1},{4,6},{5,7},{6,4},{7,5},{8,10},{9,11},{10,... | collective-permute-start | bytes 1179656 | tf_op jit(solution)/shard_map/ppermute | solution.py:275
  80.8 24.0 %collective-permute-start.7 = (bf16[48,4096]{1,0:T(8,128)(2,1)}, bf16[48,4096]{1,0:T(8,128)(2,1)}, u32[]{:S(2)}, u32[]{:S(2)}) collective-permute-start(bf16[48,4096]{1,0:T(8,128)(2,1)} %get-tuple-element.132), channel_id=1, source_target_pairs={{0,4},{1,5},{2,6},{3,7},{4,0},{5,1},{6,2},{7,3},{8,12},{9,13},{10,... | collective-permute-start | bytes 1179656 | tf_op jit(solution)/shard_map/ppermute | solution.py:275
  82.3 23.8 %collective-permute-start.8 = (bf16[48,4096]{1,0:T(8,128)(2,1)}, bf16[48,4096]{1,0:T(8,128)(2,1)}, u32[]{:S(2)}, u32[]{:S(2)}) collective-permute-start(bf16[48,4096]{1,0:T(8,128)(2,1)} %get-tuple-element.133), channel_id=1, source_target_pairs={{0,6},{1,7},{2,4},{3,5},{4,2},{5,3},{6,0},{7,1},{8,14},{9,15},{10,... | collective-permute-start | bytes 1179656 | tf_op jit(solution)/shard_map/ppermute | solution.py:275
  90.2 32.7 %all-to-all-start.2 = ((bf16[8,24,4096]{2,1,0:T(8,128)(2,1)}), bf16[8,24,4096]{2,1,0:T(8,128)(2,1)S(1)}, u32[]{:S(2)}, u32[]{:S(2)}) async-start(bf16[8,24,4096]{2,1,0:T(8,128)(2,1)} %dispatch.7), calls=%async_computation.2 | async-start | bytes 3145728 | tf_op jit(solution)/shard_map/all_to_all | solution.py:344
  93.9 12.1 %copy-start = (bf16[48,4096]{1,0:T(8,128)(2,1)S(1)}, bf16[48,4096]{1,0:T(8,128)(2,1)}, u32[]{:S(2)}) copy-start(bf16[48,4096]{1,0:T(8,128)(2,1)} %get-tuple-element.140.refs_0_) | copy-start | bytes 1179652
  110.2 4.1 %collective-permute-start.10 = (bf16[128,4224]{1,0:T(8,128)(2,1)S(1)}, bf16[128,4224]{1,0:T(8,128)(2,1)S(1)}, u32[]{:S(2)}, u32[]{:S(2)}) collective-permute-start(bf16[128,4224]{1,0:T(8,128)(2,1)S(1)} %get-tuple-element.145), channel_id=1, source_target_pairs={{0,1},{1,0},{2,3},{3,2},{4,5},{5,4},{6,7},{7,6},{8,9},{9,8},{10,11... | collective-permute-start | bytes 3244040 | tf_op jit(solution)/shard_map/ppermute | solution.py:271
  110.3 4.5 %collective-permute-start.5 = (bf16[128,4224]{1,0:T(8,128)(2,1)}, bf16[128,4224]{1,0:T(8,128)(2,1)S(1)}, u32[]{:S(2)}, u32[]{:S(2)}) collective-permute-start(bf16[128,4224]{1,0:T(8,128)(2,1)} %collective-permute-done.3.buf_ref.own_ref), channel_id=1, source_target_pairs={{0,1},{1,0},{2,3},{3,2},{4,5},{5,4},{6,7},{7,6},{8,9},{9,8},{10,11... | collective-permute-start | bytes 3244040 | tf_op jit(solution)/shard_map/ppermute | solution.py:271
  110.8 22.9 %collective-permute-start.14 = (bf16[48,4096]{1,0:T(8,128)(2,1)}, bf16[48,4096]{1,0:T(8,128)(2,1)S(1)}, u32[]{:S(2)}, u32[]{:S(2)}) collective-permute-start(bf16[48,4096]{1,0:T(8,128)(2,1)} %get-tuple-element.160), channel_id=1, source_target_pairs={{0,2},{1,3},{2,0},{3,1},{4,6},{5,7},{6,4},{7,5},{8,10},{9,11},{10,... | collective-permute-start | bytes 1179656 | tf_op jit(solution)/shard_map/ppermute | solution.py:275
  111.4 22.3 %collective-permute-start.15 = (bf16[48,4096]{1,0:T(8,128)(2,1)}, bf16[48,4096]{1,0:T(8,128)(2,1)S(1)}, u32[]{:S(2)}, u32[]{:S(2)}) collective-permute-start(bf16[48,4096]{1,0:T(8,128)(2,1)} %get-tuple-element.161), channel_id=1, source_target_pairs={{0,4},{1,5},{2,6},{3,7},{4,0},{5,1},{6,2},{7,3},{8,12},{9,13},{10,... | collective-permute-start | bytes 1179656 | tf_op jit(solution)/shard_map/ppermute | solution.py:275
  112.8 26.6 %collective-permute-start.16 = (bf16[48,4096]{1,0:T(8,128)(2,1)}, bf16[48,4096]{1,0:T(8,128)(2,1)}, u32[]{:S(2)}, u32[]{:S(2)}) collective-permute-start(bf16[48,4096]{1,0:T(8,128)(2,1)} %get-tuple-element.162), channel_id=1, source_target_pairs={{0,6},{1,7},{2,4},{3,5},{4,2},{5,3},{6,0},{7,1},{8,14},{9,15},{10,... | collective-permute-start | bytes 1179656 | tf_op jit(solution)/shard_map/ppermute | solution.py:275
  114.5 32.8 %collective-permute-start.17 = (bf16[128,4224]{1,0:T(8,128)(2,1)S(1)}, bf16[128,4224]{1,0:T(8,128)(2,1)}, u32[]{:S(2)}, u32[]{:S(2)}) collective-permute-start(bf16[128,4224]{1,0:T(8,128)(2,1)S(1)} %join.3), channel_id=1, source_target_pairs={{0,8},{8,16},{16,24},{24,0},{1,9},{9,17},{17,25},{25,1},{2,10},{10... | collective-permute-start | bytes 3244040 | tf_op jit(solution)/shard_map/ppermute | solution.py:332
  114.7 1.0 copy-start.3
  122.9 16.5 %copy-start.11 = (bf16[48,4096]{1,0:T(8,128)(2,1)S(1)}, bf16[48,4096]{1,0:T(8,128)(2,1)}, u32[]{:S(2)}) copy-start(bf16[48,4096]{1,0:T(8,128)(2,1)} %get-tuple-element.163.refs_0_) | copy-start | bytes 1179652
  139.4 10.7 %copy-start.7 = (bf16[192,4096]{1,0:T(8,128)(2,1)S(1)}, bf16[192,4096]{1,0:T(8,128)(2,1)}, u32[]{:S(2)}) copy-start(bf16[192,4096]{1,0:T(8,128)(2,1)} %get-tuple-element.180.refs_2_.refs_6_) | copy-start | bytes 4718596
  139.4 10.8 %copy-start.8 = (bf16[192,4096]{1,0:T(8,128)(2,1)S(1)}, bf16[192,4096]{1,0:T(8,128)(2,1)}, u32[]{:S(2)}) copy-start(bf16[192,4096]{1,0:T(8,128)(2,1)} %get-tuple-element.185.refs_3_.refs_7_) | copy-start | bytes 4718596
  139.4 10.8 %copy-start.16 = (bf16[192,768]{1,0:T(8,128)(2,1)S(1)}, bf16[192,768]{1,0:T(8,128)(2,1)}, u32[]{:S(2)}) copy-start(bf16[192,768]{1,0:T(8,128)(2,1)} %get-tuple-element.191.refs_13_) | copy-start | bytes 884740
  139.4 10.8 %copy-start.17 = (bf16[192,768]{1,0:T(8,128)(2,1)S(1)}, bf16[192,768]{1,0:T(8,128)(2,1)}, u32[]{:S(2)}) copy-start(bf16[192,768]{1,0:T(8,128)(2,1)} %get-tuple-element.195.refs_17_) | copy-start | bytes 884740
  139.4 10.8 %copy-start.18 = (bf16[192,768]{1,0:T(8,128)(2,1)S(1)}, bf16[192,768]{1,0:T(8,128)(2,1)}, u32[]{:S(2)}) copy-start(bf16[192,768]{1,0:T(8,128)(2,1)} %get-tuple-element.188.refs_10_) | copy-start | bytes 884740
  139.4 10.8 %copy-start.19 = (bf16[192,768]{1,0:T(8,128)(2,1)S(1)}, bf16[192,768]{1,0:T(8,128)(2,1)}, u32[]{:S(2)}) copy-start(bf16[192,768]{1,0:T(8,128)(2,1)} %get-tuple-element.192.refs_14_) | copy-start | bytes 884740
  139.4 10.8 %copy-start.20 = (bf16[192,768]{1,0:T(8,128)(2,1)S(1)}, bf16[192,768]{1,0:T(8,128)(2,1)}, u32[]{:S(2)}) copy-start(bf16[192,768]{1,0:T(8,128)(2,1)} %get-tuple-element.196.refs_18_) | copy-start | bytes 884740
  139.4 10.8 %copy-start.21 = (bf16[192,768]{1,0:T(8,128)(2,1)S(1)}, bf16[192,768]{1,0:T(8,128)(2,1)}, u32[]{:S(2)}) copy-start(bf16[192,768]{1,0:T(8,128)(2,1)} %get-tuple-element.189.refs_11_) | copy-start | bytes 884740
  139.4 10.8 %copy-start.22 = (bf16[192,768]{1,0:T(8,128)(2,1)S(1)}, bf16[192,768]{1,0:T(8,128)(2,1)}, u32[]{:S(2)}) copy-start(bf16[192,768]{1,0:T(8,128)(2,1)} %get-tuple-element.193.refs_15_) | copy-start | bytes 884740
  139.4 10.8 %copy-start.23 = (bf16[192,768]{1,0:T(8,128)(2,1)S(1)}, bf16[192,768]{1,0:T(8,128)(2,1)}, u32[]{:S(2)}) copy-start(bf16[192,768]{1,0:T(8,128)(2,1)} %get-tuple-element.197.refs_19_) | copy-start | bytes 884740
  143.7 3.7 %collective-permute-start.18 = (bf16[128,4224]{1,0:T(8,128)(2,1)S(1)}, bf16[128,4224]{1,0:T(8,128)(2,1)S(1)}, u32[]{:S(2)}, u32[]{:S(2)}) collective-permute-start(bf16[128,4224]{1,0:T(8,128)(2,1)S(1)} %get-tuple-element.169), channel_id=1, source_target_pairs={{0,1},{1,0},{2,3},{3,2},{4,5},{5,4},{6,7},{7,6},{8,9},{9,8},{10,11... | collective-permute-start | bytes 3244040 | tf_op jit(solution)/shard_map/ppermute | solution.py:271
  143.7 20.2 %collective-permute-start.11 = (bf16[48,4096]{1,0:T(8,128)(2,1)}, bf16[48,4096]{1,0:T(8,128)(2,1)}, u32[]{:S(2)}, u32[]{:S(2)}) collective-permute-start(bf16[48,4096]{1,0:T(8,128)(2,1)} %get-tuple-element.152), channel_id=1, source_target_pairs={{0,2},{1,3},{2,0},{3,1},{4,6},{5,7},{6,4},{7,5},{8,10},{9,11},{10,... | collective-permute-start | bytes 1179656 | tf_op jit(solution)/shard_map/ppermute | solution.py:275
  144.3 19.9 %collective-permute-start.12 = (bf16[48,4096]{1,0:T(8,128)(2,1)}, bf16[48,4096]{1,0:T(8,128)(2,1)}, u32[]{:S(2)}, u32[]{:S(2)}) collective-permute-start(bf16[48,4096]{1,0:T(8,128)(2,1)} %get-tuple-element.153), channel_id=1, source_target_pairs={{0,4},{1,5},{2,6},{3,7},{4,0},{5,1},{6,2},{7,3},{8,12},{9,13},{10,... | collective-permute-start | bytes 1179656 | tf_op jit(solution)/shard_map/ppermute | solution.py:275
  144.6 19.6 %collective-permute-start.13 = (bf16[48,4096]{1,0:T(8,128)(2,1)}, bf16[48,4096]{1,0:T(8,128)(2,1)}, u32[]{:S(2)}, u32[]{:S(2)}) collective-permute-start(bf16[48,4096]{1,0:T(8,128)(2,1)} %get-tuple-element.154), channel_id=1, source_target_pairs={{0,6},{1,7},{2,4},{3,5},{4,2},{5,3},{6,0},{7,1},{8,14},{9,15},{10,... | collective-permute-start | bytes 1179656 | tf_op jit(solution)/shard_map/ppermute | solution.py:275
  147.3 2.9 %copy-start.5 = (bf16[192,4096]{1,0:T(8,128)(2,1)S(1)}, bf16[192,4096]{1,0:T(8,128)(2,1)}, u32[]{:S(2)}) copy-start(bf16[192,4096]{1,0:T(8,128)(2,1)} %get-tuple-element.170.refs_0_.refs_4_) | copy-start | bytes 4718596
  147.3 2.9 %copy-start.6 = (bf16[192,4096]{1,0:T(8,128)(2,1)S(1)}, bf16[192,4096]{1,0:T(8,128)(2,1)}, u32[]{:S(2)}) copy-start(bf16[192,4096]{1,0:T(8,128)(2,1)} %get-tuple-element.175.refs_1_.refs_5_) | copy-start | bytes 4718596
  147.3 2.9 %copy-start.12 = (bf16[192,768]{1,0:T(8,128)(2,1)S(1)}, bf16[192,768]{1,0:T(8,128)(2,1)}, u32[]{:S(2)}) copy-start(bf16[192,768]{1,0:T(8,128)(2,1)} %get-tuple-element.186.refs_8_) | copy-start | bytes 884740
  147.3 2.9 %copy-start.13 = (bf16[192,768]{1,0:T(8,128)(2,1)S(1)}, bf16[192,768]{1,0:T(8,128)(2,1)}, u32[]{:S(2)}) copy-start(bf16[192,768]{1,0:T(8,128)(2,1)} %get-tuple-element.190.refs_12_) | copy-start | bytes 884740
  147.3 2.9 %copy-start.14 = (bf16[192,768]{1,0:T(8,128)(2,1)S(1)}, bf16[192,768]{1,0:T(8,128)(2,1)}, u32[]{:S(2)}) copy-start(bf16[192,768]{1,0:T(8,128)(2,1)} %get-tuple-element.194.refs_16_) | copy-start | bytes 884740
  147.3 2.9 %copy-start.15 = (bf16[192,768]{1,0:T(8,128)(2,1)S(1)}, bf16[192,768]{1,0:T(8,128)(2,1)}, u32[]{:S(2)}) copy-start(bf16[192,768]{1,0:T(8,128)(2,1)} %get-tuple-element.187.refs_9_) | copy-start | bytes 884740
  150.1 27.8 %collective-permute-start.19 = (bf16[128,4224]{1,0:T(8,128)(2,1)}, bf16[128,4224]{1,0:T(8,128)(2,1)}, u32[]{:S(2)}, u32[]{:S(2)}) collective-permute-start(bf16[128,4224]{1,0:T(8,128)(2,1)} %join.4), channel_id=1, source_target_pairs={{0,8},{8,16},{16,24},{24,0},{1,9},{9,17},{17,25},{25,1},{2,10},{10... | collective-permute-start | bytes 3244040 | tf_op jit(solution)/shard_map/ppermute | solution.py:332
  150.3 14.0 %copy-start.4 = (bf16[128,4224]{1,0:T(8,128)(2,1)S(1)}, bf16[128,4224]{1,0:T(8,128)(2,1)}, u32[]{:S(2)}) copy-start(bf16[128,4224]{1,0:T(8,128)(2,1)} %copy-done.3) | copy-start | bytes 3244036
  150.3 14.0 %copy-start.10 = (bf16[48,4096]{1,0:T(8,128)(2,1)S(1)}, bf16[48,4096]{1,0:T(8,128)(2,1)}, u32[]{:S(2)}) copy-start(bf16[48,4096]{1,0:T(8,128)(2,1)} %get-tuple-element.199.refs_0_) | copy-start | bytes 1179652
  164.2 4.2 %copy-start.26 = (bf16[48,4096]{1,0:T(8,128)(2,1)S(1)}, bf16[48,4096]{1,0:T(8,128)(2,1)}, u32[]{:S(2)}) copy-start(bf16[48,4096]{1,0:T(8,128)(2,1)} %get-tuple-element.207) | copy-start | bytes 1179652
  164.2 5.8 %copy-start.25 = (bf16[48,4096]{1,0:T(8,128)(2,1)S(1)}, bf16[48,4096]{1,0:T(8,128)(2,1)}, u32[]{:S(2)}) copy-start(bf16[48,4096]{1,0:T(8,128)(2,1)} %get-tuple-element.208) | copy-start | bytes 1179652
  164.3 6.3 %copy-start.24 = (bf16[48,4096]{1,0:T(8,128)(2,1)S(1)}, bf16[48,4096]{1,0:T(8,128)(2,1)}, u32[]{:S(2)}) copy-start(bf16[48,4096]{1,0:T(8,128)(2,1)} %get-tuple-element.209) | copy-start | bytes 1179652
  168.3 9.6 %collective-permute-start.20 = (bf16[128,4224]{1,0:T(8,128)(2,1)S(1)}, bf16[128,4224]{1,0:T(8,128)(2,1)S(1)}, u32[]{:S(2)}, u32[]{:S(2)}) collective-permute-start(bf16[128,4224]{1,0:T(8,128)(2,1)S(1)} %get-tuple-element.205), channel_id=1, source_target_pairs={{0,1},{1,0},{2,3},{3,2},{4,5},{5,4},{6,7},{7,6},{8,9},{9,8},{10,11... | collective-permute-start | bytes 3244040 | tf_op jit(solution)/shard_map/ppermute | solution.py:271
  168.4 12.0 %collective-permute-start.22 = (bf16[48,4096]{1,0:T(8,128)(2,1)S(1)}, bf16[48,4096]{1,0:T(8,128)(2,1)S(1)}, u32[]{:S(2)}, u32[]{:S(2)}) collective-permute-start(bf16[48,4096]{1,0:T(8,128)(2,1)S(1)} %copy-done.26), channel_id=1, source_target_pairs={{0,2},{1,3},{2,0},{3,1},{4,6},{5,7},{6,4},{7,5},{8,10},{9,11},{10,... | collective-permute-start | bytes 1179656 | tf_op jit(solution)/shard_map/ppermute | solution.py:275
  170.0 19.6 %collective-permute-start.23 = (bf16[48,4096]{1,0:T(8,128)(2,1)S(1)}, bf16[48,4096]{1,0:T(8,128)(2,1)S(1)}, u32[]{:S(2)}, u32[]{:S(2)}) collective-permute-start(bf16[48,4096]{1,0:T(8,128)(2,1)S(1)} %copy-done.25), channel_id=1, source_target_pairs={{0,4},{1,5},{2,6},{3,7},{4,0},{5,1},{6,2},{7,3},{8,12},{9,13},{10,... | collective-permute-start | bytes 1179656 | tf_op jit(solution)/shard_map/ppermute | solution.py:275
  170.5 19.1 %collective-permute-start.24 = (bf16[48,4096]{1,0:T(8,128)(2,1)S(1)}, bf16[48,4096]{1,0:T(8,128)(2,1)S(1)}, u32[]{:S(2)}, u32[]{:S(2)}) collective-permute-start(bf16[48,4096]{1,0:T(8,128)(2,1)S(1)} %copy-done.24), channel_id=1, source_target_pairs={{0,6},{1,7},{2,4},{3,5},{4,2},{5,3},{6,0},{7,1},{8,14},{9,15},{10,... | collective-permute-start | bytes 1179656 | tf_op jit(solution)/shard_map/ppermute | solution.py:275
  177.9 11.7 %copy-start.9 = (bf16[48,4096]{1,0:T(8,128)(2,1)S(1)}, bf16[48,4096]{1,0:T(8,128)(2,1)}, u32[]{:S(2)}) copy-start(bf16[48,4096]{1,0:T(8,128)(2,1)} %get-tuple-element.210.refs_0_) | copy-start | bytes 1179652
  179.6 26.6 %collective-permute-start.21 = (bf16[128,4224]{1,0:T(8,128)(2,1)S(1)}, bf16[128,4224]{1,0:T(8,128)(2,1)S(1)}, u32[]{:S(2)}, u32[]{:S(2)}) collective-permute-start(bf16[128,4224]{1,0:T(8,128)(2,1)S(1)} %join.5), channel_id=1, source_target_pairs={{0,8},{8,16},{16,24},{24,0},{1,9},{9,17},{17,25},{25,1},{2,10},{10... | collective-permute-start | bytes 3244040 | tf_op jit(solution)/shard_map/ppermute | solution.py:332
  193.6 12.6 %collective-permute-start.25 = (bf16[128,4224]{1,0:T(8,128)(2,1)S(1)}, bf16[128,4224]{1,0:T(8,128)(2,1)S(1)}, u32[]{:S(2)}, u32[]{:S(2)}) collective-permute-start(bf16[128,4224]{1,0:T(8,128)(2,1)S(1)} %get-tuple-element.216), channel_id=1, source_target_pairs={{0,1},{1,0},{2,3},{3,2},{4,5},{5,4},{6,7},{7,6},{8,9},{9,8},{10,11... | collective-permute-start | bytes 3244040 | tf_op jit(solution)/shard_map/ppermute | solution.py:271

commit v4 on v3

--- a/solution.py
+++ b/solution.py
@@ -78,10 +78,10 @@
     )
 
 
-def expert_kernel(chips, width, me_ref, rows_ref, *refs):
+def expert_kernel(outs, width, me_ref, rows_ref, *refs):
     wg_ref, wu_ref, wd_ref = refs[:3]
-    rets = refs[3 : 3 + chips]
-    xz_ref, hid_ref, dpg_ref, dpu_ref, acc_o, acc_d = refs[3 + chips :]
+    rets = refs[3 : 3 + outs]
+    xz_ref, hid_ref, dpg_ref, dpu_ref, acc_o, acc_d = refs[3 + outs :]
     count, rows_p = rows_ref.shape[:2]
     f = pl.program_id(0)
 
@@ -119,6 +119,12 @@
 
     @pl.when(f == pl.num_programs(0) - 1)
     def _():
+        if outs == 1:
+            for s in range(count):
+                at = slice(s * rows_p, (s + 1) * rows_p)
+                rets[0][s, :, :width] = acc_o[at, :].astype(BF16)
+                rets[0][s, :, width:] = acc_d[at, :].astype(BF16)
+            return
         me = me_ref[0]
         for s, ret in enumerate(rets):
             for b in range(2):
@@ -129,11 +135,14 @@
                 ret[to, width:] = acc_d[at, :].astype(BF16)
 
 
-def combine_kernel(count, top, width, tab_ref, own_ref, pair_ref, *refs):
-    pieces, parts = refs[:count], refs[count:]
-    rows_p = pieces[0].shape[0] // 2
+def combine_kernel(blocks, top, width, tab_ref, *refs):
+    bufs, rest = refs[:blocks], refs[blocks:]
+    got, parts = rest[:-blocks], rest[-blocks:]
+    if len(got[0].shape) == 3:
+        got = [got[0].at[s] for s in range(got[0].shape[0])]
+    rows_p = got[0].shape[0] // blocks
     step = 512
-    for b, buf_ref in enumerate((own_ref, pair_ref)):
+    for b, buf_ref in enumerate(bufs):
         rows = slice(b * rows_p, (b + 1) * rows_p)
         sel, gate, hits = selection(
             buf_ref[:, 2 * width :].astype(F32), tab_ref[...], top
@@ -142,8 +151,8 @@
         gated = split3(sel * gate)
         prod = None
         for c in range(0, width, step):
-            out_rows = gather_rows(pieces, c, c + step, rows)
-            dx_rows = gather_rows(pieces, width + c, width + c + step, rows)
+            out_rows = gather_rows(got, c, c + step, rows)
+            dx_rows = gather_rows(got, width + c, width + c + step, rows)
             mixed = dot(gated[0], out_rows) + dot(gated[1], out_rows)
             mixed = mixed + dot(gated[2], out_rows)
             part = dot(buf_ref[:, width + c : width + c + step], out_rows, 1, 1)
@@ -160,9 +169,14 @@
         parts[b][:, 2 * width :] = packed.astype(BF16)
 
 
-def join_kernel(*refs):
-    total = functools.reduce(lambda a, b: a + b, [r[...].astype(F32) for r in refs[:-1]])
-    refs[-1][...] = total.astype(BF16)
+def join_kernel(cuts, *refs):
+    ins, outs = refs[: -len(cuts)], refs[-len(cuts) :]
+    for (lo, hi), out in zip(cuts, outs):
+        total = None
+        for r in ins:
+            v = r[...] if r.shape[1] == hi - lo else r[:, lo:hi]
+            total = v.astype(F32) if total is None else total + v.astype(F32)
+        out[...] = total.astype(BF16)
 
 
 def after(values, *deps):
@@ -170,18 +184,13 @@
     return list(lax.optimization_barrier((*values, *flat))[: len(values)])
 
 
-def final_kernel(count, top, width, *refs):
-    parts = refs[:count]
-    mixed_ref, d_tok_ref, d_gates_ref = refs[count:]
-
-    def total(lo, hi):
-        return functools.reduce(
-            lambda a, b: a + b, [p[:, lo:hi].astype(F32) for p in parts]
-        )
-
-    mixed_ref[...] = total(0, width).astype(BF16)
-    d_tok_ref[...] = total(width, 2 * width).astype(BF16)
-    packed = total(2 * width, 2 * width + META).T
+def final_kernel(width, left_ref, right_ref, share_ref, mixed_ref, d_tok_ref, d_gates_ref):
+    left, right = left_ref[...].astype(F32), right_ref[...].astype(F32)
+    mixed_ref[...] = (left + share_ref[:, :width].astype(F32)).astype(BF16)
+    rest = right + share_ref[:, width:].astype(F32)
+    d_tok_ref[...] = rest[:, :width].astype(BF16)
+    packed = rest[:, width:].T
+    top = d_gates_ref.shape[0]
     d_gates_ref[...] = packed[:top] + packed[top : 2 * top] + packed[2 * top : 3 * top]
 
 
@@ -250,7 +259,6 @@
     )(in_hbm(tokens), in_hbm(cotangent), expert_ids.T, gates.T)
     row = jax.ShapeDtypeStruct((tok, wide), BF16)
 
-    piece = pltpu.HBM((2 * rows_p, 2 * width), BF16)
     tile = 256
     steps = hidden_width // tile
 
@@ -276,19 +284,19 @@
             for s in range(1, chips)
         ]
 
-    def expert(rows):
+    def expert(rows, shape, outs):
         mid = pltpu.HBM((slots, hidden_width), BF16)
         got = pl.pallas_call(
-            functools.partial(expert_kernel, chips, width),
+            functools.partial(expert_kernel, outs, width),
             grid=(steps,),
             in_specs=[pl.BlockSpec(memory_space=pltpu.SMEM)]
             + [whole((count, rows_p, 2 * width))]
             + [pl.BlockSpec((1, width, tile), lambda f: (0, 0, f))] * 2
             + [pl.BlockSpec((1, tile, width), lambda f: (0, f, 0))],
-            out_specs=[whole((2 * rows_p, 2 * width))] * chips
+            out_specs=[whole(shape)] * outs
             + [whole((slots, 2 * width))]
             + [pl.BlockSpec((slots, tile), lambda f: (0, f))] * 3,
-            out_shape=[piece] * chips
+            out_shape=[pltpu.HBM(shape, BF16)] * outs
             + [pltpu.HBM((slots, 2 * width), BF16)]
             + [mid] * 3,
             scratch_shapes=[pltpu.VMEM((slots, width), F32)] * 2,
@@ -300,25 +308,27 @@
             ),
             name="expert",
         )(me.reshape(1), rows, *[in_hbm(w) for w in (w_gate, w_up, w_down)])
-        return got[:chips], got[chips:]
-
-    def combine(buf, pair, pieces, weight):
+        return got[:outs], got[outs:]
+
+    def combine(tab, blocks, pieces, weight):
         return pl.pallas_call(
-            functools.partial(combine_kernel, chips, top, width),
-            out_shape=[row, row],
+            functools.partial(combine_kernel, len(blocks), top, width),
+            out_shape=[row] * len(blocks),
             compiler_params=params(),
             cost_estimate=pl.CostEstimate(
                 flops=10 * slots * tok * width * weight,
-                bytes_accessed=2 * (4 * tok * wide + 2 * slots * width) * weight,
+                bytes_accessed=4 * (2 * tok * wide + slots * width) * weight,
                 transcendentals=0,
             ),
             name="combine",
-        )(tab_back, buf, pair, *pieces)
-
-    def join(*parts):
+        )(tab, *blocks, *pieces)
+
+    left, right = (0, width), (width, wide)
+
+    def join(cuts, *parts):
         return pl.pallas_call(
-            join_kernel,
-            out_shape=row,
+            functools.partial(join_kernel, cuts),
+            out_shape=[jax.ShapeDtypeStruct((tok, hi - lo), BF16) for lo, hi in cuts],
             compiler_params=params(),
             cost_estimate=pl.CostEstimate(
                 flops=len(parts) * tok * wide,
@@ -331,33 +341,49 @@
     def next_plane(v):
         return lax.ppermute(v, "group", [(i, (i + 1) % groups) for i in range(groups)])
 
-    bufs, pairs, sent, came, kept, rets, outs = [], [], [], [], [], [], {}
+    bufs, sent, came, kept, rets, pairs, outs = [], [], [], [], [], {}, {}
     arriving = [buf0]
-
-    def send(k, *deps, before_dispatch=()):
+    last = groups - 1
+
+    def by_permutes(k):
+        return 0 < k < last
+
+    def exchange(v):
+        return lax.all_to_all(v, "local", split_axis=0, concat_axis=0, tiled=True)
+
+    def send(k, *deps):
         bufs.append(after(arriving[-1:], *deps)[0])
         if k + 1 < groups:
             arriving.append(next_plane(bufs[k]))
-        sent.append(dispatch(*after(bufs[k:], before_dispatch)))
-        pairs.append(other_core(*after(bufs[k:], sent[k:])))
-        came.append(
-            lax.all_to_all(sent[k], "local", split_axis=0, concat_axis=0, tiled=True)
-        )
+        sent.append(dispatch(bufs[k]))
+        if by_permutes(k):
+            pairs[k] = other_core(*after(bufs[k:], sent[k:]))
+        came.append(exchange(sent[k]))
 
     def compute(k, *deps):
-        ret, saved = expert(*after(came[k : k + 1], pairs[k : k + 1], *deps))
+        shape, parts = (count, rows_p, 2 * width), 1
+        if by_permutes(k):
+            shape, parts = (2 * rows_p, 2 * width), chips
+            deps = ([pairs[k]], *deps)
+        ret, saved = expert(*after(came[k : k + 1], *deps), shape, parts)
         rets.append(ret)
         kept.append(saved)
 
     def give_back(k, *deps):
-        outs[k] = swap(after(rets[k], *deps))
+        ready = after(rets[k], *deps)
+        outs[k] = swap(ready) if by_permutes(k) else [exchange(ready[0])]
 
     def plane_sums(k, *deps):
         weight = 1 if k == 1 else 100
-        mine, theirs = combine(bufs[k], pairs[k], after(outs[k], *deps), weight)
+        back = after(outs[k], *deps)
+        if not by_permutes(k):
+            return combine(tab_in, [bufs[k]], back, weight)
+        mine, theirs = combine(tab_back, [bufs[k], pairs[k]], back, weight)
         return [mine, other_core(theirs)]
 
-    last = groups - 1
+    def add_up(cuts, shares, sums):
+        return join(cuts, *after(shares[:1], sums), *shares[1:], *sums)
+
     send(0)
     send(1, sent)
     compute(0, sent[1:])
@@ -369,15 +395,21 @@
         send(k, rets[k - 2])
         compute(k - 1, sent[k:])
         shares = plane_sums(k - 2, rets[k - 1])
-        joined = join(*after(shares[:1], sums), shares[1], *sums)
-        sums = [next_plane(joined)]
+        joined = add_up([(0, wide)], shares, sums)
+        sums = [next_plane(joined[0])]
         give_back(k - 1)
-    compute(last, [joined])
+    compute(last, joined)
     give_back(last)
     shares = plane_sums(last - 1, rets[last])
-    joined = join(*after(shares[:1], sums), shares[1], *sums)
-    sums = [next_plane(joined)]
-    kept = [after(saved, [joined]) for saved in kept]
+    joined = add_up([left, right], shares, sums)
+    sums = [next_plane(v) for v in joined]
+    shares = plane_sums(last, joined)
+    give_back(0, outs[last], shares)
+    home = []
+    for cut, arrived in zip((left, right), sums):
+        leaving = add_up([cut], shares, [arrived])
+        home.append(next_plane(leaving[0]))
+    kept = [after(saved, leaving) for saved in kept]
     d_tile = 256
     d_steps = width // d_tile
     full = [whole((slots, hidden_width))] * groups
@@ -396,26 +428,17 @@
         ],
         compiler_params=params(),
         cost_estimate=pl.CostEstimate(
-            flops=6 * groups * slots * width * hidden_width * 20,
-            bytes_accessed=2 * (3 * width * hidden_width + 2 * groups * slots * width) * 20,
+            flops=120 * groups * slots * width * hidden_width,
+            bytes_accessed=40 * (3 * width * hidden_width + 2 * groups * slots * width),
             transcendentals=0,
         ),
         name="weight_grads",
     )(
-        *[s[0] for s in kept],
-        *[s[0] for s in kept],
-        *[s[1] for s in kept],
-        *[s[2] for s in kept],
-        *[s[3] for s in kept],
+        *[in_hbm(s[i]) for i in (0, 0, 1, 2, 3) for s in kept],
     )
-    shares = plane_sums(last, [d_w_down])
-    give_back(0, outs[last], [joined])
-    leaving = join(*after(shares[:1], sums), shares[1], *sums)
-    home = [next_plane(leaving)]
-    shares = plane_sums(0, [leaving])
-    home += [*after(shares[:1], home), shares[1]]
+    [share] = plane_sums(0, [d_w_down])
     mixed, d_tokens, d_gates = pl.pallas_call(
-        functools.partial(final_kernel, len(home), top, width),
+        functools.partial(final_kernel, width),
         out_shape=[
             jax.ShapeDtypeStruct((tok, width), BF16),
             jax.ShapeDtypeStruct((tok, width), BF16),
@@ -423,12 +446,12 @@
         ],
         compiler_params=params(),
         cost_estimate=pl.CostEstimate(
-            flops=len(home) * tok * wide,
-            bytes_accessed=2 * (1 + len(home)) * tok * wide,
+            flops=2 * tok * wide,
+            bytes_accessed=6 * tok * wide,
             transcendentals=0,
         ),
         name="final",
-    )(*home)
+    )(*home, *after([share], home))
 
     return mixed, d_tokens, d_gates.T, d_w_gate, d_w_up, d_w_down
 

time: 208 us -> 206 us (level)
    all_to_all x4 -> x6, waiting for transfers between devices: 7.16 us -> 18.5 us  [exchange(): return lax.all_to_all(v, 'local', split_axis=0, concat_axis=0, tiled=True)]
    ppermute x12 -> x6, waiting for transfers between devices: 17.2 us -> 7.01 us  [swap(): lax.ppermute(pieces[s], 'local', [(i, i ^ 2 * s) for i in range(count)])]
    all_to_all x4 -> x6, starting transfers between devices: 14.8 us -> 22.7 us  [exchange(): return lax.all_to_all(v, 'local', split_axis=0, concat_axis=0, tiled=True)]
    ppermute x12 -> x6, starting transfers between devices: 14.1 us -> 7.11 us  [swap(): lax.ppermute(pieces[s], 'local', [(i, i ^ 2 * s) for i in range(count)])]
    ppermute x6 -> x8, waiting for transfers between devices: 50 us -> 45 us  [next_plane(): lax.ppermute(v, 'group', [(i, (i + 1) % groups) for i in range(groups)])]
    ppermute x8 -> x4, waiting for transfers between devices: 0.16 us -> 2.34 us  [other_core(): return lax.ppermute(v, 'local', [(i, i ^ 1) for i in range(count)])]
    pallas_call x12 -> x13, Pallas kernels: 65.8 us -> 65.8 us  [the longest x4 42.9 us: expert(): pl.pallas_call(functools.partial(expert_kernel, outs, width), grid=(steps...]
  transfers between devices with their start and end apart: 30 -> 24, of which waited for: 12 -> 10; matrix products, arithmetic and copies ran while one was open for 0% -> 0% of each run, Pallas kernels for 44% -> 44%
where the time goes in v4:
time: 206 us; the launch traced here: 205 us
  Pallas kernels  94.4 us (46%)
  waiting for transfers between devices  72.9 us (35%)
  starting transfers between devices  35.3 us (17%)
    ppermute x8, waiting for transfers between devices, next_plane(): lax.ppermute(v, 'group', [(i, (i + 1) % groups) for i in range(groups)])  45 us
    pallas_call x4, Pallas kernels, expert(): pl.pallas_call(functools.partial(expert_kernel, outs, width), grid=(steps...  42.9 us
    all_to_all x6, starting transfers between devices, exchange(): return lax.all_to_all(v, 'local', split_axis=0, concat_axis=0, tiled=True)  22.7 us
    all_to_all x6, waiting for transfers between devices, exchange(): return lax.all_to_all(v, 'local', split_axis=0, concat_axis=0, tiled=True)  18.5 us
    pallas_call x1, Pallas kernels, local(): pl.pallas_call(functools.partial(weight_grad_kernel, groups), grid=(d_ste...  15.4 us
    pallas_call x4, Pallas kernels, combine(): pl.pallas_call(functools.partial(combine_kernel, len(blocks), top, width)...  13.8 us
    pallas_call x4, Pallas kernels, dispatch(): pl.pallas_call(functools.partial(dispatch_kernel, top, width), out_shape=...  11.8 us
    ppermute x6, starting transfers between devices, swap(): lax.ppermute(pieces[s], 'local', [(i, i ^ 2 * s) for i in range(count)])  7.11 us
  transfers between devices with their start and end apart: 24, of which 10 were waited for; matrix products, arithmetic and copies ran while one was open for 0% of the time, Pallas kernels for 44%

profile of v4, /device:TPU:0, one launch (start us, length us, event | category | flops | bytes accessed | tf_op | source)
XLA Modules:
  0.0 205.4 jit_solution(14667481129552184688)
XLA Ops:
  0.6 0.7 copy-done.3
  1.3 0.7 copy-done.4
  2.0 1.4 pack.1.buf_ref.refs_0_
  3.4 3.1 %collective-permute-start = (bf16[128,4224]{1,0:T(8,128)(2,1)S(1)}, bf16[128,4224]{1,0:T(8,128)(2,1)}, u32[]{:S(2)}, u32[]{:S(2)}) collective-permute-start(bf16[128,4224]{1,0:T(8,128)(2,1)S(1)} %pack.1.buf_ref.refs_0_), channel_id=1, source_target_pairs={{0,8},{8,16},{16,24},{24,0},{1,9},{9,17},{17,25},{25,1},{2,10},{10... | collective-permute-start | bytes 3244040 | tf_op jit(solution)/shard_map/ppermute | solution.py:342
  6.5 0.1 broadcast_in_dim.24
  6.6 0.1 convert_element_type.49
  6.7 0.1 pad.5.clone
  6.7 0.1 maximum_maximum_fusion.tab_ref
  6.8 2.0 dispatch.4
  8.8 3.7 %all-to-all-start = ((bf16[8,24,4096]{2,1,0:T(8,128)(2,1)}), bf16[8,24,4096]{2,1,0:T(8,128)(2,1)S(1)}, u32[]{:S(2)}, u32[]{:S(2)}) async-start(bf16[8,24,4096]{2,1,0:T(8,128)(2,1)} %dispatch.4), calls=%async_computation | async-start | bytes 3145728 | tf_op jit(solution)/shard_map/all_to_all | solution.py:352
  12.5 19.9 %collective-permute-done.buf_ref.refs_0_ = bf16[128,4224]{1,0:T(8,128)(2,1)} collective-permute-done((bf16[128,4224]{1,0:T(8,128)(2,1)S(1)}, bf16[128,4224]{1,0:T(8,128)(2,1)}, u32[]{:S(2)}, u32[]{:S(2)}) %collective-permute-start) | collective-permute-done | bytes 1081376 | tf_op jit(solution)/shard_map/ppermute | solution.py:342
  32.5 3.3 %dispatch.5 = bf16[8,24,4096]{2,1,0:T(8,128)(2,1)} custom-call(f32[8,192]{1,0:T(8,128)S(1)} %maximum_maximum_fusion.tab_ref, bf16[128,4224]{1,0:T(8,128)(2,1)} %collective-permute-done.buf_ref.refs_0_), custom_call_target="tpu_custom_call" | custom-call | flops 6039797760 | bytes 79626240 | tf_op jit(solution)/shard_map/dispatch/pallas_call | solution.py:266
  35.7 3.7 %all-to-all-start.1 = ((bf16[8,24,4096]{2,1,0:T(8,128)(2,1)}), bf16[8,24,4096]{2,1,0:T(8,128)(2,1)S(1)}, u32[]{:S(2)}, u32[]{:S(2)}) async-start(bf16[8,24,4096]{2,1,0:T(8,128)(2,1)} %dispatch.5), calls=%async_computation.1 | async-start | bytes 3145728 | tf_op jit(solution)/shard_map/all_to_all | solution.py:352
  39.5 0.5 collective-permute-start.3
  40.0 10.6 %expert.4 = (bf16[8,24,4096]{2,1,0:T(8,128)(2,1)}, bf16[192,4096]{1,0:T(8,128)(2,1)}, bf16[192,768]{1,0:T(8,128)(2,1)}, bf16[192,768]{1,0:T(8,128)(2,1)}, bf16[192,768]{1,0:T(8,128)(2,1)}) custom-call(s32[1]{0:T(128)} %bitcast.2.me_ref, bf16[8,24,4096]{2,1,0:T(8,128)(2,1)S(1)} %all-to-all-done.rows_ref, bf16[1,2048,768]{2,1,0:T(8,128)(2,1)} %refs_0_.7, ...), custom_call_target="tpu_custom_call" | custom-call | flops 3623878656 | bytes 15728640 | tf_op jit(solution)/shard_map/expert/pallas_call | solution.py:289
  50.6 9.0 %collective-permute-done.1.buf_ref.refs_0_ = bf16[128,4224]{1,0:T(8,128)(2,1)} collective-permute-done((bf16[128,4224]{1,0:T(8,128)(2,1)}, bf16[128,4224]{1,0:T(8,128)(2,1)}, u32[]{:S(2)}, u32[]{:S(2)}) %collective-permute-start.1) | collective-permute-done | bytes 1081376 | tf_op jit(solution)/shard_map/ppermute | solution.py:342
  59.6 0.0 collective-permute-start.2
  59.6 3.3 %dispatch.6 = bf16[8,24,4096]{2,1,0:T(8,128)(2,1)} custom-call(f32[8,192]{1,0:T(8,128)S(1)} %maximum_maximum_fusion.tab_ref, bf16[128,4224]{1,0:T(8,128)(2,1)} %collective-permute-done.1.buf_ref.refs_0_), custom_call_target="tpu_custom_call" | custom-call | flops 6039797760 | bytes 79626240 | tf_op jit(solution)/shard_map/dispatch/pallas_call | solution.py:266
  62.9 0.0 all-to-all-done.1.rows_ref
  62.9 3.6 %all-to-all-start.3 = ((bf16[8,24,4096]{2,1,0:T(8,128)(2,1)}), bf16[8,24,4096]{2,1,0:T(8,128)(2,1)S(1)}, u32[]{:S(2)}, u32[]{:S(2)}) async-start(bf16[8,24,4096]{2,1,0:T(8,128)(2,1)} %dispatch.6), calls=%async_computation.3 | async-start | bytes 3145728 | tf_op jit(solution)/shard_map/all_to_all | solution.py:352
  66.5 0.1 broadcast_in_dim.27
  66.6 0.1 convert_element_type.52
  66.7 0.5 collective-permute-start.7
  67.1 0.1 maximum_maximum_fusion.1.tab_ref
  67.2 0.0 collective-permute-done.3.refs_1_
  67.2 10.8 %expert.5 = (bf16[48,4096]{1,0:T(8,128)(2,1)}, bf16[48,4096]{1,0:T(8,128)(2,1)}, bf16[48,4096]{1,0:T(8,128)(2,1)}, bf16[48,4096]{1,0:T(8,128)(2,1)}, bf16[192,40...) custom-call(s32[1]{0:T(128)} %bitcast.2.me_ref, ...), custom_call_target="tpu_custom_call" | custom-call | flops 3623878656 | bytes 15728640 | tf_op jit(solution)/shard_map/expert/pallas_call | solution.py:289
  78.0 1.7 collective-permute-start.4
  79.8 1.5 collective-permute-start.5
  81.2 0.3 collective-permute-start.6
  81.6 4.3 %collective-permute-done.2.buf_ref.refs_0_ = bf16[128,4224]{1,0:T(8,128)(2,1)} collective-permute-done((bf16[128,4224]{1,0:T(8,128)(2,1)}, bf16[128,4224]{1,0:T(8,128)(2,1)}, u32[]{:S(2)}, u32[]{:S(2)}) %collective-permute-start.2) | collective-permute-done | bytes 1081376 | tf_op jit(solution)/shard_map/ppermute | solution.py:342
  85.9 3.2 %dispatch.7 = bf16[8,24,4096]{2,1,0:T(8,128)(2,1)} custom-call(f32[8,192]{1,0:T(8,128)S(1)} %maximum_maximum_fusion.tab_ref, bf16[128,4224]{1,0:T(8,128)(2,1)} %collective-permute-done.2.buf_ref.refs_0_), custom_call_target="tpu_custom_call" | custom-call | flops 6039797760 | bytes 79626240 | tf_op jit(solution)/shard_map/dispatch/pallas_call | solution.py:266
  89.1 0.0 all-to-all-done.3.rows_ref
  89.1 3.8 %all-to-all-start.2 = ((bf16[8,24,4096]{2,1,0:T(8,128)(2,1)}), bf16[8,24,4096]{2,1,0:T(8,128)(2,1)S(1)}, u32[]{:S(2)}, u32[]{:S(2)}) async-start(bf16[8,24,4096]{2,1,0:T(8,128)(2,1)} %dispatch.7), calls=%async_computation.2 | async-start | bytes 3145728 | tf_op jit(solution)/shard_map/all_to_all | solution.py:352
  92.9 10.8 %expert.6 = (bf16[48,4096]{1,0:T(8,128)(2,1)}, bf16[48,4096]{1,0:T(8,128)(2,1)}, bf16[48,4096]{1,0:T(8,128)(2,1)}, bf16[48,4096]{1,0:T(8,128)(2,1)}, bf16[192,40...) custom-call(s32[1]{0:T(128)} %bitcast.2.me_ref, ...), custom_call_target="tpu_custom_call" | custom-call | flops 3623878656 | bytes 15728640 | tf_op jit(solution)/shard_map/expert/pallas_call | solution.py:289
  103.8 0.0 collective-permute-done.4.refs_3_
  103.8 1.2 collective-permute-done.6.refs_5_
  105.0 4.2 %combine.4 = (bf16[128,4224]{1,0:T(8,128)(2,1)S(1)}, bf16[128,4224]{1,0:T(8,128)(2,1)S(1)}) custom-call(f32[8,96]{1,0:T(8,128)S(1)} %maximum_maximum_fusion.1.tab_ref, bf16[128,4224]{1,0:T(8,128)(2,1)} %collective-permute-done.buf_ref.refs_0_, bf16[128,4224]{1,0:T(8,128)(2,1)} %collective-permute-done.3.refs_1_, bf16[48,4096]{1,0:T(8,128)(2,1)S(1)} %copy-done.2, ...), custom_call_target="tpu_custom_call" | custom-call | flops 503316480 | bytes 5898240 | tf_op jit(solution)/shard_map/combine/pallas_call | solution.py:314
  109.1 0.1 collective-permute-start.8
  109.2 0.7 collective-permute-start.9
  109.9 1.5 collective-permute-start.10
  111.4 1.4 collective-permute-start.11
  112.8 0.0 collective-permute-done.8.refs_1_
  112.8 1.2 join.4
  114.0 0.0 collective-permute-start.12
  114.0 7.8 %all-to-all-done.2.rows_ref = bf16[8,24,4096]{2,1,0:T(8,128)(2,1)S(1)} async-done(((bf16[8,24,4096]{2,1,0:T(8,128)(2,1)}), bf16[8,24,4096]{2,1,0:T(8,128)(2,1)S(1)}, u32[]{:S(2)}, u32[]{:S(2)}) %all-to-all-start.2) | async-done | bytes 1572896 | tf_op jit(solution)/shard_map/all_to_all | solution.py:352
  121.8 10.7 %expert.7 = (bf16[8,24,4096]{2,1,0:T(8,128)(2,1)}, bf16[192,4096]{1,0:T(8,128)(2,1)}, bf16[192,768]{1,0:T(8,128)(2,1)}, bf16[192,768]{1,0:T(8,128)(2,1)}, bf16[192,768]{1,0:T(8,128)(2,1)}) custom-call(s32[1]{0:T(128)} %bitcast.2.me_ref, bf16[8,24,4096]{2,1,0:T(8,128)(2,1)S(1)} %all-to-all-done.2.rows_ref, bf16[1,2048,768]{2,1,0:T(8,128)(2,1)} %refs_0_.7, ...), custom_call_target="tpu_custom_call" | custom-call | flops 3623878656 | bytes 15728640 | tf_op jit(solution)/shard_map/expert/pallas_call | solution.py:289
  132.5 5.8 %collective-permute-done.11.refs_5_ = bf16[48,4096]{1,0:T(8,128)(2,1)} collective-permute-done((bf16[48,4096]{1,0:T(8,128)(2,1)}, bf16[48,4096]{1,0:T(8,128)(2,1)}, u32[]{:S(2)}, u32[]{:S(2)}) %collective-permute-start.11) | collective-permute-done | bytes 393248 | tf_op jit(solution)/shard_map/ppermute | solution.py:283
  138.3 3.6 %all-to-all-start.4 = ((bf16[8,24,4096]{2,1,0:T(8,128)(2,1)}), bf16[8,24,4096]{2,1,0:T(8,128)(2,1)S(1)}, u32[]{:S(2)}, u32[]{:S(2)}) async-start(bf16[8,24,4096]{2,1,0:T(8,128)(2,1)} %get-tuple-element.120), calls=%async_computation.4 | async-start | bytes 3145728 | tf_op jit(solution)/shard_map/all_to_all | solution.py:352
  141.9 4.0 %combine.5 = (bf16[128,4224]{1,0:T(8,128)(2,1)S(1)}, bf16[128,4224]{1,0:T(8,128)(2,1)S(1)}) custom-call(f32[8,96]{1,0:T(8,128)S(1)} %maximum_maximum_fusion.1.tab_ref, bf16[128,4224]{1,0:T(8,128)(2,1)} %collective-permute-done.1.buf_ref.refs_0_, bf16[128,4224]{1,0:T(8,128)(2,1)} %collective-permute-done.7.refs_1_, bf16[48,4096]{1,0:T(8,128)(2,1)S(1)} %copy-done.5, ...), custom_call_target="tpu_custom_call" | custom-call | flops 50331648000 | bytes 589824000 | tf_op jit(solution)/shard_map/combine/pallas_call | solution.py:314
  145.9 0.5 collective-permute-start.13
  146.4 2.3 %collective-permute-done.13.refs_1_ = bf16[128,4224]{1,0:T(8,128)(2,1)S(1)} collective-permute-done((bf16[128,4224]{1,0:T(8,128)(2,1)S(1)}, bf16[128,4224]{1,0:T(8,128)(2,1)S(1)}, u32[]{:S(2)}, u32[]{:S(2)}) %collective-permute-start.13) | collective-permute-done | bytes 1081376 | tf_op jit(solution)/shard_map/ppermute | solution.py:279
  148.7 2.4 %join.5 = (bf16[128,2048]{1,0:T(8,128)(2,1)}, bf16[128,2176]{1,0:T(8,128)(2,1)}) custom-call(bf16[128,4224]{1,0:T(8,128)(2,1)S(1)} %get-tuple-element.130.refs_0_, bf16[128,4224]{1,0:T(8,128)(2,1)S(1)} %collective-permute-done.13.refs_1_, bf16[128,4224]{1,0:T(8,128)(2,1)} %collective-permute-done.12.refs_2_), custom_call_target="tpu_custom_call" | custom-call | flops 1622016 | bytes 4325376 | tf_op jit(solution)/shard_map/join/pallas_call | solution.py:329
  151.2 1.0 collective-permute-start.16
  152.1 10.7 %all-to-all-done.4.refs_1_ = bf16[8,24,4096]{2,1,0:T(8,128)(2,1)S(1)} async-done(((bf16[8,24,4096]{2,1,0:T(8,128)(2,1)}), bf16[8,24,4096]{2,1,0:T(8,128)(2,1)S(1)}, u32[]{:S(2)}, u32[]{:S(2)}) %all-to-all-start.4) | async-done | bytes 1572896 | tf_op jit(solution)/shard_map/all_to_all | solution.py:352
  162.8 2.7 %combine.6.refs_0_ = bf16[128,4224]{1,0:T(8,128)(2,1)S(1)} custom-call(f32[8,192]{1,0:T(8,128)S(1)} %maximum_maximum_fusion.tab_ref, bf16[128,4224]{1,0:T(8,128)(2,1)} %collective-permute-done.2.buf_ref.refs_0_, bf16[8,24,4096]{2,1,0:T(8,128)(2,1)S(1)} %all-to-all-done.4.refs_1_), custom_call_target="tpu_custom_call" | custom-call | flops 50331648000 | bytes 589824000 | tf_op jit(solution)/shard_map/combine/pallas_call | solution.py:314
  165.6 4.3 %all-to-all-start.5 = ((bf16[8,24,4096]{2,1,0:T(8,128)(2,1)}), bf16[8,24,4096]{2,1,0:T(8,128)(2,1)}, u32[]{:S(2)}, u32[]{:S(2)}) async-start(bf16[8,24,4096]{2,1,0:T(8,128)(2,1)} %get-tuple-element.137), calls=%async_computation.5 | async-start | bytes 3145728 | tf_op jit(solution)/shard_map/all_to_all | solution.py:352
  169.9 2.0 join.6
  171.8 0.0 collective-permute-start.15
  171.8 8.0 %collective-permute-done.16.refs_1_ = bf16[128,2176]{1,0:T(8,128)(2,1)S(1)} collective-permute-done((bf16[128,2176]{1,0:T(8,128)(2,1)}, bf16[128,2176]{1,0:T(8,128)(2,1)S(1)}, u32[]{:S(2)}, u32[]{:S(2)}) %collective-permute-start.16) | collective-permute-done | bytes 557088 | tf_op jit(solution)/shard_map/ppermute | solution.py:342
  179.8 0.9 join.7
  180.8 15.4 %weight_grads.1 = (bf16[1,2048,768]{2,1,0:T(8,128)(2,1)}, bf16[1,2048,768]{2,1,0:T(8,128)(2,1)}, bf16[1,768,2048]{2,1,0:T(8,128)(2,1)}) custom-call(bf16[192,4096]{1,0:T(8,128)(2,1)} %get-tuple-element.142.refs_0_.refs_4_, bf16[192,4096]{1,0:T(8,128)(2,1)} %get-tuple-element.147.refs_1_.refs_5_, bf16[192,4096]{1,0:T(8,128)(2,1)} %get-tuple-element.152.refs_2_.refs_6_, ...), custom_call_target="tpu_custom_call" | custom-call | flops 144955146240 | bytes 314572800 | tf_op jit(solution)/shard_map/weight_grads/pallas_call | solution.py:416
  196.2 2.9 %combine.7.share_ref = bf16[128,4224]{1,0:T(8,128)(2,1)S(1)} custom-call(f32[8,192]{1,0:T(8,128)S(1)} %maximum_maximum_fusion.tab_ref, bf16[128,4224]{1,0:T(8,128)(2,1)S(1)} %copy-done.1, bf16[8,24,4096]{2,1,0:T(8,128)(2,1)} %all-to-all-done.5.refs_1_), custom_call_target="tpu_custom_call" | custom-call | flops 50331648000 | bytes 589824000 | tf_op jit(solution)/shard_map/combine/pallas_call | solution.py:314
  199.1 3.8 %collective-permute-done.17.right_ref = bf16[128,2176]{1,0:T(8,128)(2,1)} collective-permute-done((bf16[128,2176]{1,0:T(8,128)(2,1)}, bf16[128,2176]{1,0:T(8,128)(2,1)}, u32[]{:S(2)}, u32[]{:S(2)}) %collective-permute-start.17) | collective-permute-done | bytes 557088 | tf_op jit(solution)/shard_map/ppermute | solution.py:342
  202.9 2.5 %final.1 = (bf16[128,2048]{1,0:T(8,128)(2,1)}, bf16[128,2048]{1,0:T(8,128)(2,1)}, f32[4,128]{1,0:T(4,128)}) custom-call(bf16[128,2048]{1,0:T(8,128)(2,1)} %collective-permute-done.15.left_ref, bf16[128,2176]{1,0:T(8,128)(2,1)} %collective-permute-done.17.right_ref, bf16[128,4224]{1,0:T(8,128)(2,1)S(1)} %combine.7.share_ref), custom_call_target="tpu_custom_call" | custom-call | flops 1081344 | bytes 3244032 | tf_op jit(solution)/shard_map/final/pallas_call | solution.py:440
  (27 shorter events, 0.1 us)
Async XLA Ops:
  0.6 0.7 copy-start.3
  1.3 0.7 copy-start.4
  3.4 5.4 %copy-start = (bf16[128,4224]{1,0:T(8,128)(2,1)}, bf16[128,4224]{1,0:T(8,128)(2,1)S(1)}, u32[]{:S(2)}) copy-start(bf16[128,4224]{1,0:T(8,128)(2,1)S(1)} %pack.1.buf_ref.refs_0_) | copy-start | bytes 3244036
  3.4 29.1 %collective-permute-start = (bf16[128,4224]{1,0:T(8,128)(2,1)S(1)}, bf16[128,4224]{1,0:T(8,128)(2,1)}, u32[]{:S(2)}, u32[]{:S(2)}) collective-permute-start(bf16[128,4224]{1,0:T(8,128)(2,1)S(1)} %pack.1.buf_ref.refs_0_), channel_id=1, source_target_pairs={{0,8},{8,16},{16,24},{24,0},{1,9},{9,17},{17,25},{25,1},{2,10},{10... | collective-permute-start | bytes 3244040 | tf_op jit(solution)/shard_map/ppermute | solution.py:342
  8.8 26.9 %all-to-all-start = ((bf16[8,24,4096]{2,1,0:T(8,128)(2,1)}), bf16[8,24,4096]{2,1,0:T(8,128)(2,1)S(1)}, u32[]{:S(2)}, u32[]{:S(2)}) async-start(bf16[8,24,4096]{2,1,0:T(8,128)(2,1)} %dispatch.4), calls=%async_computation | async-start | bytes 3145728 | tf_op jit(solution)/shard_map/all_to_all | solution.py:352
  32.5 27.2 %collective-permute-start.1 = (bf16[128,4224]{1,0:T(8,128)(2,1)}, bf16[128,4224]{1,0:T(8,128)(2,1)}, u32[]{:S(2)}, u32[]{:S(2)}) collective-permute-start(bf16[128,4224]{1,0:T(8,128)(2,1)} %collective-permute-done.buf_ref.refs_0_), channel_id=1, source_target_pairs={{0,8},{8,16},{16,24},{24,0},{1,9},{9,17},{17,25},{25,1},{2,10},{10... | collective-permute-start | bytes 3244040 | tf_op jit(solution)/shard_map/ppermute | solution.py:342
  35.7 27.2 %all-to-all-start.1 = ((bf16[8,24,4096]{2,1,0:T(8,128)(2,1)}), bf16[8,24,4096]{2,1,0:T(8,128)(2,1)S(1)}, u32[]{:S(2)}, u32[]{:S(2)}) async-start(bf16[8,24,4096]{2,1,0:T(8,128)(2,1)} %dispatch.5), calls=%async_computation.1 | async-start | bytes 3145728 | tf_op jit(solution)/shard_map/all_to_all | solution.py:352
  39.5 27.7 %collective-permute-start.3 = (bf16[128,4224]{1,0:T(8,128)(2,1)}, bf16[128,4224]{1,0:T(8,128)(2,1)}, u32[]{:S(2)}, u32[]{:S(2)}) collective-permute-start(bf16[128,4224]{1,0:T(8,128)(2,1)} %collective-permute-done.buf_ref.refs_0_), channel_id=1, source_target_pairs={{0,1},{1,0},{2,3},{3,2},{4,5},{5,4},{6,7},{7,6},{8,9},{9,8},{10,11... | collective-permute-start | bytes 3244040 | tf_op jit(solution)/shard_map/ppermute | solution.py:279
  59.6 26.2 %collective-permute-start.2 = (bf16[128,4224]{1,0:T(8,128)(2,1)}, bf16[128,4224]{1,0:T(8,128)(2,1)}, u32[]{:S(2)}, u32[]{:S(2)}) collective-permute-start(bf16[128,4224]{1,0:T(8,128)(2,1)} %collective-permute-done.1.buf_ref.refs_0_), channel_id=1, source_target_pairs={{0,8},{8,16},{16,24},{24,0},{1,9},{9,17},{17,25},{25,1},{2,10},{10... | collective-permute-start | bytes 3244040 | tf_op jit(solution)/shard_map/ppermute | solution.py:342
  62.9 26.2 %all-to-all-start.3 = ((bf16[8,24,4096]{2,1,0:T(8,128)(2,1)}), bf16[8,24,4096]{2,1,0:T(8,128)(2,1)S(1)}, u32[]{:S(2)}, u32[]{:S(2)}) async-start(bf16[8,24,4096]{2,1,0:T(8,128)(2,1)} %dispatch.6), calls=%async_computation.3 | async-start | bytes 3145728 | tf_op jit(solution)/shard_map/all_to_all | solution.py:352
  66.7 26.2 %collective-permute-start.7 = (bf16[128,4224]{1,0:T(8,128)(2,1)}, bf16[128,4224]{1,0:T(8,128)(2,1)}, u32[]{:S(2)}, u32[]{:S(2)}) collective-permute-start(bf16[128,4224]{1,0:T(8,128)(2,1)} %collective-permute-done.1.buf_ref.refs_0_), channel_id=1, source_target_pairs={{0,1},{1,0},{2,3},{3,2},{4,5},{5,4},{6,7},{7,6},{8,9},{9,8},{10,11... | collective-permute-start | bytes 3244040 | tf_op jit(solution)/shard_map/ppermute | solution.py:279
  78.0 25.7 %collective-permute-start.4 = (bf16[48,4096]{1,0:T(8,128)(2,1)}, bf16[48,4096]{1,0:T(8,128)(2,1)S(1)}, u32[]{:S(2)}, u32[]{:S(2)}) collective-permute-start(bf16[48,4096]{1,0:T(8,128)(2,1)} %get-tuple-element.104), channel_id=1, source_target_pairs={{0,2},{1,3},{2,0},{3,1},{4,6},{5,7},{6,4},{7,5},{8,10},{9,11},{10,... | collective-permute-start | bytes 1179656 | tf_op jit(solution)/shard_map/ppermute | solution.py:283
  79.8 24.0 %collective-permute-start.5 = (bf16[48,4096]{1,0:T(8,128)(2,1)}, bf16[48,4096]{1,0:T(8,128)(2,1)}, u32[]{:S(2)}, u32[]{:S(2)}) collective-permute-start(bf16[48,4096]{1,0:T(8,128)(2,1)} %get-tuple-element.105), channel_id=1, source_target_pairs={{0,4},{1,5},{2,6},{3,7},{4,0},{5,1},{6,2},{7,3},{8,12},{9,13},{10,... | collective-permute-start | bytes 1179656 | tf_op jit(solution)/shard_map/ppermute | solution.py:283
  81.2 23.7 %collective-permute-start.6 = (bf16[48,4096]{1,0:T(8,128)(2,1)}, bf16[48,4096]{1,0:T(8,128)(2,1)}, u32[]{:S(2)}, u32[]{:S(2)}) collective-permute-start(bf16[48,4096]{1,0:T(8,128)(2,1)} %get-tuple-element.106), channel_id=1, source_target_pairs={{0,6},{1,7},{2,4},{3,5},{4,2},{5,3},{6,0},{7,1},{8,14},{9,15},{10,... | collective-permute-start | bytes 1179656 | tf_op jit(solution)/shard_map/ppermute | solution.py:283
  89.1 32.7 %all-to-all-start.2 = ((bf16[8,24,4096]{2,1,0:T(8,128)(2,1)}), bf16[8,24,4096]{2,1,0:T(8,128)(2,1)S(1)}, u32[]{:S(2)}, u32[]{:S(2)}) async-start(bf16[8,24,4096]{2,1,0:T(8,128)(2,1)} %dispatch.7), calls=%async_computation.2 | async-start | bytes 3145728 | tf_op jit(solution)/shard_map/all_to_all | solution.py:352
  92.9 12.1 %copy-start.2 = (bf16[48,4096]{1,0:T(8,128)(2,1)S(1)}, bf16[48,4096]{1,0:T(8,128)(2,1)}, u32[]{:S(2)}) copy-start(bf16[48,4096]{1,0:T(8,128)(2,1)} %get-tuple-element.113.refs_2_) | copy-start | bytes 1179652
  109.1 3.6 %collective-permute-start.8 = (bf16[128,4224]{1,0:T(8,128)(2,1)S(1)}, bf16[128,4224]{1,0:T(8,128)(2,1)S(1)}, u32[]{:S(2)}, u32[]{:S(2)}) collective-permute-start(bf16[128,4224]{1,0:T(8,128)(2,1)S(1)} %get-tuple-element.118), channel_id=1, source_target_pairs={{0,1},{1,0},{2,3},{3,2},{4,5},{5,4},{6,7},{7,6},{8,9},{9,8},{10,11... | collective-permute-start | bytes 3244040 | tf_op jit(solution)/shard_map/ppermute | solution.py:279
  109.2 23.3 %collective-permute-start.9 = (bf16[48,4096]{1,0:T(8,128)(2,1)}, bf16[48,4096]{1,0:T(8,128)(2,1)S(1)}, u32[]{:S(2)}, u32[]{:S(2)}) collective-permute-start(bf16[48,4096]{1,0:T(8,128)(2,1)} %get-tuple-element.122), channel_id=1, source_target_pairs={{0,2},{1,3},{2,0},{3,1},{4,6},{5,7},{6,4},{7,5},{8,10},{9,11},{10,... | collective-permute-start | bytes 1179656 | tf_op jit(solution)/shard_map/ppermute | solution.py:283
  109.9 22.6 %collective-permute-start.10 = (bf16[48,4096]{1,0:T(8,128)(2,1)}, bf16[48,4096]{1,0:T(8,128)(2,1)S(1)}, u32[]{:S(2)}, u32[]{:S(2)}) collective-permute-start(bf16[48,4096]{1,0:T(8,128)(2,1)} %get-tuple-element.123), channel_id=1, source_target_pairs={{0,4},{1,5},{2,6},{3,7},{4,0},{5,1},{6,2},{7,3},{8,12},{9,13},{10,... | collective-permute-start | bytes 1179656 | tf_op jit(solution)/shard_map/ppermute | solution.py:283
  111.4 26.9 %collective-permute-start.11 = (bf16[48,4096]{1,0:T(8,128)(2,1)}, bf16[48,4096]{1,0:T(8,128)(2,1)}, u32[]{:S(2)}, u32[]{:S(2)}) collective-permute-start(bf16[48,4096]{1,0:T(8,128)(2,1)} %get-tuple-element.124), channel_id=1, source_target_pairs={{0,6},{1,7},{2,4},{3,5},{4,2},{5,3},{6,0},{7,1},{8,14},{9,15},{10,... | collective-permute-start | bytes 1179656 | tf_op jit(solution)/shard_map/ppermute | solution.py:283
  114.0 32.4 %collective-permute-start.12 = (bf16[128,4224]{1,0:T(8,128)(2,1)}, bf16[128,4224]{1,0:T(8,128)(2,1)}, u32[]{:S(2)}, u32[]{:S(2)}) collective-permute-start(bf16[128,4224]{1,0:T(8,128)(2,1)} %join.4), channel_id=1, source_target_pairs={{0,8},{8,16},{16,24},{24,0},{1,9},{9,17},{17,25},{25,1},{2,10},{10... | collective-permute-start | bytes 3244040 | tf_op jit(solution)/shard_map/ppermute | solution.py:342
  132.5 9.4 %copy-start.5 = (bf16[48,4096]{1,0:T(8,128)(2,1)S(1)}, bf16[48,4096]{1,0:T(8,128)(2,1)}, u32[]{:S(2)}) copy-start(bf16[48,4096]{1,0:T(8,128)(2,1)} %get-tuple-element.125.refs_2_) | copy-start | bytes 1179652
  138.3 24.5 %all-to-all-start.4 = ((bf16[8,24,4096]{2,1,0:T(8,128)(2,1)}), bf16[8,24,4096]{2,1,0:T(8,128)(2,1)S(1)}, u32[]{:S(2)}, u32[]{:S(2)}) async-start(bf16[8,24,4096]{2,1,0:T(8,128)(2,1)} %get-tuple-element.120), calls=%async_computation.4 | async-start | bytes 3145728 | tf_op jit(solution)/shard_map/all_to_all | solution.py:352
  145.9 2.8 %collective-permute-start.13 = (bf16[128,4224]{1,0:T(8,128)(2,1)S(1)}, bf16[128,4224]{1,0:T(8,128)(2,1)S(1)}, u32[]{:S(2)}, u32[]{:S(2)}) collective-permute-start(bf16[128,4224]{1,0:T(8,128)(2,1)S(1)} %get-tuple-element.131), channel_id=1, source_target_pairs={{0,1},{1,0},{2,3},{3,2},{4,5},{5,4},{6,7},{7,6},{8,9},{9,8},{10,11... | collective-permute-start | bytes 3244040 | tf_op jit(solution)/shard_map/ppermute | solution.py:279
  151.2 18.7 %collective-permute-start.14 = (bf16[128,2048]{1,0:T(8,128)(2,1)}, bf16[128,2048]{1,0:T(8,128)(2,1)}, u32[]{:S(2)}, u32[]{:S(2)}) collective-permute-start(bf16[128,2048]{1,0:T(8,128)(2,1)} %get-tuple-element.132), channel_id=1, source_target_pairs={{0,8},{8,16},{16,24},{24,0},{1,9},{9,17},{17,25},{25,1},{2,10},{10... | collective-permute-start | bytes 1572872 | tf_op jit(solution)/shard_map/ppermute | solution.py:342
  151.2 28.7 %collective-permute-start.16 = (bf16[128,2176]{1,0:T(8,128)(2,1)}, bf16[128,2176]{1,0:T(8,128)(2,1)S(1)}, u32[]{:S(2)}, u32[]{:S(2)}) collective-permute-start(bf16[128,2176]{1,0:T(8,128)(2,1)} %get-tuple-element.133), channel_id=1, source_target_pairs={{0,8},{8,16},{16,24},{24,0},{1,9},{9,17},{17,25},{25,1},{2,10},{10... | collective-permute-start | bytes 1671176 | tf_op jit(solution)/shard_map/ppermute | solution.py:342
  165.6 30.6 %all-to-all-start.5 = ((bf16[8,24,4096]{2,1,0:T(8,128)(2,1)}), bf16[8,24,4096]{2,1,0:T(8,128)(2,1)}, u32[]{:S(2)}, u32[]{:S(2)}) async-start(bf16[8,24,4096]{2,1,0:T(8,128)(2,1)} %get-tuple-element.137), calls=%async_computation.5 | async-start | bytes 3145728 | tf_op jit(solution)/shard_map/all_to_all | solution.py:352
  171.8 27.2 %collective-permute-start.15 = (bf16[128,2048]{1,0:T(8,128)(2,1)}, bf16[128,2048]{1,0:T(8,128)(2,1)}, u32[]{:S(2)}, u32[]{:S(2)}) collective-permute-start(bf16[128,2048]{1,0:T(8,128)(2,1)} %join.6), channel_id=1, source_target_pairs={{0,8},{8,16},{16,24},{24,0},{1,9},{9,17},{17,25},{25,1},{2,10},{10... | collective-permute-start | bytes 1572872 | tf_op jit(solution)/shard_map/ppermute | solution.py:342
  180.8 22.1 %collective-permute-start.17 = (bf16[128,2176]{1,0:T(8,128)(2,1)}, bf16[128,2176]{1,0:T(8,128)(2,1)}, u32[]{:S(2)}, u32[]{:S(2)}) collective-permute-start(bf16[128,2176]{1,0:T(8,128)(2,1)} %join.7), channel_id=1, source_target_pairs={{0,8},{8,16},{16,24},{24,0},{1,9},{9,17},{17,25},{25,1},{2,10},{10... | collective-permute-start | bytes 1671176 | tf_op jit(solution)/shard_map/ppermute | solution.py:342
  180.8 15.4 %copy-start.1 = (bf16[128,4224]{1,0:T(8,128)(2,1)S(1)}, bf16[128,4224]{1,0:T(8,128)(2,1)}, u32[]{:S(2)}) copy-start(bf16[128,4224]{1,0:T(8,128)(2,1)} %copy-done) | copy-start | bytes 3244036

commit v5 on v4

--- a/solution.py
+++ b/solution.py
@@ -135,38 +135,32 @@
                 ret[to, width:] = acc_d[at, :].astype(BF16)
 
 
-def combine_kernel(blocks, top, width, tab_ref, *refs):
-    bufs, rest = refs[:blocks], refs[blocks:]
-    got, parts = rest[:-blocks], rest[-blocks:]
-    if len(got[0].shape) == 3:
-        got = [got[0].at[s] for s in range(got[0].shape[0])]
-    rows_p = got[0].shape[0] // blocks
+def combine_kernel(lo_row, rows_p, top, width, tab_ref, buf_ref, *refs):
+    got, part_ref = refs[:-1], refs[-1]
+    got = got if len(got[0].shape) == 2 else [got[0].at[s] for s in range(got[0].shape[0])]
+    rows = slice(lo_row, lo_row + rows_p)
     step = 512
-    for b, buf_ref in enumerate(bufs):
-        rows = slice(b * rows_p, (b + 1) * rows_p)
-        sel, gate, hits = selection(
-            buf_ref[:, 2 * width :].astype(F32), tab_ref[...], top
-        )
-        plain = sel.astype(BF16)
-        gated = split3(sel * gate)
-        prod = None
-        for c in range(0, width, step):
-            out_rows = gather_rows(got, c, c + step, rows)
-            dx_rows = gather_rows(got, width + c, width + c + step, rows)
-            mixed = dot(gated[0], out_rows) + dot(gated[1], out_rows)
-            mixed = mixed + dot(gated[2], out_rows)
-            part = dot(buf_ref[:, width + c : width + c + step], out_rows, 1, 1)
-            prod = part if prod is None else prod + part
-            parts[b][:, c : c + step] = mixed.astype(BF16)
-            parts[b][:, width + c : width + c + step] = dot(plain, dx_rows).astype(BF16)
-        prod = prod * sel
-        lane = lax.broadcasted_iota(jnp.int32, (buf_ref.shape[0], META), 1)
-        packed = jnp.zeros((buf_ref.shape[0], META), F32)
-        for k, h in enumerate(hits):
-            column = jnp.sum(prod * h, axis=1, keepdims=True)
-            for i, piece in enumerate(split3(column)):
-                packed = jnp.where(lane == i * top + k, piece.astype(F32), packed)
-        parts[b][:, 2 * width :] = packed.astype(BF16)
+    sel, gate, hits = selection(buf_ref[:, 2 * width :].astype(F32), tab_ref[...], top)
+    plain = sel.astype(BF16)
+    gated = split3(sel * gate)
+    prod = None
+    for c in range(0, width, step):
+        out_rows = gather_rows(got, c, c + step, rows)
+        dx_rows = gather_rows(got, width + c, width + c + step, rows)
+        mixed = dot(gated[0], out_rows) + dot(gated[1], out_rows)
+        mixed = mixed + dot(gated[2], out_rows)
+        part = dot(buf_ref[:, width + c : width + c + step], out_rows, 1, 1)
+        prod = part if prod is None else prod + part
+        part_ref[:, c : c + step] = mixed.astype(BF16)
+        part_ref[:, width + c : width + c + step] = dot(plain, dx_rows).astype(BF16)
+    prod = prod * sel
+    lane = lax.broadcasted_iota(jnp.int32, (buf_ref.shape[0], META), 1)
+    packed = jnp.zeros((buf_ref.shape[0], META), F32)
+    for k, h in enumerate(hits):
+        column = jnp.sum(prod * h, axis=1, keepdims=True)
+        for i, piece in enumerate(split3(column)):
+            packed = jnp.where(lane == i * top + k, piece.astype(F32), packed)
+    part_ref[:, 2 * width :] = packed.astype(BF16)
 
 
 def join_kernel(cuts, *refs):
@@ -184,10 +178,12 @@
     return list(lax.optimization_barrier((*values, *flat))[: len(values)])
 
 
-def final_kernel(width, left_ref, right_ref, share_ref, mixed_ref, d_tok_ref, d_gates_ref):
-    left, right = left_ref[...].astype(F32), right_ref[...].astype(F32)
-    mixed_ref[...] = (left + share_ref[:, :width].astype(F32)).astype(BF16)
-    rest = right + share_ref[:, width:].astype(F32)
+def final_left_kernel(sum_ref, share_ref, mixed_ref):
+    mixed_ref[...] = (sum_ref[...].astype(F32) + share_ref[...].astype(F32)).astype(BF16)
+
+
+def final_right_kernel(width, sum_ref, share_ref, d_tok_ref, d_gates_ref):
+    rest = sum_ref[...].astype(F32) + share_ref[:, width:].astype(F32)
     d_tok_ref[...] = rest[:, :width].astype(BF16)
     packed = rest[:, width:].T
     top = d_gates_ref.shape[0]
@@ -256,7 +252,7 @@
             flops=tok * META, bytes_accessed=4 * tok * wide, transcendentals=0
         ),
         name="pack",
-    )(in_hbm(tokens), in_hbm(cotangent), expert_ids.T, gates.T)
+    )(*[in_hbm(v) for v in (tokens, cotangent, expert_ids.T, gates.T)])
     row = jax.ShapeDtypeStruct((tok, wide), BF16)
 
     tile = 256
@@ -310,10 +306,10 @@
         )(me.reshape(1), rows, *[in_hbm(w) for w in (w_gate, w_up, w_down)])
         return got[:outs], got[outs:]
 
-    def combine(tab, blocks, pieces, weight):
+    def combine(tab, block, pieces, lo_row, weight):
         return pl.pallas_call(
-            functools.partial(combine_kernel, len(blocks), top, width),
-            out_shape=[row] * len(blocks),
+            functools.partial(combine_kernel, lo_row, rows_p, top, width),
+            out_shape=row,
             compiler_params=params(),
             cost_estimate=pl.CostEstimate(
                 flops=10 * slots * tok * width * weight,
@@ -321,7 +317,7 @@
                 transcendentals=0,
             ),
             name="combine",
-        )(tab, *blocks, *pieces)
+        )(tab, block, *pieces)
 
     left, right = (0, width), (width, wide)
 
@@ -377,8 +373,9 @@
         weight = 1 if k == 1 else 100
         back = after(outs[k], *deps)
         if not by_permutes(k):
-            return combine(tab_in, [bufs[k]], back, weight)
-        mine, theirs = combine(tab_back, [bufs[k], pairs[k]], back, weight)
+            return [combine(tab_in, bufs[k], back, 0, weight)]
+        theirs = combine(tab_back, pairs[k], back, rows_p, weight)
+        mine = combine(tab_back, *after(bufs[k : k + 1], [theirs]), back, 0, 1)
         return [mine, other_core(theirs)]
 
     def add_up(cuts, shares, sums):
@@ -437,22 +434,29 @@
         *[in_hbm(s[i]) for i in (0, 0, 1, 2, 3) for s in kept],
     )
     [share] = plane_sums(0, [d_w_down])
-    mixed, d_tokens, d_gates = pl.pallas_call(
-        functools.partial(final_kernel, width),
+    cost = pl.CostEstimate(
+        flops=tok * wide, bytes_accessed=3 * tok * wide, transcendentals=0
+    )
+    mixed = pl.pallas_call(
+        final_left_kernel,
+        grid=(1,),
+        in_specs=[pl.BlockSpec((tok, width), lambda i: (0, 0))] * 2,
+        out_specs=pl.BlockSpec((tok, width), lambda i: (0, 0)),
+        out_shape=jax.ShapeDtypeStruct((tok, width), BF16),
+        compiler_params=params(),
+        cost_estimate=cost,
+        name="final_left",
+    )(home[0], share)
+    d_tokens, d_gates = pl.pallas_call(
+        functools.partial(final_right_kernel, width),
         out_shape=[
-            jax.ShapeDtypeStruct((tok, width), BF16),
             jax.ShapeDtypeStruct((tok, width), BF16),
             jax.ShapeDtypeStruct((top, tok), F32),
         ],
         compiler_params=params(),
-        cost_estimate=pl.CostEstimate(
-            flops=2 * tok * wide,
-            bytes_accessed=6 * tok * wide,
-            transcendentals=0,
-        ),
-        name="final",
-    )(*home, *after([share], home))
-
+        cost_estimate=cost,
+        name="final_right",
+    )(*after([home[1]], [mixed]), share)
     return mixed, d_tokens, d_gates.T, d_w_gate, d_w_up, d_w_down
 
 

time: 206 us -> 204 us (level)
  waiting for transfers between devices: 72.9 us -> 66.7 us
  Pallas kernels: 94.4 us -> 98.9 us
    pallas_call x5 -> x8, Pallas kernels: 16.3 us -> 20.9 us  [the longest x6 16.8 us: combine(): pl.pallas_call(functools.partial(combine_kernel, lo_row, rows_p, top, wid...]
    ppermute x8, waiting for transfers between devices: 45 us -> 41.8 us  [next_plane(): lax.ppermute(v, 'group', [(i, (i + 1) % groups) for i in range(groups)])]
    ppermute x4, waiting for transfers between devices: 2.34 us -> 0.01 us  [other_core(): return lax.ppermute(v, 'local', [(i, i ^ 1) for i in range(count)])]
  transfers between devices with their start and end apart: 24 -> 24, of which waited for: 10 -> 9; matrix products, arithmetic and copies ran while one was open for 0% -> 0% of each run, Pallas kernels for 44% -> 47%
where the time goes in v5:
time: 204 us; the launch traced here: 203 us
  Pallas kernels  98.9 us (48%)
  waiting for transfers between devices  66.7 us (33%)
  starting transfers between devices  35.6 us (17%)
    pallas_call x4, Pallas kernels, expert(): pl.pallas_call(functools.partial(expert_kernel, outs, width), grid=(steps...  42.8 us
    ppermute x8, waiting for transfers between devices, next_plane(): lax.ppermute(v, 'group', [(i, (i + 1) % groups) for i in range(groups)])  41.8 us
    all_to_all x6, starting transfers between devices, exchange(): return lax.all_to_all(v, 'local', split_axis=0, concat_axis=0, tiled=True)  22.9 us
    all_to_all x6, waiting for transfers between devices, exchange(): return lax.all_to_all(v, 'local', split_axis=0, concat_axis=0, tiled=True)  17.8 us
    pallas_call x6, Pallas kernels, combine(): pl.pallas_call(functools.partial(combine_kernel, lo_row, rows_p, top, wid...  16.8 us
    pallas_call x1, Pallas kernels, local(): pl.pallas_call(functools.partial(weight_grad_kernel, groups), grid=(d_ste...  15.4 us
    pallas_call x4, Pallas kernels, dispatch(): pl.pallas_call(functools.partial(dispatch_kernel, top, width), out_shape=...  11.8 us
    ppermute x6, starting transfers between devices, swap(): lax.ppermute(pieces[s], 'local', [(i, i ^ 2 * s) for i in range(count)])  7.11 us
  transfers between devices with their start and end apart: 24, of which 9 were waited for; matrix products, arithmetic and copies ran while one was open for 0% of the time, Pallas kernels for 47%

profile of v5, /device:TPU:0, one launch (start us, length us, event | category | flops | bytes accessed | tf_op | source)
XLA Modules:
  0.0 202.6 jit_solution(11805648692034177893)
XLA Ops:
  0.6 1.4 pack.1.buf_ref
  2.0 3.1 %collective-permute-start = (bf16[128,4224]{1,0:T(8,128)(2,1)S(1)}, bf16[128,4224]{1,0:T(8,128)(2,1)}, u32[]{:S(2)}, u32[]{:S(2)}) collective-permute-start(bf16[128,4224]{1,0:T(8,128)(2,1)S(1)} %pack.1.buf_ref), channel_id=1, source_target_pairs={{0,8},{8,16},{16,24},{24,0},{1,9},{9,17},{17,25},{25,1},{2,10},{10... | collective-permute-start | bytes 3244040 | tf_op jit(solution)/shard_map/ppermute | solution.py:338
  5.1 0.1 broadcast_in_dim.24
  5.2 0.1 convert_element_type.49
  5.3 0.1 pad.5.clone
  5.4 0.1 maximum_maximum_fusion.tab_ref
  5.4 2.0 dispatch.4
  7.5 3.7 %all-to-all-start = ((bf16[8,24,4096]{2,1,0:T(8,128)(2,1)}), bf16[8,24,4096]{2,1,0:T(8,128)(2,1)S(1)}, u32[]{:S(2)}, u32[]{:S(2)}) async-start(bf16[8,24,4096]{2,1,0:T(8,128)(2,1)} %dispatch.4), calls=%async_computation | async-start | bytes 3145728 | tf_op jit(solution)/shard_map/all_to_all | solution.py:348
  11.2 19.9 %collective-permute-done.buf_ref = bf16[128,4224]{1,0:T(8,128)(2,1)} collective-permute-done((bf16[128,4224]{1,0:T(8,128)(2,1)S(1)}, bf16[128,4224]{1,0:T(8,128)(2,1)}, u32[]{:S(2)}, u32[]{:S(2)}) %collective-permute-start) | collective-permute-done | bytes 1081376 | tf_op jit(solution)/shard_map/ppermute | solution.py:338
  31.1 0.0 collective-permute-start.1
  31.1 3.3 %dispatch.5 = bf16[8,24,4096]{2,1,0:T(8,128)(2,1)} custom-call(f32[8,192]{1,0:T(8,128)S(1)} %maximum_maximum_fusion.tab_ref, bf16[128,4224]{1,0:T(8,128)(2,1)} %collective-permute-done.buf_ref), custom_call_target="tpu_custom_call" | custom-call | flops 6039797760 | bytes 79626240 | tf_op jit(solution)/shard_map/dispatch/pallas_call | solution.py:262
  34.4 0.0 all-to-all-done.rows_ref
  34.4 3.7 %all-to-all-start.1 = ((bf16[8,24,4096]{2,1,0:T(8,128)(2,1)}), bf16[8,24,4096]{2,1,0:T(8,128)(2,1)S(1)}, u32[]{:S(2)}, u32[]{:S(2)}) async-start(bf16[8,24,4096]{2,1,0:T(8,128)(2,1)} %dispatch.5), calls=%async_computation.1 | async-start | bytes 3145728 | tf_op jit(solution)/shard_map/all_to_all | solution.py:348
  38.1 0.5 collective-permute-start.3
  38.6 10.7 %expert.4 = (bf16[8,24,4096]{2,1,0:T(8,128)(2,1)}, bf16[192,4096]{1,0:T(8,128)(2,1)}, bf16[192,768]{1,0:T(8,128)(2,1)}, bf16[192,768]{1,0:T(8,128)(2,1)}, bf16[192,768]{1,0:T(8,128)(2,1)}) custom-call(s32[1]{0:T(128)} %bitcast.2.me_ref, bf16[8,24,4096]{2,1,0:T(8,128)(2,1)S(1)} %all-to-all-done.rows_ref, bf16[1,2048,768]{2,1,0:T(8,128)(2,1)} %refs_0_.7, ...), custom_call_target="tpu_custom_call" | custom-call | flops 3623878656 | bytes 15728640 | tf_op jit(solution)/shard_map/expert/pallas_call | solution.py:285
  49.3 9.0 %collective-permute-done.1.buf_ref = bf16[128,4224]{1,0:T(8,128)(2,1)} collective-permute-done((bf16[128,4224]{1,0:T(8,128)(2,1)}, bf16[128,4224]{1,0:T(8,128)(2,1)}, u32[]{:S(2)}, u32[]{:S(2)}) %collective-permute-start.1) | collective-permute-done | bytes 1081376 | tf_op jit(solution)/shard_map/ppermute | solution.py:338
  58.3 3.3 %dispatch.6 = bf16[8,24,4096]{2,1,0:T(8,128)(2,1)} custom-call(f32[8,192]{1,0:T(8,128)S(1)} %maximum_maximum_fusion.tab_ref, bf16[128,4224]{1,0:T(8,128)(2,1)} %collective-permute-done.1.buf_ref), custom_call_target="tpu_custom_call" | custom-call | flops 6039797760 | bytes 79626240 | tf_op jit(solution)/shard_map/dispatch/pallas_call | solution.py:262
  61.6 3.6 %all-to-all-start.3 = ((bf16[8,24,4096]{2,1,0:T(8,128)(2,1)}), bf16[8,24,4096]{2,1,0:T(8,128)(2,1)S(1)}, u32[]{:S(2)}, u32[]{:S(2)}) async-start(bf16[8,24,4096]{2,1,0:T(8,128)(2,1)} %dispatch.6), calls=%async_computation.3 | async-start | bytes 3145728 | tf_op jit(solution)/shard_map/all_to_all | solution.py:348
  65.2 0.1 broadcast_in_dim.27
  65.2 0.1 convert_element_type.52
  65.3 0.5 collective-permute-start.7
  65.8 0.1 maximum_maximum_fusion.1.tab_ref
  65.9 10.7 %expert.5 = (bf16[48,4096]{1,0:T(8,128)(2,1)}, bf16[48,4096]{1,0:T(8,128)(2,1)}, bf16[48,4096]{1,0:T(8,128)(2,1)}, bf16[48,4096]{1,0:T(8,128)(2,1)}, bf16[192,40...) custom-call(s32[1]{0:T(128)} %bitcast.2.me_ref, ...), custom_call_target="tpu_custom_call" | custom-call | flops 3623878656 | bytes 15728640 | tf_op jit(solution)/shard_map/expert/pallas_call | solution.py:285
  76.6 1.7 collective-permute-start.4
  78.3 1.5 collective-permute-start.5
  79.8 0.3 collective-permute-start.6
  80.1 4.4 %collective-permute-done.2.buf_ref = bf16[128,4224]{1,0:T(8,128)(2,1)} collective-permute-done((bf16[128,4224]{1,0:T(8,128)(2,1)}, bf16[128,4224]{1,0:T(8,128)(2,1)}, u32[]{:S(2)}, u32[]{:S(2)}) %collective-permute-start.2) | collective-permute-done | bytes 1081376 | tf_op jit(solution)/shard_map/ppermute | solution.py:338
  84.5 3.2 %dispatch.7 = bf16[8,24,4096]{2,1,0:T(8,128)(2,1)} custom-call(f32[8,192]{1,0:T(8,128)S(1)} %maximum_maximum_fusion.tab_ref, bf16[128,4224]{1,0:T(8,128)(2,1)} %collective-permute-done.2.buf_ref), custom_call_target="tpu_custom_call" | custom-call | flops 6039797760 | bytes 79626240 | tf_op jit(solution)/shard_map/dispatch/pallas_call | solution.py:262
  87.8 3.8 %all-to-all-start.2 = ((bf16[8,24,4096]{2,1,0:T(8,128)(2,1)}), bf16[8,24,4096]{2,1,0:T(8,128)(2,1)S(1)}, u32[]{:S(2)}, u32[]{:S(2)}) async-start(bf16[8,24,4096]{2,1,0:T(8,128)(2,1)} %dispatch.7), calls=%async_computation.2 | async-start | bytes 3145728 | tf_op jit(solution)/shard_map/all_to_all | solution.py:348
  91.5 0.0 collective-permute-done.7.buf_ref
  91.5 10.8 %expert.6 = (bf16[48,4096]{1,0:T(8,128)(2,1)}, bf16[48,4096]{1,0:T(8,128)(2,1)}, bf16[48,4096]{1,0:T(8,128)(2,1)}, bf16[48,4096]{1,0:T(8,128)(2,1)}, bf16[192,40...) custom-call(s32[1]{0:T(128)} %bitcast.2.me_ref, ...), custom_call_target="tpu_custom_call" | custom-call | flops 3623878656 | bytes 15728640 | tf_op jit(solution)/shard_map/expert/pallas_call | solution.py:285
  102.3 0.0 collective-permute-done.4.refs_1_
  102.3 0.0 collective-permute-done.5.refs_2_
  102.4 1.3 collective-permute-done.6.refs_3_
  103.6 2.8 %combine.6 = bf16[128,4224]{1,0:T(8,128)(2,1)S(1)} custom-call(f32[8,96]{1,0:T(8,128)S(1)} %maximum_maximum_fusion.1.tab_ref, bf16[128,4224]{1,0:T(8,128)(2,1)} %collective-permute-done.3.buf_ref, bf16[48,4096]{1,0:T(8,128)(2,1)S(1)} %copy-done, bf16[48,4096]{1,0:T(8,128)(2,1)S(1)} %collective-permute-done.4.refs_1_, ...), custom_call_target="tpu_custom_call" | custom-call | flops 503316480 | bytes 5898240 | tf_op jit(solution)/shard_map/combine/pallas_call | solution.py:310
  106.4 0.1 collective-permute-start.8
  106.5 0.7 collective-permute-start.9
  107.2 1.4 collective-permute-start.10
  108.6 1.4 collective-permute-start.11
  110.1 2.8 %combine.7.refs_0_ = bf16[128,4224]{1,0:T(8,128)(2,1)S(1)} custom-call(f32[8,96]{1,0:T(8,128)S(1)} %maximum_maximum_fusion.1.tab_ref, bf16[128,4224]{1,0:T(8,128)(2,1)} %collective-permute-done.buf_ref, bf16[48,4096]{1,0:T(8,128)(2,1)S(1)} %copy-done, bf16[48,4096]{1,0:T(8,128)(2,1)S(1)} %collective-permute-done.4.refs_1_, ...), custom_call_target="tpu_custom_call" | custom-call | flops 503316480 | bytes 5898240 | tf_op jit(solution)/shard_map/combine/pallas_call | solution.py:310
  112.9 1.2 join.4
  114.1 6.3 %all-to-all-done.2.rows_ref = bf16[8,24,4096]{2,1,0:T(8,128)(2,1)S(1)} async-done(((bf16[8,24,4096]{2,1,0:T(8,128)(2,1)}), bf16[8,24,4096]{2,1,0:T(8,128)(2,1)S(1)}, u32[]{:S(2)}, u32[]{:S(2)}) %all-to-all-start.2) | async-done | bytes 1572896 | tf_op jit(solution)/shard_map/all_to_all | solution.py:348
  120.5 10.7 %expert.7 = (bf16[8,24,4096]{2,1,0:T(8,128)(2,1)}, bf16[192,4096]{1,0:T(8,128)(2,1)}, bf16[192,768]{1,0:T(8,128)(2,1)}, bf16[192,768]{1,0:T(8,128)(2,1)}, bf16[192,768]{1,0:T(8,128)(2,1)}) custom-call(s32[1]{0:T(128)} %bitcast.2.me_ref, bf16[8,24,4096]{2,1,0:T(8,128)(2,1)S(1)} %all-to-all-done.2.rows_ref, bf16[1,2048,768]{2,1,0:T(8,128)(2,1)} %refs_0_.7, ...), custom_call_target="tpu_custom_call" | custom-call | flops 3623878656 | bytes 15728640 | tf_op jit(solution)/shard_map/expert/pallas_call | solution.py:285
  131.1 0.0 collective-permute-done.10.refs_2_
  131.1 5.8 %collective-permute-done.11.refs_3_ = bf16[48,4096]{1,0:T(8,128)(2,1)} collective-permute-done((bf16[48,4096]{1,0:T(8,128)(2,1)}, bf16[48,4096]{1,0:T(8,128)(2,1)}, u32[]{:S(2)}, u32[]{:S(2)}) %collective-permute-start.11) | collective-permute-done | bytes 393248 | tf_op jit(solution)/shard_map/ppermute | solution.py:279
  136.9 3.6 %all-to-all-start.4 = ((bf16[8,24,4096]{2,1,0:T(8,128)(2,1)}), bf16[8,24,4096]{2,1,0:T(8,128)(2,1)S(1)}, u32[]{:S(2)}, u32[]{:S(2)}) async-start(bf16[8,24,4096]{2,1,0:T(8,128)(2,1)} %get-tuple-element.116), calls=%async_computation.4 | async-start | bytes 3145728 | tf_op jit(solution)/shard_map/all_to_all | solution.py:348
  140.5 2.8 %combine.8 = bf16[128,4224]{1,0:T(8,128)(2,1)S(1)} custom-call(f32[8,96]{1,0:T(8,128)S(1)} %maximum_maximum_fusion.1.tab_ref, bf16[128,4224]{1,0:T(8,128)(2,1)} %collective-permute-done.7.buf_ref, bf16[48,4096]{1,0:T(8,128)(2,1)S(1)} %copy-done.3, bf16[48,4096]{1,0:T(8,128)(2,1)S(1)} %collective-permute-done.9.refs_1_, ...), custom_call_target="tpu_custom_call" | custom-call | flops 50331648000 | bytes 589824000 | tf_op jit(solution)/shard_map/combine/pallas_call | solution.py:310
  143.4 0.5 collective-permute-start.13
  143.8 2.8 %combine.9.refs_0_ = bf16[128,4224]{1,0:T(8,128)(2,1)S(1)} custom-call(f32[8,96]{1,0:T(8,128)S(1)} %maximum_maximum_fusion.1.tab_ref, bf16[128,4224]{1,0:T(8,128)(2,1)} %collective-permute-done.1.buf_ref, bf16[48,4096]{1,0:T(8,128)(2,1)S(1)} %copy-done.3, bf16[48,4096]{1,0:T(8,128)(2,1)S(1)} %collective-permute-done.9.refs_1_, ...), custom_call_target="tpu_custom_call" | custom-call | flops 503316480 | bytes 5898240 | tf_op jit(solution)/shard_map/combine/pallas_call | solution.py:310
  146.6 0.0 collective-permute-done.13.refs_1_
  146.7 2.4 %join.5 = (bf16[128,2048]{1,0:T(8,128)(2,1)}, bf16[128,2176]{1,0:T(8,128)(2,1)}) custom-call(bf16[128,4224]{1,0:T(8,128)(2,1)S(1)} %combine.9.refs_0_, bf16[128,4224]{1,0:T(8,128)(2,1)S(1)} %collective-permute-done.13.refs_1_, bf16[128,4224]{1,0:T(8,128)(2,1)} %collective-permute-done.12.refs_2_), custom_call_target="tpu_custom_call" | custom-call | flops 1622016 | bytes 4325376 | tf_op jit(solution)/shard_map/join/pallas_call | solution.py:325
  149.1 0.0 collective-permute-start.14
  149.1 1.0 collective-permute-start.16
  150.0 11.4 %all-to-all-done.4.refs_0_ = bf16[8,24,4096]{2,1,0:T(8,128)(2,1)S(1)} async-done(((bf16[8,24,4096]{2,1,0:T(8,128)(2,1)}), bf16[8,24,4096]{2,1,0:T(8,128)(2,1)S(1)}, u32[]{:S(2)}, u32[]{:S(2)}) %all-to-all-start.4) | async-done | bytes 1572896 | tf_op jit(solution)/shard_map/all_to_all | solution.py:348
  161.5 2.7 %combine.10.refs_0_ = bf16[128,4224]{1,0:T(8,128)(2,1)S(1)} custom-call(f32[8,192]{1,0:T(8,128)S(1)} %maximum_maximum_fusion.tab_ref, bf16[128,4224]{1,0:T(8,128)(2,1)} %collective-permute-done.2.buf_ref, bf16[8,24,4096]{2,1,0:T(8,128)(2,1)S(1)} %all-to-all-done.4.refs_0_), custom_call_target="tpu_custom_call" | custom-call | flops 50331648000 | bytes 589824000 | tf_op jit(solution)/shard_map/combine/pallas_call | solution.py:310
  164.2 4.5 %all-to-all-start.5 = ((bf16[8,24,4096]{2,1,0:T(8,128)(2,1)}), bf16[8,24,4096]{2,1,0:T(8,128)(2,1)}, u32[]{:S(2)}, u32[]{:S(2)}) async-start(bf16[8,24,4096]{2,1,0:T(8,128)(2,1)} %get-tuple-element.131), calls=%async_computation.5 | async-start | bytes 3145728 | tf_op jit(solution)/shard_map/all_to_all | solution.py:348
  168.8 2.0 join.6
  170.7 7.0 %collective-permute-done.16.refs_1_ = bf16[128,2176]{1,0:T(8,128)(2,1)S(1)} collective-permute-done((bf16[128,2176]{1,0:T(8,128)(2,1)}, bf16[128,2176]{1,0:T(8,128)(2,1)S(1)}, u32[]{:S(2)}, u32[]{:S(2)}) %collective-permute-start.16) | collective-permute-done | bytes 557088 | tf_op jit(solution)/shard_map/ppermute | solution.py:338
  177.8 1.0 join.7
  178.8 15.4 %weight_grads.1 = (bf16[1,2048,768]{2,1,0:T(8,128)(2,1)}, bf16[1,2048,768]{2,1,0:T(8,128)(2,1)}, bf16[1,768,2048]{2,1,0:T(8,128)(2,1)}) custom-call(bf16[192,4096]{1,0:T(8,128)(2,1)} %get-tuple-element.137.refs_0_.refs_4_, bf16[192,4096]{1,0:T(8,128)(2,1)} %get-tuple-element.142.refs_1_.refs_5_, bf16[192,4096]{1,0:T(8,128)(2,1)} %get-tuple-element.147.refs_2_.refs_6_, ...), custom_call_target="tpu_custom_call" | custom-call | flops 144955146240 | bytes 314572800 | tf_op jit(solution)/shard_map/weight_grads/pallas_call | solution.py:413
  194.1 2.9 %combine.11.share_ref = bf16[128,4224]{1,0:T(8,128)(2,1)S(1)} custom-call(f32[8,192]{1,0:T(8,128)S(1)} %maximum_maximum_fusion.tab_ref, bf16[128,4224]{1,0:T(8,128)(2,1)S(1)} %copy-done.2, bf16[8,24,4096]{2,1,0:T(8,128)(2,1)} %all-to-all-done.5.refs_0_), custom_call_target="tpu_custom_call" | custom-call | flops 50331648000 | bytes 589824000 | tf_op jit(solution)/shard_map/combine/pallas_call | solution.py:310
  197.0 2.0 final_left.1
  199.0 1.5 collective-permute-done.17.sum_ref
  200.5 2.1 %final_right.1 = (bf16[128,2048]{1,0:T(8,128)(2,1)}, f32[4,128]{1,0:T(4,128)}) custom-call(bf16[128,2176]{1,0:T(8,128)(2,1)} %collective-permute-done.17.sum_ref, bf16[128,4224]{1,0:T(8,128)(2,1)S(1)} %combine.11.share_ref), custom_call_target="tpu_custom_call" | custom-call | flops 540672 | bytes 1622016 | tf_op jit(solution)/shard_map/final_right/pallas_call | solution.py:450
  (26 shorter events, 0.1 us)
Async XLA Ops:
  2.0 5.4 %copy-start.1 = (bf16[128,4224]{1,0:T(8,128)(2,1)}, bf16[128,4224]{1,0:T(8,128)(2,1)S(1)}, u32[]{:S(2)}) copy-start(bf16[128,4224]{1,0:T(8,128)(2,1)S(1)} %pack.1.buf_ref) | copy-start | bytes 3244036
  2.0 29.1 %collective-permute-start = (bf16[128,4224]{1,0:T(8,128)(2,1)S(1)}, bf16[128,4224]{1,0:T(8,128)(2,1)}, u32[]{:S(2)}, u32[]{:S(2)}) collective-permute-start(bf16[128,4224]{1,0:T(8,128)(2,1)S(1)} %pack.1.buf_ref), channel_id=1, source_target_pairs={{0,8},{8,16},{16,24},{24,0},{1,9},{9,17},{17,25},{25,1},{2,10},{10... | collective-permute-start | bytes 3244040 | tf_op jit(solution)/shard_map/ppermute | solution.py:338
  7.5 26.9 %all-to-all-start = ((bf16[8,24,4096]{2,1,0:T(8,128)(2,1)}), bf16[8,24,4096]{2,1,0:T(8,128)(2,1)S(1)}, u32[]{:S(2)}, u32[]{:S(2)}) async-start(bf16[8,24,4096]{2,1,0:T(8,128)(2,1)} %dispatch.4), calls=%async_computation | async-start | bytes 3145728 | tf_op jit(solution)/shard_map/all_to_all | solution.py:348
  31.1 27.2 %collective-permute-start.1 = (bf16[128,4224]{1,0:T(8,128)(2,1)}, bf16[128,4224]{1,0:T(8,128)(2,1)}, u32[]{:S(2)}, u32[]{:S(2)}) collective-permute-start(bf16[128,4224]{1,0:T(8,128)(2,1)} %collective-permute-done.buf_ref), channel_id=1, source_target_pairs={{0,8},{8,16},{16,24},{24,0},{1,9},{9,17},{17,25},{25,1},{2,10},{10... | collective-permute-start | bytes 3244040 | tf_op jit(solution)/shard_map/ppermute | solution.py:338
  34.4 27.2 %all-to-all-start.1 = ((bf16[8,24,4096]{2,1,0:T(8,128)(2,1)}), bf16[8,24,4096]{2,1,0:T(8,128)(2,1)S(1)}, u32[]{:S(2)}, u32[]{:S(2)}) async-start(bf16[8,24,4096]{2,1,0:T(8,128)(2,1)} %dispatch.5), calls=%async_computation.1 | async-start | bytes 3145728 | tf_op jit(solution)/shard_map/all_to_all | solution.py:348
  38.1 27.8 %collective-permute-start.3 = (bf16[128,4224]{1,0:T(8,128)(2,1)}, bf16[128,4224]{1,0:T(8,128)(2,1)}, u32[]{:S(2)}, u32[]{:S(2)}) collective-permute-start(bf16[128,4224]{1,0:T(8,128)(2,1)} %collective-permute-done.buf_ref), channel_id=1, source_target_pairs={{0,1},{1,0},{2,3},{3,2},{4,5},{5,4},{6,7},{7,6},{8,9},{9,8},{10,11... | collective-permute-start | bytes 3244040 | tf_op jit(solution)/shard_map/ppermute | solution.py:275
  58.3 26.2 %collective-permute-start.2 = (bf16[128,4224]{1,0:T(8,128)(2,1)}, bf16[128,4224]{1,0:T(8,128)(2,1)}, u32[]{:S(2)}, u32[]{:S(2)}) collective-permute-start(bf16[128,4224]{1,0:T(8,128)(2,1)} %collective-permute-done.1.buf_ref), channel_id=1, source_target_pairs={{0,8},{8,16},{16,24},{24,0},{1,9},{9,17},{17,25},{25,1},{2,10},{10... | collective-permute-start | bytes 3244040 | tf_op jit(solution)/shard_map/ppermute | solution.py:338
  61.6 26.2 %all-to-all-start.3 = ((bf16[8,24,4096]{2,1,0:T(8,128)(2,1)}), bf16[8,24,4096]{2,1,0:T(8,128)(2,1)S(1)}, u32[]{:S(2)}, u32[]{:S(2)}) async-start(bf16[8,24,4096]{2,1,0:T(8,128)(2,1)} %dispatch.6), calls=%async_computation.3 | async-start | bytes 3145728 | tf_op jit(solution)/shard_map/all_to_all | solution.py:348
  65.3 26.2 %collective-permute-start.7 = (bf16[128,4224]{1,0:T(8,128)(2,1)}, bf16[128,4224]{1,0:T(8,128)(2,1)}, u32[]{:S(2)}, u32[]{:S(2)}) collective-permute-start(bf16[128,4224]{1,0:T(8,128)(2,1)} %collective-permute-done.1.buf_ref), channel_id=1, source_target_pairs={{0,1},{1,0},{2,3},{3,2},{4,5},{5,4},{6,7},{7,6},{8,9},{9,8},{10,11... | collective-permute-start | bytes 3244040 | tf_op jit(solution)/shard_map/ppermute | solution.py:275
  76.6 25.8 %collective-permute-start.4 = (bf16[48,4096]{1,0:T(8,128)(2,1)}, bf16[48,4096]{1,0:T(8,128)(2,1)S(1)}, u32[]{:S(2)}, u32[]{:S(2)}) collective-permute-start(bf16[48,4096]{1,0:T(8,128)(2,1)} %get-tuple-element.101), channel_id=1, source_target_pairs={{0,2},{1,3},{2,0},{3,1},{4,6},{5,7},{6,4},{7,5},{8,10},{9,11},{10,... | collective-permute-start | bytes 1179656 | tf_op jit(solution)/shard_map/ppermute | solution.py:279
  78.3 24.0 %collective-permute-start.5 = (bf16[48,4096]{1,0:T(8,128)(2,1)}, bf16[48,4096]{1,0:T(8,128)(2,1)}, u32[]{:S(2)}, u32[]{:S(2)}) collective-permute-start(bf16[48,4096]{1,0:T(8,128)(2,1)} %get-tuple-element.102), channel_id=1, source_target_pairs={{0,4},{1,5},{2,6},{3,7},{4,0},{5,1},{6,2},{7,3},{8,12},{9,13},{10,... | collective-permute-start | bytes 1179656 | tf_op jit(solution)/shard_map/ppermute | solution.py:279
  79.8 23.8 %collective-permute-start.6 = (bf16[48,4096]{1,0:T(8,128)(2,1)}, bf16[48,4096]{1,0:T(8,128)(2,1)}, u32[]{:S(2)}, u32[]{:S(2)}) collective-permute-start(bf16[48,4096]{1,0:T(8,128)(2,1)} %get-tuple-element.103), channel_id=1, source_target_pairs={{0,6},{1,7},{2,4},{3,5},{4,2},{5,3},{6,0},{7,1},{8,14},{9,15},{10,... | collective-permute-start | bytes 1179656 | tf_op jit(solution)/shard_map/ppermute | solution.py:279
  87.8 32.7 %all-to-all-start.2 = ((bf16[8,24,4096]{2,1,0:T(8,128)(2,1)}), bf16[8,24,4096]{2,1,0:T(8,128)(2,1)S(1)}, u32[]{:S(2)}, u32[]{:S(2)}) async-start(bf16[8,24,4096]{2,1,0:T(8,128)(2,1)} %dispatch.7), calls=%async_computation.2 | async-start | bytes 3145728 | tf_op jit(solution)/shard_map/all_to_all | solution.py:348
  91.5 12.1 %copy-start = (bf16[48,4096]{1,0:T(8,128)(2,1)S(1)}, bf16[48,4096]{1,0:T(8,128)(2,1)}, u32[]{:S(2)}) copy-start(bf16[48,4096]{1,0:T(8,128)(2,1)} %get-tuple-element.110.refs_0_) | copy-start | bytes 1179652
  106.4 6.5 %collective-permute-start.8 = (bf16[128,4224]{1,0:T(8,128)(2,1)S(1)}, bf16[128,4224]{1,0:T(8,128)(2,1)S(1)}, u32[]{:S(2)}, u32[]{:S(2)}) collective-permute-start(bf16[128,4224]{1,0:T(8,128)(2,1)S(1)} %combine.6), channel_id=1, source_target_pairs={{0,1},{1,0},{2,3},{3,2},{4,5},{5,4},{6,7},{7,6},{8,9},{9,8},{10,11... | collective-permute-start | bytes 3244040 | tf_op jit(solution)/shard_map/ppermute | solution.py:275
  106.5 24.6 %collective-permute-start.9 = (bf16[48,4096]{1,0:T(8,128)(2,1)}, bf16[48,4096]{1,0:T(8,128)(2,1)S(1)}, u32[]{:S(2)}, u32[]{:S(2)}) collective-permute-start(bf16[48,4096]{1,0:T(8,128)(2,1)} %get-tuple-element.118), channel_id=1, source_target_pairs={{0,2},{1,3},{2,0},{3,1},{4,6},{5,7},{6,4},{7,5},{8,10},{9,11},{10,... | collective-permute-start | bytes 1179656 | tf_op jit(solution)/shard_map/ppermute | solution.py:279
  107.2 23.9 %collective-permute-start.10 = (bf16[48,4096]{1,0:T(8,128)(2,1)}, bf16[48,4096]{1,0:T(8,128)(2,1)}, u32[]{:S(2)}, u32[]{:S(2)}) collective-permute-start(bf16[48,4096]{1,0:T(8,128)(2,1)} %get-tuple-element.119), channel_id=1, source_target_pairs={{0,4},{1,5},{2,6},{3,7},{4,0},{5,1},{6,2},{7,3},{8,12},{9,13},{10,... | collective-permute-start | bytes 1179656 | tf_op jit(solution)/shard_map/ppermute | solution.py:279
  108.6 28.3 %collective-permute-start.11 = (bf16[48,4096]{1,0:T(8,128)(2,1)}, bf16[48,4096]{1,0:T(8,128)(2,1)}, u32[]{:S(2)}, u32[]{:S(2)}) collective-permute-start(bf16[48,4096]{1,0:T(8,128)(2,1)} %get-tuple-element.120), channel_id=1, source_target_pairs={{0,6},{1,7},{2,4},{3,5},{4,2},{5,3},{6,0},{7,1},{8,14},{9,15},{10,... | collective-permute-start | bytes 1179656 | tf_op jit(solution)/shard_map/ppermute | solution.py:279
  114.1 32.5 %collective-permute-start.12 = (bf16[128,4224]{1,0:T(8,128)(2,1)}, bf16[128,4224]{1,0:T(8,128)(2,1)}, u32[]{:S(2)}, u32[]{:S(2)}) collective-permute-start(bf16[128,4224]{1,0:T(8,128)(2,1)} %join.4), channel_id=1, source_target_pairs={{0,8},{8,16},{16,24},{24,0},{1,9},{9,17},{17,25},{25,1},{2,10},{10... | collective-permute-start | bytes 3244040 | tf_op jit(solution)/shard_map/ppermute | solution.py:338
  131.1 9.4 %copy-start.3 = (bf16[48,4096]{1,0:T(8,128)(2,1)S(1)}, bf16[48,4096]{1,0:T(8,128)(2,1)}, u32[]{:S(2)}) copy-start(bf16[48,4096]{1,0:T(8,128)(2,1)} %get-tuple-element.121.refs_0_) | copy-start | bytes 1179652
  136.9 24.5 %all-to-all-start.4 = ((bf16[8,24,4096]{2,1,0:T(8,128)(2,1)}), bf16[8,24,4096]{2,1,0:T(8,128)(2,1)S(1)}, u32[]{:S(2)}, u32[]{:S(2)}) async-start(bf16[8,24,4096]{2,1,0:T(8,128)(2,1)} %get-tuple-element.116), calls=%async_computation.4 | async-start | bytes 3145728 | tf_op jit(solution)/shard_map/all_to_all | solution.py:348
  143.4 3.3 %collective-permute-start.13 = (bf16[128,4224]{1,0:T(8,128)(2,1)S(1)}, bf16[128,4224]{1,0:T(8,128)(2,1)S(1)}, u32[]{:S(2)}, u32[]{:S(2)}) collective-permute-start(bf16[128,4224]{1,0:T(8,128)(2,1)S(1)} %combine.8), channel_id=1, source_target_pairs={{0,1},{1,0},{2,3},{3,2},{4,5},{5,4},{6,7},{7,6},{8,9},{9,8},{10,11... | collective-permute-start | bytes 3244040 | tf_op jit(solution)/shard_map/ppermute | solution.py:275
  149.1 19.7 %collective-permute-start.14 = (bf16[128,2048]{1,0:T(8,128)(2,1)}, bf16[128,2048]{1,0:T(8,128)(2,1)}, u32[]{:S(2)}, u32[]{:S(2)}) collective-permute-start(bf16[128,2048]{1,0:T(8,128)(2,1)} %get-tuple-element.127), channel_id=1, source_target_pairs={{0,8},{8,16},{16,24},{24,0},{1,9},{9,17},{17,25},{25,1},{2,10},{10... | collective-permute-start | bytes 1572872 | tf_op jit(solution)/shard_map/ppermute | solution.py:338
  149.1 28.7 %collective-permute-start.16 = (bf16[128,2176]{1,0:T(8,128)(2,1)}, bf16[128,2176]{1,0:T(8,128)(2,1)S(1)}, u32[]{:S(2)}, u32[]{:S(2)}) collective-permute-start(bf16[128,2176]{1,0:T(8,128)(2,1)} %get-tuple-element.128), channel_id=1, source_target_pairs={{0,8},{8,16},{16,24},{24,0},{1,9},{9,17},{17,25},{25,1},{2,10},{10... | collective-permute-start | bytes 1671176 | tf_op jit(solution)/shard_map/ppermute | solution.py:338
  164.2 29.9 %all-to-all-start.5 = ((bf16[8,24,4096]{2,1,0:T(8,128)(2,1)}), bf16[8,24,4096]{2,1,0:T(8,128)(2,1)}, u32[]{:S(2)}, u32[]{:S(2)}) async-start(bf16[8,24,4096]{2,1,0:T(8,128)(2,1)} %get-tuple-element.131), calls=%async_computation.5 | async-start | bytes 3145728 | tf_op jit(solution)/shard_map/all_to_all | solution.py:348
  170.7 26.3 %collective-permute-start.15 = (bf16[128,2048]{1,0:T(8,128)(2,1)}, bf16[128,2048]{1,0:T(8,128)(2,1)}, u32[]{:S(2)}, u32[]{:S(2)}) collective-permute-start(bf16[128,2048]{1,0:T(8,128)(2,1)} %join.6), channel_id=1, source_target_pairs={{0,8},{8,16},{16,24},{24,0},{1,9},{9,17},{17,25},{25,1},{2,10},{10... | collective-permute-start | bytes 1572872 | tf_op jit(solution)/shard_map/ppermute | solution.py:338
  178.8 21.8 %collective-permute-start.17 = (bf16[128,2176]{1,0:T(8,128)(2,1)}, bf16[128,2176]{1,0:T(8,128)(2,1)}, u32[]{:S(2)}, u32[]{:S(2)}) collective-permute-start(bf16[128,2176]{1,0:T(8,128)(2,1)} %join.7), channel_id=1, source_target_pairs={{0,8},{8,16},{16,24},{24,0},{1,9},{9,17},{17,25},{25,1},{2,10},{10... | collective-permute-start | bytes 1671176 | tf_op jit(solution)/shard_map/ppermute | solution.py:338
  178.8 15.4 %copy-start.2 = (bf16[128,4224]{1,0:T(8,128)(2,1)S(1)}, bf16[128,4224]{1,0:T(8,128)(2,1)}, u32[]{:S(2)}) copy-start(bf16[128,4224]{1,0:T(8,128)(2,1)} %copy-done.1) | copy-start | bytes 3244036

commit v6 on v5

--- a/solution.py
+++ b/solution.py
@@ -401,11 +401,12 @@
     joined = add_up([left, right], shares, sums)
     sums = [next_plane(v) for v in joined]
     shares = plane_sums(last, joined)
-    give_back(0, outs[last], shares)
     home = []
     for cut, arrived in zip((left, right), sums):
         leaving = add_up([cut], shares, [arrived])
         home.append(next_plane(leaving[0]))
+        if not outs.get(0):
+            give_back(0, outs[last], leaving)
     kept = [after(saved, leaving) for saved in kept]
     d_tile = 256
     d_steps = width // d_tile

time: 204 us -> 204 us (level)
  transfers between devices with their start and end apart: 24 -> 24, of which waited for: 9 -> 10; matrix products, arithmetic and copies ran while one was open for 0% -> 0% of each run, Pallas kernels for 47% -> 47%
where the time goes in v6:
time: 204 us; the launch traced here: 203 us
  Pallas kernels  98.9 us (48%)
  waiting for transfers between devices  66.9 us (33%)
  starting transfers between devices  35.3 us (17%)
    pallas_call x4, Pallas kernels, expert(): pl.pallas_call(functools.partial(expert_kernel, outs, width), grid=(steps...  42.8 us
    ppermute x8, waiting for transfers between devices, next_plane(): lax.ppermute(v, 'group', [(i, (i + 1) % groups) for i in range(groups)])  42 us
    all_to_all x6, starting transfers between devices, exchange(): return lax.all_to_all(v, 'local', split_axis=0, concat_axis=0, tiled=True)  22.7 us
    all_to_all x6, waiting for transfers between devices, exchange(): return lax.all_to_all(v, 'local', split_axis=0, concat_axis=0, tiled=True)  17.8 us
    pallas_call x6, Pallas kernels, combine(): pl.pallas_call(functools.partial(combine_kernel, lo_row, rows_p, top, wid...  16.8 us
    pallas_call x1, Pallas kernels, local(): pl.pallas_call(functools.partial(weight_grad_kernel, groups), grid=(d_ste...  15.4 us
    pallas_call x4, Pallas kernels, dispatch(): pl.pallas_call(functools.partial(dispatch_kernel, top, width), out_shape=...  11.8 us
    ppermute x6, starting transfers between devices, swap(): lax.ppermute(pieces[s], 'local', [(i, i ^ 2 * s) for i in range(count)])  7.11 us
  transfers between devices with their start and end apart: 24, of which 10 were waited for; matrix products, arithmetic and copies ran while one was open for 0% of the time, Pallas kernels for 47%

profile of v6, /device:TPU:0, one launch (start us, length us, event | category | flops | bytes accessed | tf_op | source)
XLA Modules:
  0.0 202.6 jit_solution(9773248987391205036)
XLA Ops:
  0.6 1.4 pack.1.buf_ref
  2.0 3.1 %collective-permute-start = (bf16[128,4224]{1,0:T(8,128)(2,1)S(1)}, bf16[128,4224]{1,0:T(8,128)(2,1)}, u32[]{:S(2)}, u32[]{:S(2)}) collective-permute-start(bf16[128,4224]{1,0:T(8,128)(2,1)S(1)} %pack.1.buf_ref), channel_id=1, source_target_pairs={{0,8},{8,16},{16,24},{24,0},{1,9},{9,17},{17,25},{25,1},{2,10},{10... | collective-permute-start | bytes 3244040 | tf_op jit(solution)/shard_map/ppermute | solution.py:338
  5.1 0.1 broadcast_in_dim.24
  5.2 0.1 convert_element_type.49
  5.3 0.1 pad.5.clone
  5.4 0.1 maximum_maximum_fusion.tab_ref
  5.4 2.0 dispatch.4
  7.5 3.7 %all-to-all-start = ((bf16[8,24,4096]{2,1,0:T(8,128)(2,1)}), bf16[8,24,4096]{2,1,0:T(8,128)(2,1)S(1)}, u32[]{:S(2)}, u32[]{:S(2)}) async-start(bf16[8,24,4096]{2,1,0:T(8,128)(2,1)} %dispatch.4), calls=%async_computation | async-start | bytes 3145728 | tf_op jit(solution)/shard_map/all_to_all | solution.py:348
  11.2 19.9 %collective-permute-done.buf_ref = bf16[128,4224]{1,0:T(8,128)(2,1)} collective-permute-done((bf16[128,4224]{1,0:T(8,128)(2,1)S(1)}, bf16[128,4224]{1,0:T(8,128)(2,1)}, u32[]{:S(2)}, u32[]{:S(2)}) %collective-permute-start) | collective-permute-done | bytes 1081376 | tf_op jit(solution)/shard_map/ppermute | solution.py:338
  31.1 3.3 %dispatch.5 = bf16[8,24,4096]{2,1,0:T(8,128)(2,1)} custom-call(f32[8,192]{1,0:T(8,128)S(1)} %maximum_maximum_fusion.tab_ref, bf16[128,4224]{1,0:T(8,128)(2,1)} %collective-permute-done.buf_ref), custom_call_target="tpu_custom_call" | custom-call | flops 6039797760 | bytes 79626240 | tf_op jit(solution)/shard_map/dispatch/pallas_call | solution.py:262
  34.4 0.0 all-to-all-done.rows_ref
  34.4 3.7 %all-to-all-start.1 = ((bf16[8,24,4096]{2,1,0:T(8,128)(2,1)}), bf16[8,24,4096]{2,1,0:T(8,128)(2,1)S(1)}, u32[]{:S(2)}, u32[]{:S(2)}) async-start(bf16[8,24,4096]{2,1,0:T(8,128)(2,1)} %dispatch.5), calls=%async_computation.1 | async-start | bytes 3145728 | tf_op jit(solution)/shard_map/all_to_all | solution.py:348
  38.1 0.5 collective-permute-start.3
  38.6 10.7 %expert.4 = (bf16[8,24,4096]{2,1,0:T(8,128)(2,1)}, bf16[192,4096]{1,0:T(8,128)(2,1)}, bf16[192,768]{1,0:T(8,128)(2,1)}, bf16[192,768]{1,0:T(8,128)(2,1)}, bf16[192,768]{1,0:T(8,128)(2,1)}) custom-call(s32[1]{0:T(128)} %bitcast.2.me_ref, bf16[8,24,4096]{2,1,0:T(8,128)(2,1)S(1)} %all-to-all-done.rows_ref, bf16[1,2048,768]{2,1,0:T(8,128)(2,1)} %refs_0_.7, ...), custom_call_target="tpu_custom_call" | custom-call | flops 3623878656 | bytes 15728640 | tf_op jit(solution)/shard_map/expert/pallas_call | solution.py:285
  49.3 9.0 %collective-permute-done.1.buf_ref = bf16[128,4224]{1,0:T(8,128)(2,1)} collective-permute-done((bf16[128,4224]{1,0:T(8,128)(2,1)}, bf16[128,4224]{1,0:T(8,128)(2,1)}, u32[]{:S(2)}, u32[]{:S(2)}) %collective-permute-start.1) | collective-permute-done | bytes 1081376 | tf_op jit(solution)/shard_map/ppermute | solution.py:338
  58.3 3.3 %dispatch.6 = bf16[8,24,4096]{2,1,0:T(8,128)(2,1)} custom-call(f32[8,192]{1,0:T(8,128)S(1)} %maximum_maximum_fusion.tab_ref, bf16[128,4224]{1,0:T(8,128)(2,1)} %collective-permute-done.1.buf_ref), custom_call_target="tpu_custom_call" | custom-call | flops 6039797760 | bytes 79626240 | tf_op jit(solution)/shard_map/dispatch/pallas_call | solution.py:262
  61.6 3.6 %all-to-all-start.3 = ((bf16[8,24,4096]{2,1,0:T(8,128)(2,1)}), bf16[8,24,4096]{2,1,0:T(8,128)(2,1)S(1)}, u32[]{:S(2)}, u32[]{:S(2)}) async-start(bf16[8,24,4096]{2,1,0:T(8,128)(2,1)} %dispatch.6), calls=%async_computation.3 | async-start | bytes 3145728 | tf_op jit(solution)/shard_map/all_to_all | solution.py:348
  65.2 0.1 broadcast_in_dim.27
  65.2 0.1 convert_element_type.52
  65.3 0.5 collective-permute-start.7
  65.8 0.1 maximum_maximum_fusion.1.tab_ref
  65.9 10.7 %expert.5 = (bf16[48,4096]{1,0:T(8,128)(2,1)}, bf16[48,4096]{1,0:T(8,128)(2,1)}, bf16[48,4096]{1,0:T(8,128)(2,1)}, bf16[48,4096]{1,0:T(8,128)(2,1)}, bf16[192,40...) custom-call(s32[1]{0:T(128)} %bitcast.2.me_ref, ...), custom_call_target="tpu_custom_call" | custom-call | flops 3623878656 | bytes 15728640 | tf_op jit(solution)/shard_map/expert/pallas_call | solution.py:285
  76.6 1.7 collective-permute-start.4
  78.3 1.5 collective-permute-start.5
  79.8 0.3 collective-permute-start.6
  80.1 4.4 %collective-permute-done.2.buf_ref = bf16[128,4224]{1,0:T(8,128)(2,1)} collective-permute-done((bf16[128,4224]{1,0:T(8,128)(2,1)}, bf16[128,4224]{1,0:T(8,128)(2,1)}, u32[]{:S(2)}, u32[]{:S(2)}) %collective-permute-start.2) | collective-permute-done | bytes 1081376 | tf_op jit(solution)/shard_map/ppermute | solution.py:338
  84.5 3.2 %dispatch.7 = bf16[8,24,4096]{2,1,0:T(8,128)(2,1)} custom-call(f32[8,192]{1,0:T(8,128)S(1)} %maximum_maximum_fusion.tab_ref, bf16[128,4224]{1,0:T(8,128)(2,1)} %collective-permute-done.2.buf_ref), custom_call_target="tpu_custom_call" | custom-call | flops 6039797760 | bytes 79626240 | tf_op jit(solution)/shard_map/dispatch/pallas_call | solution.py:262
  87.8 3.8 %all-to-all-start.2 = ((bf16[8,24,4096]{2,1,0:T(8,128)(2,1)}), bf16[8,24,4096]{2,1,0:T(8,128)(2,1)S(1)}, u32[]{:S(2)}, u32[]{:S(2)}) async-start(bf16[8,24,4096]{2,1,0:T(8,128)(2,1)} %dispatch.7), calls=%async_computation.2 | async-start | bytes 3145728 | tf_op jit(solution)/shard_map/all_to_all | solution.py:348
  91.5 0.0 collective-permute-done.7.buf_ref
  91.5 10.8 %expert.6 = (bf16[48,4096]{1,0:T(8,128)(2,1)}, bf16[48,4096]{1,0:T(8,128)(2,1)}, bf16[48,4096]{1,0:T(8,128)(2,1)}, bf16[48,4096]{1,0:T(8,128)(2,1)}, bf16[192,40...) custom-call(s32[1]{0:T(128)} %bitcast.2.me_ref, ...), custom_call_target="tpu_custom_call" | custom-call | flops 3623878656 | bytes 15728640 | tf_op jit(solution)/shard_map/expert/pallas_call | solution.py:285
  102.3 0.0 collective-permute-done.4.refs_1_
  102.3 0.0 collective-permute-done.5.refs_2_
  102.4 1.3 collective-permute-done.6.refs_3_
  103.6 2.8 %combine.6 = bf16[128,4224]{1,0:T(8,128)(2,1)S(1)} custom-call(f32[8,96]{1,0:T(8,128)S(1)} %maximum_maximum_fusion.1.tab_ref, bf16[128,4224]{1,0:T(8,128)(2,1)} %collective-permute-done.3.buf_ref, bf16[48,4096]{1,0:T(8,128)(2,1)S(1)} %copy-done, bf16[48,4096]{1,0:T(8,128)(2,1)S(1)} %collective-permute-done.4.refs_1_, ...), custom_call_target="tpu_custom_call" | custom-call | flops 503316480 | bytes 5898240 | tf_op jit(solution)/shard_map/combine/pallas_call | solution.py:310
  106.4 0.1 collective-permute-start.8
  106.5 0.7 collective-permute-start.9
  107.2 1.4 collective-permute-start.10
  108.6 1.4 collective-permute-start.11
  110.1 2.8 %combine.7.refs_0_ = bf16[128,4224]{1,0:T(8,128)(2,1)S(1)} custom-call(f32[8,96]{1,0:T(8,128)S(1)} %maximum_maximum_fusion.1.tab_ref, bf16[128,4224]{1,0:T(8,128)(2,1)} %collective-permute-done.buf_ref, bf16[48,4096]{1,0:T(8,128)(2,1)S(1)} %copy-done, bf16[48,4096]{1,0:T(8,128)(2,1)S(1)} %collective-permute-done.4.refs_1_, ...), custom_call_target="tpu_custom_call" | custom-call | flops 503316480 | bytes 5898240 | tf_op jit(solution)/shard_map/combine/pallas_call | solution.py:310
  112.9 0.0 collective-permute-done.8.refs_1_
  112.9 1.2 join.4
  114.1 0.0 collective-permute-start.12
  114.1 6.3 %all-to-all-done.2.rows_ref = bf16[8,24,4096]{2,1,0:T(8,128)(2,1)S(1)} async-done(((bf16[8,24,4096]{2,1,0:T(8,128)(2,1)}), bf16[8,24,4096]{2,1,0:T(8,128)(2,1)S(1)}, u32[]{:S(2)}, u32[]{:S(2)}) %all-to-all-start.2) | async-done | bytes 1572896 | tf_op jit(solution)/shard_map/all_to_all | solution.py:348
  120.5 10.7 %expert.7 = (bf16[8,24,4096]{2,1,0:T(8,128)(2,1)}, bf16[192,4096]{1,0:T(8,128)(2,1)}, bf16[192,768]{1,0:T(8,128)(2,1)}, bf16[192,768]{1,0:T(8,128)(2,1)}, bf16[192,768]{1,0:T(8,128)(2,1)}) custom-call(s32[1]{0:T(128)} %bitcast.2.me_ref, bf16[8,24,4096]{2,1,0:T(8,128)(2,1)S(1)} %all-to-all-done.2.rows_ref, bf16[1,2048,768]{2,1,0:T(8,128)(2,1)} %refs_0_.7, ...), custom_call_target="tpu_custom_call" | custom-call | flops 3623878656 | bytes 15728640 | tf_op jit(solution)/shard_map/expert/pallas_call | solution.py:285
  131.1 5.8 %collective-permute-done.11.refs_3_ = bf16[48,4096]{1,0:T(8,128)(2,1)} collective-permute-done((bf16[48,4096]{1,0:T(8,128)(2,1)}, bf16[48,4096]{1,0:T(8,128)(2,1)}, u32[]{:S(2)}, u32[]{:S(2)}) %collective-permute-start.11) | collective-permute-done | bytes 393248 | tf_op jit(solution)/shard_map/ppermute | solution.py:279
  136.9 3.6 %all-to-all-start.4 = ((bf16[8,24,4096]{2,1,0:T(8,128)(2,1)}), bf16[8,24,4096]{2,1,0:T(8,128)(2,1)S(1)}, u32[]{:S(2)}, u32[]{:S(2)}) async-start(bf16[8,24,4096]{2,1,0:T(8,128)(2,1)} %get-tuple-element.116), calls=%async_computation.4 | async-start | bytes 3145728 | tf_op jit(solution)/shard_map/all_to_all | solution.py:348
  140.5 2.8 %combine.8 = bf16[128,4224]{1,0:T(8,128)(2,1)S(1)} custom-call(f32[8,96]{1,0:T(8,128)S(1)} %maximum_maximum_fusion.1.tab_ref, bf16[128,4224]{1,0:T(8,128)(2,1)} %collective-permute-done.7.buf_ref, bf16[48,4096]{1,0:T(8,128)(2,1)S(1)} %copy-done.3, bf16[48,4096]{1,0:T(8,128)(2,1)S(1)} %collective-permute-done.9.refs_1_, ...), custom_call_target="tpu_custom_call" | custom-call | flops 50331648000 | bytes 589824000 | tf_op jit(solution)/shard_map/combine/pallas_call | solution.py:310
  143.4 0.5 collective-permute-start.13
  143.8 2.8 %combine.9.refs_0_ = bf16[128,4224]{1,0:T(8,128)(2,1)S(1)} custom-call(f32[8,96]{1,0:T(8,128)S(1)} %maximum_maximum_fusion.1.tab_ref, bf16[128,4224]{1,0:T(8,128)(2,1)} %collective-permute-done.1.buf_ref, bf16[48,4096]{1,0:T(8,128)(2,1)S(1)} %copy-done.3, bf16[48,4096]{1,0:T(8,128)(2,1)S(1)} %collective-permute-done.9.refs_1_, ...), custom_call_target="tpu_custom_call" | custom-call | flops 503316480 | bytes 5898240 | tf_op jit(solution)/shard_map/combine/pallas_call | solution.py:310
  146.7 2.4 %join.5 = (bf16[128,2048]{1,0:T(8,128)(2,1)}, bf16[128,2176]{1,0:T(8,128)(2,1)}) custom-call(bf16[128,4224]{1,0:T(8,128)(2,1)S(1)} %combine.9.refs_0_, bf16[128,4224]{1,0:T(8,128)(2,1)S(1)} %collective-permute-done.13.refs_1_, bf16[128,4224]{1,0:T(8,128)(2,1)} %collective-permute-done.12.refs_2_), custom_call_target="tpu_custom_call" | custom-call | flops 1622016 | bytes 4325376 | tf_op jit(solution)/shard_map/join/pallas_call | solution.py:325
  149.1 1.0 collective-permute-start.16
  150.0 11.4 %all-to-all-done.4.refs_0_ = bf16[8,24,4096]{2,1,0:T(8,128)(2,1)S(1)} async-done(((bf16[8,24,4096]{2,1,0:T(8,128)(2,1)}), bf16[8,24,4096]{2,1,0:T(8,128)(2,1)S(1)}, u32[]{:S(2)}, u32[]{:S(2)}) %all-to-all-start.4) | async-done | bytes 1572896 | tf_op jit(solution)/shard_map/all_to_all | solution.py:348
  161.5 2.7 %combine.10.refs_0_ = bf16[128,4224]{1,0:T(8,128)(2,1)S(1)} custom-call(f32[8,192]{1,0:T(8,128)S(1)} %maximum_maximum_fusion.tab_ref, bf16[128,4224]{1,0:T(8,128)(2,1)} %collective-permute-done.2.buf_ref, bf16[8,24,4096]{2,1,0:T(8,128)(2,1)S(1)} %all-to-all-done.4.refs_0_), custom_call_target="tpu_custom_call" | custom-call | flops 50331648000 | bytes 589824000 | tf_op jit(solution)/shard_map/combine/pallas_call | solution.py:310
  164.2 1.7 collective-permute-done.14.refs_1_
  165.9 2.0 join.6
  167.9 0.0 collective-permute-start.15
  167.9 4.3 %all-to-all-start.5 = ((bf16[8,24,4096]{2,1,0:T(8,128)(2,1)}), bf16[8,24,4096]{2,1,0:T(8,128)(2,1)}, u32[]{:S(2)}, u32[]{:S(2)}) async-start(bf16[8,24,4096]{2,1,0:T(8,128)(2,1)} %get-tuple-element.131), calls=%async_computation.5 | async-start | bytes 3145728 | tf_op jit(solution)/shard_map/all_to_all | solution.py:348
  172.2 5.5 %collective-permute-done.16.refs_1_ = bf16[128,2176]{1,0:T(8,128)(2,1)S(1)} collective-permute-done((bf16[128,2176]{1,0:T(8,128)(2,1)}, bf16[128,2176]{1,0:T(8,128)(2,1)S(1)}, u32[]{:S(2)}, u32[]{:S(2)}) %collective-permute-start.16) | collective-permute-done | bytes 557088 | tf_op jit(solution)/shard_map/ppermute | solution.py:338
  177.8 1.0 join.7
  178.8 15.4 %weight_grads.1 = (bf16[1,2048,768]{2,1,0:T(8,128)(2,1)}, bf16[1,2048,768]{2,1,0:T(8,128)(2,1)}, bf16[1,768,2048]{2,1,0:T(8,128)(2,1)}) custom-call(bf16[192,4096]{1,0:T(8,128)(2,1)} %get-tuple-element.137.refs_0_.refs_4_, bf16[192,4096]{1,0:T(8,128)(2,1)} %get-tuple-element.142.refs_1_.refs_5_, bf16[192,4096]{1,0:T(8,128)(2,1)} %get-tuple-element.147.refs_2_.refs_6_, ...), custom_call_target="tpu_custom_call" | custom-call | flops 144955146240 | bytes 314572800 | tf_op jit(solution)/shard_map/weight_grads/pallas_call | solution.py:414
  194.2 2.9 %combine.11.share_ref = bf16[128,4224]{1,0:T(8,128)(2,1)S(1)} custom-call(f32[8,192]{1,0:T(8,128)S(1)} %maximum_maximum_fusion.tab_ref, bf16[128,4224]{1,0:T(8,128)(2,1)S(1)} %copy-done.2, bf16[8,24,4096]{2,1,0:T(8,128)(2,1)} %all-to-all-done.5.refs_0_), custom_call_target="tpu_custom_call" | custom-call | flops 50331648000 | bytes 589824000 | tf_op jit(solution)/shard_map/combine/pallas_call | solution.py:310
  197.1 2.0 final_left.1
  199.0 1.5 collective-permute-done.17.sum_ref
  200.5 2.1 %final_right.1 = (bf16[128,2048]{1,0:T(8,128)(2,1)}, f32[4,128]{1,0:T(4,128)}) custom-call(bf16[128,2176]{1,0:T(8,128)(2,1)} %collective-permute-done.17.sum_ref, bf16[128,4224]{1,0:T(8,128)(2,1)S(1)} %combine.11.share_ref), custom_call_target="tpu_custom_call" | custom-call | flops 540672 | bytes 1622016 | tf_op jit(solution)/shard_map/final_right/pallas_call | solution.py:451
  (26 shorter events, 0.1 us)
Async XLA Ops:
  2.0 5.4 %copy-start.1 = (bf16[128,4224]{1,0:T(8,128)(2,1)}, bf16[128,4224]{1,0:T(8,128)(2,1)S(1)}, u32[]{:S(2)}) copy-start(bf16[128,4224]{1,0:T(8,128)(2,1)S(1)} %pack.1.buf_ref) | copy-start | bytes 3244036
  2.0 29.1 %collective-permute-start = (bf16[128,4224]{1,0:T(8,128)(2,1)S(1)}, bf16[128,4224]{1,0:T(8,128)(2,1)}, u32[]{:S(2)}, u32[]{:S(2)}) collective-permute-start(bf16[128,4224]{1,0:T(8,128)(2,1)S(1)} %pack.1.buf_ref), channel_id=1, source_target_pairs={{0,8},{8,16},{16,24},{24,0},{1,9},{9,17},{17,25},{25,1},{2,10},{10... | collective-permute-start | bytes 3244040 | tf_op jit(solution)/shard_map/ppermute | solution.py:338
  7.5 26.9 %all-to-all-start = ((bf16[8,24,4096]{2,1,0:T(8,128)(2,1)}), bf16[8,24,4096]{2,1,0:T(8,128)(2,1)S(1)}, u32[]{:S(2)}, u32[]{:S(2)}) async-start(bf16[8,24,4096]{2,1,0:T(8,128)(2,1)} %dispatch.4), calls=%async_computation | async-start | bytes 3145728 | tf_op jit(solution)/shard_map/all_to_all | solution.py:348
  31.1 27.2 %collective-permute-start.1 = (bf16[128,4224]{1,0:T(8,128)(2,1)}, bf16[128,4224]{1,0:T(8,128)(2,1)}, u32[]{:S(2)}, u32[]{:S(2)}) collective-permute-start(bf16[128,4224]{1,0:T(8,128)(2,1)} %collective-permute-done.buf_ref), channel_id=1, source_target_pairs={{0,8},{8,16},{16,24},{24,0},{1,9},{9,17},{17,25},{25,1},{2,10},{10... | collective-permute-start | bytes 3244040 | tf_op jit(solution)/shard_map/ppermute | solution.py:338
  34.4 27.2 %all-to-all-start.1 = ((bf16[8,24,4096]{2,1,0:T(8,128)(2,1)}), bf16[8,24,4096]{2,1,0:T(8,128)(2,1)S(1)}, u32[]{:S(2)}, u32[]{:S(2)}) async-start(bf16[8,24,4096]{2,1,0:T(8,128)(2,1)} %dispatch.5), calls=%async_computation.1 | async-start | bytes 3145728 | tf_op jit(solution)/shard_map/all_to_all | solution.py:348
  38.1 27.8 %collective-permute-start.3 = (bf16[128,4224]{1,0:T(8,128)(2,1)}, bf16[128,4224]{1,0:T(8,128)(2,1)}, u32[]{:S(2)}, u32[]{:S(2)}) collective-permute-start(bf16[128,4224]{1,0:T(8,128)(2,1)} %collective-permute-done.buf_ref), channel_id=1, source_target_pairs={{0,1},{1,0},{2,3},{3,2},{4,5},{5,4},{6,7},{7,6},{8,9},{9,8},{10,11... | collective-permute-start | bytes 3244040 | tf_op jit(solution)/shard_map/ppermute | solution.py:275
  58.3 26.2 %collective-permute-start.2 = (bf16[128,4224]{1,0:T(8,128)(2,1)}, bf16[128,4224]{1,0:T(8,128)(2,1)}, u32[]{:S(2)}, u32[]{:S(2)}) collective-permute-start(bf16[128,4224]{1,0:T(8,128)(2,1)} %collective-permute-done.1.buf_ref), channel_id=1, source_target_pairs={{0,8},{8,16},{16,24},{24,0},{1,9},{9,17},{17,25},{25,1},{2,10},{10... | collective-permute-start | bytes 3244040 | tf_op jit(solution)/shard_map/ppermute | solution.py:338
  61.6 26.2 %all-to-all-start.3 = ((bf16[8,24,4096]{2,1,0:T(8,128)(2,1)}), bf16[8,24,4096]{2,1,0:T(8,128)(2,1)S(1)}, u32[]{:S(2)}, u32[]{:S(2)}) async-start(bf16[8,24,4096]{2,1,0:T(8,128)(2,1)} %dispatch.6), calls=%async_computation.3 | async-start | bytes 3145728 | tf_op jit(solution)/shard_map/all_to_all | solution.py:348
  65.3 26.2 %collective-permute-start.7 = (bf16[128,4224]{1,0:T(8,128)(2,1)}, bf16[128,4224]{1,0:T(8,128)(2,1)}, u32[]{:S(2)}, u32[]{:S(2)}) collective-permute-start(bf16[128,4224]{1,0:T(8,128)(2,1)} %collective-permute-done.1.buf_ref), channel_id=1, source_target_pairs={{0,1},{1,0},{2,3},{3,2},{4,5},{5,4},{6,7},{7,6},{8,9},{9,8},{10,11... | collective-permute-start | bytes 3244040 | tf_op jit(solution)/shard_map/ppermute | solution.py:275
  76.6 25.8 %collective-permute-start.4 = (bf16[48,4096]{1,0:T(8,128)(2,1)}, bf16[48,4096]{1,0:T(8,128)(2,1)S(1)}, u32[]{:S(2)}, u32[]{:S(2)}) collective-permute-start(bf16[48,4096]{1,0:T(8,128)(2,1)} %get-tuple-element.101), channel_id=1, source_target_pairs={{0,2},{1,3},{2,0},{3,1},{4,6},{5,7},{6,4},{7,5},{8,10},{9,11},{10,... | collective-permute-start | bytes 1179656 | tf_op jit(solution)/shard_map/ppermute | solution.py:279
  78.3 24.0 %collective-permute-start.5 = (bf16[48,4096]{1,0:T(8,128)(2,1)}, bf16[48,4096]{1,0:T(8,128)(2,1)}, u32[]{:S(2)}, u32[]{:S(2)}) collective-permute-start(bf16[48,4096]{1,0:T(8,128)(2,1)} %get-tuple-element.102), channel_id=1, source_target_pairs={{0,4},{1,5},{2,6},{3,7},{4,0},{5,1},{6,2},{7,3},{8,12},{9,13},{10,... | collective-permute-start | bytes 1179656 | tf_op jit(solution)/shard_map/ppermute | solution.py:279
  79.8 23.8 %collective-permute-start.6 = (bf16[48,4096]{1,0:T(8,128)(2,1)}, bf16[48,4096]{1,0:T(8,128)(2,1)}, u32[]{:S(2)}, u32[]{:S(2)}) collective-permute-start(bf16[48,4096]{1,0:T(8,128)(2,1)} %get-tuple-element.103), channel_id=1, source_target_pairs={{0,6},{1,7},{2,4},{3,5},{4,2},{5,3},{6,0},{7,1},{8,14},{9,15},{10,... | collective-permute-start | bytes 1179656 | tf_op jit(solution)/shard_map/ppermute | solution.py:279
  87.8 32.7 %all-to-all-start.2 = ((bf16[8,24,4096]{2,1,0:T(8,128)(2,1)}), bf16[8,24,4096]{2,1,0:T(8,128)(2,1)S(1)}, u32[]{:S(2)}, u32[]{:S(2)}) async-start(bf16[8,24,4096]{2,1,0:T(8,128)(2,1)} %dispatch.7), calls=%async_computation.2 | async-start | bytes 3145728 | tf_op jit(solution)/shard_map/all_to_all | solution.py:348
  91.5 12.1 %copy-start = (bf16[48,4096]{1,0:T(8,128)(2,1)S(1)}, bf16[48,4096]{1,0:T(8,128)(2,1)}, u32[]{:S(2)}) copy-start(bf16[48,4096]{1,0:T(8,128)(2,1)} %get-tuple-element.110.refs_0_) | copy-start | bytes 1179652
  106.4 6.5 %collective-permute-start.8 = (bf16[128,4224]{1,0:T(8,128)(2,1)S(1)}, bf16[128,4224]{1,0:T(8,128)(2,1)S(1)}, u32[]{:S(2)}, u32[]{:S(2)}) collective-permute-start(bf16[128,4224]{1,0:T(8,128)(2,1)S(1)} %combine.6), channel_id=1, source_target_pairs={{0,1},{1,0},{2,3},{3,2},{4,5},{5,4},{6,7},{7,6},{8,9},{9,8},{10,11... | collective-permute-start | bytes 3244040 | tf_op jit(solution)/shard_map/ppermute | solution.py:275
  106.5 24.6 %collective-permute-start.9 = (bf16[48,4096]{1,0:T(8,128)(2,1)}, bf16[48,4096]{1,0:T(8,128)(2,1)S(1)}, u32[]{:S(2)}, u32[]{:S(2)}) collective-permute-start(bf16[48,4096]{1,0:T(8,128)(2,1)} %get-tuple-element.118), channel_id=1, source_target_pairs={{0,2},{1,3},{2,0},{3,1},{4,6},{5,7},{6,4},{7,5},{8,10},{9,11},{10,... | collective-permute-start | bytes 1179656 | tf_op jit(solution)/shard_map/ppermute | solution.py:279
  107.2 23.9 %collective-permute-start.10 = (bf16[48,4096]{1,0:T(8,128)(2,1)}, bf16[48,4096]{1,0:T(8,128)(2,1)}, u32[]{:S(2)}, u32[]{:S(2)}) collective-permute-start(bf16[48,4096]{1,0:T(8,128)(2,1)} %get-tuple-element.119), channel_id=1, source_target_pairs={{0,4},{1,5},{2,6},{3,7},{4,0},{5,1},{6,2},{7,3},{8,12},{9,13},{10,... | collective-permute-start | bytes 1179656 | tf_op jit(solution)/shard_map/ppermute | solution.py:279
  108.6 28.3 %collective-permute-start.11 = (bf16[48,4096]{1,0:T(8,128)(2,1)}, bf16[48,4096]{1,0:T(8,128)(2,1)}, u32[]{:S(2)}, u32[]{:S(2)}) collective-permute-start(bf16[48,4096]{1,0:T(8,128)(2,1)} %get-tuple-element.120), channel_id=1, source_target_pairs={{0,6},{1,7},{2,4},{3,5},{4,2},{5,3},{6,0},{7,1},{8,14},{9,15},{10,... | collective-permute-start | bytes 1179656 | tf_op jit(solution)/shard_map/ppermute | solution.py:279
  114.1 32.5 %collective-permute-start.12 = (bf16[128,4224]{1,0:T(8,128)(2,1)}, bf16[128,4224]{1,0:T(8,128)(2,1)}, u32[]{:S(2)}, u32[]{:S(2)}) collective-permute-start(bf16[128,4224]{1,0:T(8,128)(2,1)} %join.4), channel_id=1, source_target_pairs={{0,8},{8,16},{16,24},{24,0},{1,9},{9,17},{17,25},{25,1},{2,10},{10... | collective-permute-start | bytes 3244040 | tf_op jit(solution)/shard_map/ppermute | solution.py:338
  131.1 9.4 %copy-start.3 = (bf16[48,4096]{1,0:T(8,128)(2,1)S(1)}, bf16[48,4096]{1,0:T(8,128)(2,1)}, u32[]{:S(2)}) copy-start(bf16[48,4096]{1,0:T(8,128)(2,1)} %get-tuple-element.121.refs_0_) | copy-start | bytes 1179652
  136.9 24.5 %all-to-all-start.4 = ((bf16[8,24,4096]{2,1,0:T(8,128)(2,1)}), bf16[8,24,4096]{2,1,0:T(8,128)(2,1)S(1)}, u32[]{:S(2)}, u32[]{:S(2)}) async-start(bf16[8,24,4096]{2,1,0:T(8,128)(2,1)} %get-tuple-element.116), calls=%async_computation.4 | async-start | bytes 3145728 | tf_op jit(solution)/shard_map/all_to_all | solution.py:348
  143.4 3.3 %collective-permute-start.13 = (bf16[128,4224]{1,0:T(8,128)(2,1)S(1)}, bf16[128,4224]{1,0:T(8,128)(2,1)S(1)}, u32[]{:S(2)}, u32[]{:S(2)}) collective-permute-start(bf16[128,4224]{1,0:T(8,128)(2,1)S(1)} %combine.8), channel_id=1, source_target_pairs={{0,1},{1,0},{2,3},{3,2},{4,5},{5,4},{6,7},{7,6},{8,9},{9,8},{10,11... | collective-permute-start | bytes 3244040 | tf_op jit(solution)/shard_map/ppermute | solution.py:275
  149.1 16.8 %collective-permute-start.14 = (bf16[128,2048]{1,0:T(8,128)(2,1)}, bf16[128,2048]{1,0:T(8,128)(2,1)}, u32[]{:S(2)}, u32[]{:S(2)}) collective-permute-start(bf16[128,2048]{1,0:T(8,128)(2,1)} %get-tuple-element.127), channel_id=1, source_target_pairs={{0,8},{8,16},{16,24},{24,0},{1,9},{9,17},{17,25},{25,1},{2,10},{10... | collective-permute-start | bytes 1572872 | tf_op jit(solution)/shard_map/ppermute | solution.py:338
  149.1 28.7 %collective-permute-start.16 = (bf16[128,2176]{1,0:T(8,128)(2,1)}, bf16[128,2176]{1,0:T(8,128)(2,1)S(1)}, u32[]{:S(2)}, u32[]{:S(2)}) collective-permute-start(bf16[128,2176]{1,0:T(8,128)(2,1)} %get-tuple-element.128), channel_id=1, source_target_pairs={{0,8},{8,16},{16,24},{24,0},{1,9},{9,17},{17,25},{25,1},{2,10},{10... | collective-permute-start | bytes 1671176 | tf_op jit(solution)/shard_map/ppermute | solution.py:338
  167.9 29.2 %collective-permute-start.15 = (bf16[128,2048]{1,0:T(8,128)(2,1)}, bf16[128,2048]{1,0:T(8,128)(2,1)}, u32[]{:S(2)}, u32[]{:S(2)}) collective-permute-start(bf16[128,2048]{1,0:T(8,128)(2,1)} %join.6), channel_id=1, source_target_pairs={{0,8},{8,16},{16,24},{24,0},{1,9},{9,17},{17,25},{25,1},{2,10},{10... | collective-permute-start | bytes 1572872 | tf_op jit(solution)/shard_map/ppermute | solution.py:338
  167.9 26.3 %all-to-all-start.5 = ((bf16[8,24,4096]{2,1,0:T(8,128)(2,1)}), bf16[8,24,4096]{2,1,0:T(8,128)(2,1)}, u32[]{:S(2)}, u32[]{:S(2)}) async-start(bf16[8,24,4096]{2,1,0:T(8,128)(2,1)} %get-tuple-element.131), calls=%async_computation.5 | async-start | bytes 3145728 | tf_op jit(solution)/shard_map/all_to_all | solution.py:348
  178.8 21.8 %collective-permute-start.17 = (bf16[128,2176]{1,0:T(8,128)(2,1)}, bf16[128,2176]{1,0:T(8,128)(2,1)}, u32[]{:S(2)}, u32[]{:S(2)}) collective-permute-start(bf16[128,2176]{1,0:T(8,128)(2,1)} %join.7), channel_id=1, source_target_pairs={{0,8},{8,16},{16,24},{24,0},{1,9},{9,17},{17,25},{25,1},{2,10},{10... | collective-permute-start | bytes 1671176 | tf_op jit(solution)/shard_map/ppermute | solution.py:338
  178.8 15.4 %copy-start.2 = (bf16[128,4224]{1,0:T(8,128)(2,1)S(1)}, bf16[128,4224]{1,0:T(8,128)(2,1)}, u32[]{:S(2)}) copy-start(bf16[128,4224]{1,0:T(8,128)(2,1)} %copy-done.1) | copy-start | bytes 3244036
